TPU v7x, 32 devices: a whole 2x2x4 slice. The times are simulated.
32 devices in a mesh: dp: 16 (over z, y, x), tensor: 2 (over core).
Axes of the slice: x: 2, y: 2, z: 4, core: 2. Of those that a mesh axis runs over, the one named last changes fastest.
Arguments:
- activations: bfloat16 [24576, 768], P('dp'), may hold values from -6 to 6
- cotangent: bfloat16 [24576, 768], P('dp'), may hold values from -6 to 6
- token_weight: int32 [24576], P('dp'), may hold values from 1 to 4
- lengths: int32 [48], P('dp'), may hold values from 64 to 512, as said below
- step_count: int32 [1], replicated, may hold values from 1 to 20
- inward_weight: float32 [3, 768, 768], P(None, 'dp', 'tensor'), may hold values from -0.21875 to 0.21875
- output_weight: float32 [768, 768], P('tensor', 'dp'), may hold values from -2 to 2
- up_weight: float32 [768, 3072], P('dp', 'tensor'), may hold values from -0.21875 to 0.21875
- down_weight: float32 [3072, 768], P('tensor', 'dp'), may hold values from -0.109375 to 0.109375
- heads_bias: float32 [2, 48, 16], P(None, 'tensor', 'dp'), may hold values from -3 to 3
- hidden_bias: float32 [192, 16], P('tensor', 'dp'), may hold values from -3 to 3
- norm_vectors: float32 [6, 768], P(None, 'dp'), may hold values from -0.9 to 1.6
- inward_first: float32 [3, 768, 768], P(None, 'dp', 'tensor'), may hold values from -1792 to 1792
- output_first: float32 [768, 768], P('tensor', 'dp'), may hold values from -192 to 192
- up_first: float32 [768, 3072], P('dp', 'tensor'), may hold values from -512 to 512
- down_first: float32 [3072, 768], P('tensor', 'dp'), may hold values from -1024 to 1024
- heads_first: float32 [2, 48, 16], P(None, 'tensor', 'dp'), may hold values from -1792 to 1792
- hidden_first: float32 [192, 16], P('tensor', 'dp'), may hold values from -512 to 512
- norm_first: float32 [6, 768], P(None, 'dp'), may hold values from -1280 to 1280
- inward_second: float32 [3, 768, 768], P(None, 'dp', 'tensor'), may hold values from 98304 to 393216
- output_second: float32 [768, 768], P('tensor', 'dp'), may hold values from 1152 to 4608
- up_second: float32 [768, 3072], P('dp', 'tensor'), may hold values from 8847.36 to 35389.44
- down_second: float32 [3072, 768], P('tensor', 'dp'), may hold values from 29491.2 to 117964.8
- heads_second: float32 [2, 48, 16], P(None, 'tensor', 'dp'), may hold values from 98304 to 393216
- hidden_second: float32 [192, 16], P('tensor', 'dp'), may hold values from 8847.36 to 35389.44
- norm_second: float32 [6, 768], P(None, 'dp'), may hold values from 55296 to 221184
Outputs:
- layer_output: bfloat16 [24576, 768], P('dp')
- input_grad: float32 [24576, 768], P('dp')
- new_inward: float32 [3, 768, 768], P(None, 'dp', 'tensor')
- new_inward_first: float32 [3, 768, 768], P(None, 'dp', 'tensor')
- new_inward_second: float32 [3, 768, 768], P(None, 'dp', 'tensor')
- new_output: float32 [768, 768], P('tensor', 'dp')
- new_output_first: float32 [768, 768], P('tensor', 'dp')
- new_output_second: float32 [768, 768], P('tensor', 'dp')
- new_up: float32 [768, 3072], P('dp', 'tensor')
- new_up_first: float32 [768, 3072], P('dp', 'tensor')
- new_up_second: float32 [768, 3072], P('dp', 'tensor')
- new_down: float32 [3072, 768], P('tensor', 'dp')
- new_down_first: float32 [3072, 768], P('tensor', 'dp')
- new_down_second: float32 [3072, 768], P('tensor', 'dp')
- new_heads: float32 [2, 48, 16], P(None, 'tensor', 'dp')
- new_heads_first: float32 [2, 48, 16], P(None, 'tensor', 'dp')
- new_heads_second: float32 [2, 48, 16], P(None, 'tensor', 'dp')
- new_hidden: float32 [192, 16], P('tensor', 'dp')
- new_hidden_first: float32 [192, 16], P('tensor', 'dp')
- new_hidden_second: float32 [192, 16], P('tensor', 'dp')
- new_norm: float32 [6, 768], P(None, 'dp')
- new_norm_first: float32 [6, 768], P(None, 'dp')
- new_norm_second: float32 [6, 768], P(None, 'dp')
Inputs may be any that keep to these rules, and one draw needn't show every extreme that they name: Sequence s holds lengths[s] real tokens followed by padding; some sequence is full and some has an eighth of 512.
All inputs are finite; a program needn't handle non-finite values.
Results may differ from a plain program's by a relative error of at most 0.018.
Values may be sent and summed in bfloat16 or wider, within the bound.
No kernel may reach another device: no remote copies, remote signals or barrier semaphores. Data moves between devices by JAX's collectives and lax.ppermute only.
A program may use at most 192 MiB of HBM per device.

v0:
```python
from functools import partial
import math

import jax
import jax.numpy as jnp
from jax import lax
from jax.experimental import pallas as pl
from jax.experimental.pallas import tpu as pltpu
from jax.sharding import PartitionSpec as P

D = 768
HEAD_DIM = 64
FF = 3072
LEN = 512
LANES = 128
ROWS = 256
COST_SHARE = 1
ATTEND, BACK, EXPAND, CONTRACT, GRADS = 12, 12, 16, 24, 20

norm_epsilon = 1e-12
low = jnp.bfloat16
full = jnp.float32


def dot_nn(left, right):
    return lax.dot_general(left, right, (((1,), (0,)), ((), ())), preferred_element_type=full)


def dot_nt(left, right):
    return lax.dot_general(left, right, (((1,), (1,)), ((), ())), preferred_element_type=full)


def column_sum(values):
    return jnp.sum(values, axis=0, keepdims=True)


def row_mean(values):
    return jnp.mean(values, axis=-1, keepdims=True)


def normalize(total_in):
    centred = total_in - row_mean(total_in)
    inverse = lax.rsqrt(row_mean(centred * centred) + norm_epsilon)
    return (centred * inverse, inverse)


def norm_back(incoming, normed, inverse, gain):
    scaled = incoming * gain
    return inverse * (scaled - row_mean(scaled) - normed * row_mean(scaled * normed))


def cost(flops, moved, exps=0):
    return pl.CostEstimate(
        flops=int(flops / COST_SHARE),
        bytes_accessed=int(moved / COST_SHARE),
        transcendentals=int(exps / COST_SHARE),
    )


def params(mebibytes=12):
    return pltpu.CompilerParams(vmem_limit_bytes=mebibytes * 1024 * 1024)


def shape(dims, kind):
    return jax.ShapeDtypeStruct(dims, kind)


def main(dims, kind):
    return pltpu.HBM(dims, kind)


def streamed(*arrays):
    return [pltpu.with_memory_space_constraint(array, pltpu.HBM) for array in arrays]


def after(value, *others):
    return lax.optimization_barrier((value,) + others)[0]


def after_all(values, *others):
    return lax.optimization_barrier(tuple(values) + others)[: len(values)]


def hop(value, offset, size):
    return lax.ppermute(value, "dp", [(d, d ^ offset) for d in range(size)])


def swap_cores(value):
    return lax.ppermute(value, "tensor", [(0, 1), (1, 0)])


def split_columns(width):
    return -(-width // (2 * LANES)) * LANES


def gather_planes(shard, size):
    found = [shard] + [hop(shard, 4 * k, size) for k in range(1, size // 4)]
    return found


def gather_doubled(shard, size):
    pair = jnp.stack([shard, hop(shard, 8, size)])
    return (pair, hop(pair, 4, size))


def doubled_planes(pair, near):
    return [pair[0], near[0], pair[1], near[1]]


def split_halves(found):
    stacked = jnp.stack(found)
    cut = split_columns(stacked.shape[2])
    return lax.optimization_barrier((stacked[..., :cut], stacked[..., cut:]))


def gather_near(own, size):
    return (hop(own[0], 2, size), hop(own[1], 1, size))


def gather_pairs(own, near):
    return lax.optimization_barrier(
        (jnp.concatenate([own[0], near[0]]), jnp.concatenate([own[1], near[1]]))
    )


def gather_far(pairs, size):
    return (hop(pairs[0], 1, size), hop(pairs[1], 2, size))


def place_kernel(me_ref, pair_a, far_a, pair_b, far_b, out_ref):
    layers, rows, cut = pair_a.shape
    layers //= 2
    sources = (
        (pair_a, 0, pair_b, 0),
        (far_a, 0, pair_b, layers),
        (pair_a, layers, far_b, 0),
        (far_a, layers, far_b, layers),
    )
    for plane, (left, left_at, right, right_at) in enumerate(sources):
        for k in range(layers):
            start = pl.multiple_of((me_ref[0] ^ (4 * k + plane)) * rows, 16)
            out_ref[pl.ds(start, rows), :cut] = left[left_at + k]
            out_ref[pl.ds(start, rows), cut:] = right[right_at + k]


def place(pairs, far, me):
    flat = (pairs[0], far[0], pairs[1], far[1])
    layers, rows, cut = pairs[0].shape
    width = cut + pairs[1].shape[2]
    total = 2 * layers * rows
    return pl.pallas_call(
        place_kernel,
        out_shape=shape((total, width), low),
        grid_spec=pltpu.PrefetchScalarGridSpec(
            num_scalar_prefetch=1,
            grid=(1,),
            in_specs=[pl.BlockSpec(piece.shape, lambda i, m: (0, 0, 0)) for piece in flat],
            out_specs=pl.BlockSpec((total, width), lambda i, m: (0, 0)),
        ),
        compiler_params=params(12),
        cost_estimate=cost(0, 4 * total * width),
        name="place",
    )(me, *flat)


def turn_kernel(source_ref, out_ref):
    out_ref[...] = source_ref[...].astype(full).T.astype(low)


def turn(source):
    rows, width = source.shape
    return pl.pallas_call(
        turn_kernel,
        out_shape=shape((width, rows), low),
        grid=(rows // LEN,),
        in_specs=[pl.BlockSpec((LEN, width), lambda i: (i, 0))],
        out_specs=pl.BlockSpec((width, LEN), lambda i: (0, i)),
        compiler_params=params(16),
        cost_estimate=cost(0, 4 * rows * width),
        name="turn",
    )(source)


def combine_kernel(count, *refs):
    own_ref, out_ref = refs[-2:]
    start = 0
    for at in range(count):
        kept, got, more = refs[3 * at : 3 * at + 3]
        total = kept[0].astype(full) + got[0].astype(full) + more[...].astype(full)
        width = total.shape[2]
        for k in range(total.shape[0]):
            if k % 2:
                out_ref[k // 2, :, start : start + width] = total[k].astype(low)
            else:
                own_ref[k // 2, :, start : start + width] = total[k]
        start += width


def combine(halves):
    layers, rows = halves[0][2].shape[:2]
    width = sum(more.shape[2] for _, _, more in halves)
    flat, specs = [], []
    for kept, got, more in halves:
        part = (1,) + more.shape
        flat += [kept, got, more]
        specs += [pl.BlockSpec(part, lambda i: (0, 0, 0, 0))] * 2
        specs += [pl.BlockSpec(more.shape, lambda i: (0, 0, 0))]
    piece = (layers // 2, rows, width)
    return pl.pallas_call(
        partial(combine_kernel, len(halves)),
        out_shape=(shape(piece, full), shape(piece, low)),
        grid=(1,),
        in_specs=specs,
        out_specs=(pl.BlockSpec(piece, lambda i: (0, 0, 0)),) * 2,
        compiler_params=params(16),
        cost_estimate=cost(3 * layers * rows * width, 8 * layers * rows * width),
        name="combine",
    )(*flat)


def far_half(own, near):
    return (own[1] + near[1].astype(full)).astype(low)


def reduce_sum(own, near, far):
    return own[0] + near[0].astype(full) + far.astype(full)


def attend_kernel(length_ref, x_ref, w_ref, bias_ref, qkv_ref, weight_ref, context_ref):
    length = length_ref[pl.program_id(1)]
    mixed = dot_nn(x_ref[...], w_ref[...])
    queries = (mixed[:, :LANES] + bias_ref[0:1, :]).astype(low)
    key_rows = mixed[:, LANES : 2 * LANES].astype(low)
    values_full = mixed[:, 2 * LANES :] + bias_ref[1:2, :]
    values = values_full.astype(low)
    qkv_ref[:, :LANES] = queries
    qkv_ref[:, LANES : 2 * LANES] = key_rows
    qkv_ref[:, 2 * LANES :] = values
    values_t = values_full.T.astype(low)
    rows = queries.shape[0]
    lane = lax.broadcasted_iota(jnp.int32, (rows, LANES), 1)
    live = lax.broadcasted_iota(jnp.int32, (rows, 1), 0) < length
    scaled = queries * (1.0 / math.sqrt(HEAD_DIM))
    parts = []
    for head in range(2):
        picked = jnp.where((lane >= HEAD_DIM) == bool(head), scaled, jnp.zeros_like(scaled))
        scores = jnp.where(live, dot_nt(key_rows, picked), -jnp.inf)
        grown = jnp.exp(scores - jnp.max(scores, axis=0, keepdims=True))
        weights = (grown * (1.0 / jnp.sum(grown, axis=0, keepdims=True))).astype(low)
        weight_ref[0, head] = weights
        parts.append(dot_nn(values_t[head * HEAD_DIM : (head + 1) * HEAD_DIM, :], weights))
    context_ref[...] = jnp.concatenate(parts, axis=0).T.astype(low)


def attend(lengths, source, inward, biases, first, groups):
    rows = source.shape[0]
    count = rows // LEN
    width = 3 * LANES
    return pl.pallas_call(
        attend_kernel,
        out_shape=(
            main((rows, groups * width), low),
            main((groups * count, 2, LEN, LEN), low),
            main((rows, groups * LANES), low),
        ),
        grid_spec=pltpu.PrefetchScalarGridSpec(
            num_scalar_prefetch=1,
            grid=(groups, count),
            in_specs=[
                pl.BlockSpec((LEN, D), lambda g, s, n: (s, 0)),
                pl.BlockSpec((D, width), lambda g, s, n: (0, first + g)),
                pl.BlockSpec((2, LANES), lambda g, s, n: (0, first + g)),
            ],
            out_specs=(
                pl.BlockSpec((LEN, width), lambda g, s, n: (s, g)),
                pl.BlockSpec((1, 2, LEN, LEN), lambda g, s, n: (g * count + s, 0, 0, 0)),
                pl.BlockSpec((LEN, LANES), lambda g, s, n: (s, g)),
            ),
        ),
        compiler_params=params(ATTEND),
        cost_estimate=cost(
            groups * (2 * rows * D * width + 8 * count * LEN * LEN * LANES),
            groups * count * 2 * LEN * LEN * 2,
            groups * count * 2 * LEN * LEN,
        ),
        name="attend",
    )(lengths, *streamed(source), inward, biases)


def attend_back_kernel(qkv_ref, weight_ref, grad_ref, out_ref, sum_ref):
    @pl.when(pl.program_id(0) == 0)
    def _():
        sum_ref[...] = jnp.zeros_like(sum_ref)

    queries = qkv_ref[:, :LANES]
    key_rows = qkv_ref[:, LANES : 2 * LANES]
    values = qkv_ref[:, 2 * LANES :]
    grads = grad_ref[...]
    keys_t = key_rows.astype(full).T.astype(low)
    rows = queries.shape[0]
    lane = lax.broadcasted_iota(jnp.int32, (rows, LANES), 1)
    score_scale = 1.0 / math.sqrt(HEAD_DIM)
    query_parts, key_parts, value_parts = [], [], []
    for head in range(2):
        picked = jnp.where((lane >= HEAD_DIM) == bool(head), grads, jnp.zeros_like(grads))
        weights = weight_ref[0, head]
        wide = weights.astype(full)
        mixed = wide * dot_nt(values, picked)
        score_grads = (mixed - wide * jnp.sum(mixed, axis=0, keepdims=True)).astype(low)
        value_parts.append(dot_nn(weights, grads))
        key_parts.append(dot_nn(score_grads, queries))
        query_parts.append(
            dot_nn(keys_t[head * HEAD_DIM : (head + 1) * HEAD_DIM, :], score_grads)
        )
    first = lane < HEAD_DIM
    query_grads = (jnp.concatenate(query_parts, axis=0).T * score_scale).astype(low)
    key_grads = (jnp.where(first, key_parts[0], key_parts[1]) * score_scale).astype(low)
    value_grads = jnp.where(first, value_parts[0], value_parts[1]).astype(low)
    out_ref[:, :LANES] = query_grads
    out_ref[:, LANES : 2 * LANES] = key_grads
    out_ref[:, 2 * LANES :] = value_grads
    sum_ref[0:1, :] += column_sum(query_grads.astype(full))
    sum_ref[1:2, :] += column_sum(value_grads.astype(full))


def attend_back(qkv, weights, at, grads, group):
    rows = qkv.shape[0]
    count = rows // LEN
    width = 3 * LANES
    return pl.pallas_call(
        attend_back_kernel,
        out_shape=(main((rows, width), low), shape((2, LANES), full)),
        grid=(count,),
        in_specs=[
            pl.BlockSpec((LEN, width), lambda s: (s, at)),
            pl.BlockSpec((1, 2, LEN, LEN), lambda s: (at * count + s, 0, 0, 0)),
            pl.BlockSpec((LEN, LANES), lambda s: (s, group)),
        ],
        out_specs=(
            pl.BlockSpec((LEN, width), lambda s: (s, 0)),
            pl.BlockSpec((2, LANES), lambda s: (0, 0)),
        ),
        compiler_params=params(BACK),
        cost_estimate=cost(
            16 * count * LEN * LEN * LANES, count * 2 * LEN * LEN * 2 + 4 * rows * width
        ),
        name="attend_back",
    )(*streamed(qkv, weights, grads))


def outward_kernel(*refs):
    contexts, w_ref, out_ref = refs[:-2], refs[-2], refs[-1]
    context = jnp.concatenate([ref[...] for ref in contexts], axis=1)
    out_ref[...] = dot_nt(context, w_ref[...]).astype(low)


def row_block(width):
    return pl.BlockSpec((ROWS, width), lambda i: (i, 0))


def fixed_block(dims, at=0):
    return pl.BlockSpec(dims, lambda i: (0, at))


def outward_part(contexts, mid, outward_at):
    rows = contexts[0].shape[0]
    width = sum(context.shape[1] for context in contexts)
    return pl.pallas_call(
        outward_kernel,
        out_shape=shape((rows, D), low),
        grid=(rows // ROWS,),
        in_specs=[row_block(context.shape[1]) for context in contexts]
        + [fixed_block((D, width), outward_at // width)],
        out_specs=row_block(D),
        compiler_params=params(),
        cost_estimate=cost(2 * rows * D * width, 2 * (rows * D + rows * width + D * width)),
        name="outward",
    )(*streamed(*contexts), mid)


def gelu_parts(hidden):
    half = 0.5 + 0.5 * lax.erf(hidden * 0.7071067811865476)
    slope = half + hidden * 0.3989422804014327 * jnp.exp(-0.5 * hidden * hidden)
    return ((hidden * half).astype(low), slope.astype(low))


def expand_first_kernel(
    mine_ref, other_ref, x_ref, vector_ref, bias_ref, up_ref, down_ref,
    total_ref, active_ref, slope_ref, middle_ref, normed_ref, inverse_ref,
):
    summed = (
        mine_ref[...].astype(full)
        + other_ref[...].astype(full)
        + vector_ref[0:1, :]
        + x_ref[...].astype(full)
    )
    normed, inverse = normalize(summed)
    normed_ref[...] = normed
    inverse_ref[...] = inverse
    held = (normed * vector_ref[1:2, :] + vector_ref[2:3, :]).astype(low)
    middle_ref[...] = held
    active, slope = gelu_parts(dot_nn(held, up_ref[...]) + bias_ref[...])
    active_ref[...] = active
    slope_ref[...] = slope
    total_ref[...] = dot_nt(active, down_ref[...])


def expand_first(mine, other, source, vectors, hidden_bias, mid):
    rows, hidden = source.shape[0], hidden_bias.shape[1]
    block = hidden // 2
    return pl.pallas_call(
        expand_first_kernel,
        out_shape=(
            main((rows, D), full),
            main((rows, block), low),
            main((rows, block), low),
            main((rows, D), low),
            main((rows, D), full),
            main((rows, 1), full),
        ),
        grid=(rows // ROWS,),
        in_specs=[
            row_block(D),
            row_block(D),
            row_block(D),
            fixed_block(vectors.shape),
            fixed_block((1, block)),
            fixed_block((D, block)),
            fixed_block((D, block), 1),
        ],
        out_specs=(
            row_block(D), row_block(block), row_block(block), row_block(D), row_block(D),
            row_block(1),
        ),
        compiler_params=params(EXPAND),
        cost_estimate=cost(4 * rows * D * block, 4 * D * block + 16 * rows * D, 2 * rows * block),
        name="expand_first",
    )(mine, other, *streamed(source), vectors, hidden_bias, mid, mid)


def expand_last_kernel(
    total_ref, middle_ref, bias_ref, up_ref, down_ref, part_ref, active_ref, slope_ref
):
    active, slope = gelu_parts(dot_nn(middle_ref[...], up_ref[...]) + bias_ref[...])
    active_ref[...] = active
    slope_ref[...] = slope
    part_ref[...] = (total_ref[...] + dot_nt(active, down_ref[...])).astype(low)


def expand_last(total, middle, hidden_bias, mid):
    rows, hidden = total.shape[0], hidden_bias.shape[1]
    block = hidden // 2
    return pl.pallas_call(
        expand_last_kernel,
        out_shape=(shape((rows, D), low), main((rows, block), low), main((rows, block), low)),
        grid=(rows // ROWS,),
        in_specs=[
            row_block(D),
            row_block(D),
            fixed_block((1, block), 1),
            fixed_block((D, block)),
            fixed_block((D, block), 1),
        ],
        out_specs=(row_block(D), row_block(block), row_block(block)),
        compiler_params=params(EXPAND),
        cost_estimate=cost(4 * rows * D * block, 4 * D * block + 10 * rows * D, 2 * rows * block),
        name="expand_last",
    )(*streamed(total, middle), hidden_bias, mid, mid)


def contract_kernel(
    mine_ref, other_ref, normed_ref, cotangent_ref, scale_ref, vector_ref,
    slope_first, slope_last, up_first, down_first, up_last, down_last,
    part_ref, sum_ref, hidden_sum_ref, out_ref, wide_ref, low_ref, hidden_first, hidden_last,
):
    @pl.when(pl.program_id(0) == 0)
    def _():
        sum_ref[...] = jnp.zeros_like(sum_ref)
        hidden_sum_ref[...] = jnp.zeros_like(hidden_sum_ref)

    middle = normed_ref[...] * vector_ref[1:2, :] + vector_ref[2:3, :]
    summed = (
        mine_ref[...].astype(full) + other_ref[...].astype(full) + vector_ref[3:4, :] + middle
    )
    normed, inverse = normalize(summed)
    out_ref[...] = (normed * vector_ref[4:5, :] + vector_ref[5:6, :]).astype(low)
    incoming = cotangent_ref[...].astype(full) * scale_ref[...]
    second = norm_back(incoming, normed, inverse, vector_ref[4:5, :])
    sum_ref[0:1, :] += column_sum(second)
    sum_ref[1:2, :] += column_sum(incoming * normed)
    sum_ref[2:3, :] += column_sum(incoming)
    wide_ref[...] = second
    held = second.astype(low)
    low_ref[...] = held
    block = up_first.shape[1]
    total = None
    for at, slope_ref, up_ref, down_ref, hidden_ref in (
        (0, slope_first, up_first, down_first, hidden_first),
        (block, slope_last, up_last, down_last, hidden_last),
    ):
        hidden_grad = (dot_nn(held, down_ref[...]) * slope_ref[...].astype(full)).astype(low)
        hidden_ref[...] = hidden_grad
        hidden_sum_ref[:, at : at + block] += column_sum(hidden_grad.astype(full))
        part = dot_nt(hidden_grad, up_ref[...])
        total = part if total is None else total + part
    part_ref[...] = total.astype(low)


def contract(mine, other, normed, cotangent, scale, vectors, slopes, mids):
    rows, block = slopes[0].shape
    hidden = 2 * block
    weights = [fixed_block((D, block)), fixed_block((D, block), 1)]
    return pl.pallas_call(
        contract_kernel,
        out_shape=(
            shape((rows, D), low),
            shape((3, D), full),
            shape((1, hidden), full),
            main((rows, D), low),
            main((rows, D), full),
            main((rows, D), low),
            main((rows, block), low),
            main((rows, block), low),
        ),
        grid=(rows // ROWS,),
        in_specs=[
            row_block(D),
            row_block(D),
            row_block(D),
            row_block(D),
            row_block(1),
            fixed_block(vectors.shape),
            row_block(block),
            row_block(block),
        ]
        + weights
        + weights,
        out_specs=(
            row_block(D),
            fixed_block((3, D)),
            fixed_block((1, hidden)),
            row_block(D),
            row_block(D),
            row_block(D),
            row_block(block),
            row_block(block),
        ),
        compiler_params=params(CONTRACT),
        cost_estimate=cost(4 * rows * D * hidden, 4 * D * hidden + 4 * rows * hidden),
        name="contract",
    )(
        mine, other, *streamed(normed, cotangent), scale, vectors, *streamed(*slopes),
        mids[0], mids[0], mids[1], mids[1],
    )


def first_back_kernel(
    mine_ref, other_ref, second_ref, normed_ref, inverse_ref, vector_ref, w_ref,
    sum_ref, wide_ref, low_ref, grad_ref,
):
    @pl.when(pl.program_id(0) == 0)
    def _():
        sum_ref[...] = jnp.zeros_like(sum_ref)

    incoming = mine_ref[...].astype(full) + other_ref[...].astype(full) + second_ref[...]
    normed = normed_ref[...]
    first = norm_back(incoming, normed, inverse_ref[...], vector_ref[1:2, :])
    sum_ref[0:1, :] += column_sum(first)
    sum_ref[1:2, :] += column_sum(incoming * normed)
    sum_ref[2:3, :] += column_sum(incoming)
    wide_ref[...] = first
    held = first.astype(low)
    low_ref[...] = held
    grad_ref[...] = dot_nn(held, w_ref[...]).astype(low)


def first_back(mine, other, second, normed, inverse, vectors, mid, outward_at, width):
    rows = second.shape[0]
    return pl.pallas_call(
        first_back_kernel,
        out_shape=(
            shape((3, D), full),
            main((rows, D), full),
            main((rows, D), low),
            main((rows, width), low),
        ),
        grid=(rows // ROWS,),
        in_specs=[row_block(D)] * 4
        + [
            row_block(1),
            fixed_block(vectors.shape),
            fixed_block((D, width), outward_at // width),
        ],
        out_specs=(fixed_block((3, D)), row_block(D), row_block(D), row_block(width)),
        compiler_params=params(BACK),
        cost_estimate=cost(2 * rows * D * width, 20 * rows * D),
        name="first_back",
    )(mine, other, *streamed(second, normed, inverse), vectors, mid)


def source_kernel(*refs):
    grads, weights, out_ref = refs[:-2], refs[-2], refs[-1]
    width = 3 * LANES
    total = None
    for group, grad_ref in enumerate(grads):
        part = dot_nt(grad_ref[...], weights[:, group * width : (group + 1) * width])
        total = part if total is None else total + part
    out_ref[...] = total.astype(low)


def source_part(grads, inward):
    rows, width = grads[0].shape
    groups = len(grads)
    return pl.pallas_call(
        source_kernel,
        out_shape=shape((rows, D), low),
        grid=(rows // ROWS,),
        in_specs=[row_block(width) for _ in grads] + [fixed_block((D, groups * width))],
        out_specs=row_block(D),
        compiler_params=params(),
        cost_estimate=cost(2 * rows * D * width * groups, 2 * (rows + D) * width * groups),
        name="source",
    )(*streamed(*grads), inward)


def finish_kernel(mine_ref, other_ref, first_ref, out_ref):
    out_ref[...] = mine_ref[...].astype(full) + other_ref[...].astype(full) + first_ref[...]


def finish(mine, other, first):
    rows = first.shape[0]
    return pl.pallas_call(
        finish_kernel,
        out_shape=main((rows, D), full),
        grid=(rows // ROWS,),
        in_specs=[row_block(D)] * 3,
        out_specs=row_block(D),
        compiler_params=params(),
        cost_estimate=cost(2 * rows * D, 12 * rows * D),
        name="finish",
    )(mine, other, *streamed(first))


def weight_grad_kernel(bit, count, turned, extra, me_ref, left_ref, *refs):
    rights, refs = refs[:count], refs[count:]
    if extra:
        extra_ref, refs = refs[0], refs[1:]
    left = left_ref
    if not turned:
        left, refs = refs[-1], refs[:-1]

        def turn_block(i, carry):
            start = pl.multiple_of(i * ROWS, ROWS)
            block = left_ref[pl.ds(start, ROWS), :].astype(full)
            left[:, pl.ds(start, ROWS)] = block.T.astype(low)
            return carry

        lax.fori_loop(0, left_ref.shape[0] // ROWS, turn_block, 0, unroll=True)
    total_ref = refs[-1] if bit is not None else refs[0]
    block = 2 * ROWS if rights[0].shape[1] % D else D
    if rights[0].shape[1] % block:
        right = jnp.concatenate([piece[...] for piece in rights], axis=1)
        total_ref[...] = dot_nn(left[...], right)
    else:
        for at, piece in enumerate(rights):
            steps = piece.shape[1] // block

            def multiply(j, carry, at=at, piece=piece, steps=steps):
                start = pl.multiple_of(j * block, LANES)
                into = pl.multiple_of((at * steps + j) * block, LANES)
                total_ref[:, pl.ds(into, block)] = dot_nn(
                    left[...], piece[:, pl.ds(start, block)]
                )
                return carry

            if steps == 1:
                multiply(0, 0)
            else:
                lax.fori_loop(0, steps, multiply, 0)
    if bit is None:
        return
    layers, rows = refs[0].shape[1:3]
    width = total_ref.shape[1]
    for target, far in ((refs[0], 1), (refs[1], 0)):

        def spread(i, carry, target=target, far=far):
            other, k = i // layers, i % layers
            plane = 2 * other + far if bit == 0 else other + 2 * far
            owner = me_ref[0] ^ (4 * k + plane)
            start = pl.multiple_of(owner * rows, 8)
            target[other, k, :, :width] = total_ref[pl.ds(start, rows), :].astype(low)
            if extra:
                target[other, k, :, width:] = extra_ref[owner]
            return carry

        lax.fori_loop(0, 2 * layers, spread, 0)


def weight_grad(left, rights, me, size, bit, turned=False, extra=None):
    tokens = rights[0].shape[0]
    width = sum(right.shape[1] for right in rights)
    layers, rows = size // 4, D // size
    extras = () if extra is None else (extra,)
    if me is not None:
        total = width + (0 if extra is None else LANES)
        outs = (shape((2, layers, rows, total), low),) * 2
        scratch = [pltpu.VMEM((D, width), full)]
    else:
        outs = (shape((D, width), full),)
        scratch = []
        me = jnp.zeros((1,), jnp.int32)
        bit = None
    if not turned:
        scratch.append(pltpu.VMEM((D, tokens), low))

    def whole(array):
        return pl.BlockSpec(array.shape, lambda j, m: (0,) * len(array.shape))

    flat = (left, *rights, *extras)
    return pl.pallas_call(
        partial(weight_grad_kernel, bit, len(rights), turned, extra is not None),
        out_shape=outs,
        grid_spec=pltpu.PrefetchScalarGridSpec(
            num_scalar_prefetch=1,
            grid=(1,),
            in_specs=[whole(array) for array in flat],
            out_specs=tuple(whole(array) for array in outs),
            scratch_shapes=scratch,
        ),
        compiler_params=params(GRADS),
        cost_estimate=cost(2 * tokens * D * width, 2 * tokens * (D + width)),
        name="weight_grad",
    )(me, *flat)


def adamw(master, gradient, first_moment, second_moment, step_rate, decay_rate, correct):
    first_new = 0.5 * first_moment + 0.5 * gradient
    second_new = 0.5 * second_moment + 0.5 * gradient * gradient
    moved = first_new / correct / (jnp.sqrt(second_new / correct) + 1e-08)
    return (master - step_rate * (moved + decay_rate * master), first_new, second_new)


def per_device(
    activations,
    cotangent,
    token_weight,
    lengths,
    step_count,
    inward_weight,
    output_weight,
    up_weight,
    down_weight,
    heads_bias,
    hidden_bias,
    norm_vectors,
    *moments,
):
    size = lax.axis_size("dp")
    rows, width = inward_weight.shape[1], inward_weight.shape[2]
    hidden_width = up_weight.shape[1]
    groups = width // LANES
    tokens = activations.shape[0]
    count = tokens // LEN
    fast = size == 16 and rows % 16 == 0
    me = lax.axis_index("dp").astype(jnp.int32).reshape(1) if fast else None

    small = jnp.concatenate(
        [heads_bias.reshape(-1), hidden_bias.reshape(-1), norm_vectors.reshape(-1)]
    )
    per_row = small.shape[0] // rows
    small_block = jnp.pad(small.reshape(rows, per_row), ((0, 0), (0, LANES - per_row)))
    inward_shard = jnp.concatenate(
        [
            inward_weight.reshape(3, rows, groups, LANES)
            .transpose(1, 2, 0, 3)
            .reshape(rows, 3 * width),
            small_block,
        ],
        axis=1,
    ).astype(low)
    block = hidden_width // 2
    outward_at = 2 * block
    up_shard, down_shard = up_weight.astype(low), down_weight.T.astype(low)
    first_shard = jnp.concatenate(
        [up_shard[:, :block], down_shard[:, :block], output_weight.T.astype(low)], axis=1
    )
    last_shard = jnp.concatenate([up_shard[:, block:], down_shard[:, block:]], axis=1)

    if fast:
        found = gather_planes(inward_shard, size)
        found_first = gather_doubled(after(first_shard, *found[1:]), size)
        found_last = gather_doubled(after(last_shard, found_first[1]), size)
        turned = turn(activations)
        found[0] = after(found[0], turned)
        own = split_halves(found)
        pairs = gather_pairs(own, gather_near(own, size))
        far = gather_far(pairs, size)
        own_first = split_halves(doubled_planes(*found_first))
        far = after_all(far, *own_first)
        own_first = after_all(own_first, *far)
        inward = place(pairs, far, me)
        near_first = gather_near(own_first, size)
        inward = after(inward, *own_first)
    else:
        inward, mid_first, mid_last = [
            lax.all_gather(shard, "dp", axis=0, tiled=True)
            for shard in (inward_shard, first_shard, last_shard)
        ]
        turned = turn(activations)

    smalls = inward[:, 3 * width : 3 * width + per_row].astype(full).reshape(size, -1)
    heads_size, hidden_size = heads_bias.size, hidden_bias.size
    head_biases = (
        smalls[:, :heads_size].reshape(size, 2, -1).transpose(1, 2, 0).reshape(2, width)
    )
    hidden_biases = smalls[:, heads_size : heads_size + hidden_size].T.reshape(1, hidden_width)
    vectors = (
        smalls[:, heads_size + hidden_size :].reshape(size, 6, rows).transpose(1, 0, 2)
    ).reshape(6, D)

    live = lax.broadcasted_iota(jnp.int32, (count, LEN), 1) < lengths[:, None]
    scale = (token_weight.reshape(count, LEN) * live.astype(jnp.int32)).astype(full)
    scale = scale.reshape(tokens, 1)

    first_pair = attend(lengths, activations, inward, head_biases, 0, 1)
    if fast:
        near_first = after_all(near_first, first_pair[2])
        pairs_first = gather_pairs(own_first, near_first)
        far_first = gather_far(pairs_first, size)
        own_last = split_halves(doubled_planes(*after_all(found_last, *pairs_first)))
        near_last = gather_near(own_last, size)
        gated = after(activations, *pairs_first, *own_last, vectors, hidden_biases)
    else:
        gated = after(activations, first_pair[2])
    later_pairs = attend(lengths, gated, inward, head_biases, 1, groups - 1)
    contexts = [first_pair[2], later_pairs[2]]
    if fast:
        pairs_last = gather_pairs(own_last, after_all(near_last, later_pairs[2]))
        far_last = gather_far(pairs_last, size)
        mid_first = place(pairs_first, after_all(far_first, *pairs_last), me)

    mine = outward_part(contexts, mid_first, outward_at)
    total, active_first, slope_first, middle, normed, inverse = expand_first(
        mine, swap_cores(mine), activations, vectors, hidden_biases, mid_first
    )
    if fast:
        mid_last = place(pairs_last, after_all(far_last, total), me)
    mine_down, active_last, slope_last = expand_last(total, middle, hidden_biases, mid_last)
    (
        mine_middle, second_sums, hidden_sums, output_rows,
        second_grad, second_low, hidden_first, hidden_last,
    ) = contract(
        mine_down, swap_cores(mine_down), normed, cotangent, scale, vectors,
        (slope_first, slope_last), (mid_first, mid_last),
    )
    other_middle = swap_cores(mine_middle)
    actives, hiddens = (active_first, active_last), (hidden_first, hidden_last)

    def back_first(*gates):
        return first_back(
            after(mine_middle, *gates), other_middle, second_grad, normed, inverse, vectors,
            mid_first, outward_at, width,
        )

    def attention_grads(group, *gates):
        at = max(group - 1, 0)
        qkv, weights, _ = later_pairs if group else first_pair
        return attend_back(after(qkv, *gates), weights, at, context_grad, group)

    def heads_outgoing(sums):
        return jnp.concatenate(sums, axis=1).reshape(2, -1, size).transpose(2, 0, 1)

    def small_outgoing(first_sums, head_sums):
        norm_grad = jnp.concatenate([first_sums, second_sums])
        return jnp.concatenate(
            [
                heads_outgoing(head_sums).reshape(size, -1),
                hidden_sums.reshape(-1, size).T,
                norm_grad.reshape(6, size, rows).transpose(1, 0, 2).reshape(size, -1),
            ],
            axis=1,
        )

    stacked, head_sums = [], []
    if fast:
        sent_down, kept_down = weight_grad(second_low, actives, me, size, 0)
        got_down = hop(sent_down, 1, size)
        sent_up, kept_up = weight_grad(after(middle, sent_down), hiddens, me, size, 1)
        got_up = hop(sent_up, 2, size)
        first_sums, first_grad, first_low, context_grad = back_first(sent_up)

        got_down = after(got_down, first_low)
        next_down = kept_down[1] + got_down[1]
        more_down = hop(next_down, 2, size)
        sent_out, kept_out = weight_grad(after(first_low, next_down), contexts, me, size, 0)
        got_out = hop(sent_out, 1, size)

        def attention(group, *gates):
            grads, sums = attention_grads(group, *gates)
            stacked.append(grads)
            head_sums.append(sums)

        attention(0, sent_out)
        sent_0, kept_0 = weight_grad(turned, [stacked[0]], me, size, 1, True)
        got_0 = hop(sent_0, 2, size)
        got_up = after(got_up, sent_0)
        next_up = kept_up[1] + got_up[1]
        more_up = hop(next_up, 1, size)

        attention(1, next_up)
        got_out, got_0, more_down = after_all((got_out, got_0, more_down), stacked[1])
        next_out, next_0 = after_all((kept_out[1] + got_out[1], kept_0[1] + got_0[1]))
        more_out, more_0 = hop(next_out, 2, size), hop(next_0, 1, size)
        own_down, out_down = combine([(kept_down, got_down, more_down)])
        near_down = hop(out_down, 4, size)
        gated = after(turned, next_out, next_0, out_down)
        sent_1, kept_1 = weight_grad(gated, [stacked[1]], me, size, 0, True)
        got_1 = hop(sent_1, 1, size)

        attention(2, sent_1)
        extra = small_outgoing(first_sums, head_sums).reshape(size, rows, per_row)
        extra = jnp.pad(extra, ((0, 0), (0, 0), (0, LANES - per_row))).astype(low)
        more_up, near_down, more_out, more_0 = after_all(
            (more_up, near_down, more_out, more_0), stacked[2]
        )
        own_up, out_up = combine([(kept_up, got_up, more_up)])
        near_up = hop(out_up, 4, size)
        next_far = far_half(own_down, near_down)
        far_down = hop(next_far, 8, size)
        own_near, out_near = combine([(kept_out, got_out, more_out), (kept_0, got_0, more_0)])
        near_near = hop(out_near, 4, size)
        gated = after(turned, out_up, next_far, out_near)
        sent_2, kept_2 = weight_grad(gated, [stacked[2]], me, size, 1, True, extra)
        got_2 = hop(sent_2, 2, size)

        mine_source = source_part([after(stacked[0], sent_2)] + stacked[1:], inward)
        other_source = swap_cores(mine_source)
        near_up, got_1, got_2 = after_all((near_up, got_1, got_2), mine_source)
        next_far = far_half(own_up, near_up)
        far_up = hop(next_far, 8, size)
        got_1, got_2 = after_all((got_1, got_2), next_far)
        next_1, next_2 = after_all((kept_1[1] + got_1[1], kept_2[1] + got_2[1]))
        more_1, more_2 = hop(next_1, 2, size), hop(next_2, 1, size)
        near_near, far_down = after_all((near_near, far_down), next_1, next_2)
        next_far = far_half(own_near, near_near)
        far_near = hop(next_far, 8, size)
        more_1, more_2 = after_all((more_1, more_2), next_far)
        own_last, out_last = combine([(kept_1, got_1, more_1), (kept_2, got_2, more_2)])
        near_last = hop(out_last, 4, size)
        input_grad = finish(mine_source, after(other_source, out_last), first_grad)
        near_last = after(near_last, input_grad)
        far_last = hop(far_half(own_last, near_last), 8, size)
        downward_grad = reduce_sum(own_down, near_down, far_down)
        upward_grad = reduce_sum(own_up, near_up, far_up)
        near_grad = reduce_sum(own_near, near_near, far_near)
        far_grad = reduce_sum(own_last, near_last, far_last)
        outward_grad = near_grad[:, :width]
        cut = 3 * LANES
        inward_grads = [near_grad[:, width:], far_grad[:, :cut], far_grad[:, cut : 2 * cut]]
        small_grad = far_grad[:, 2 * cut : 2 * cut + per_row].reshape(-1)
    else:

        def reduced(left, rights, turned=False):
            (value,) = weight_grad(left, rights, None, size, None, turned)
            return lax.psum_scatter(value, "dp", scatter_dimension=0, tiled=True)

        first_sums, first_grad, first_low, context_grad = back_first()
        downward_grad = reduced(second_low, actives)
        upward_grad = reduced(middle, hiddens)
        outward_grad = reduced(first_low, contexts)
        inward_grads = []
        for group in range(groups):
            grads, sums = attention_grads(group)
            stacked.append(grads)
            head_sums.append(sums)
            inward_grads.append(reduced(turned, [grads], True))
        mine_source = source_part(stacked, inward)
        small_grad = lax.psum_scatter(
            small_outgoing(first_sums, head_sums), "dp", scatter_dimension=0, tiled=True
        ).reshape(-1)
        input_grad = finish(mine_source, swap_cores(mine_source), first_grad)

    inward_grad = jnp.stack(
        [
            jnp.concatenate(
                [grad[:, kind * LANES : (kind + 1) * LANES] for grad in inward_grads], axis=1
            )
            for kind in range(3)
        ]
    )
    grads = (
        inward_grad,
        outward_grad.T,
        upward_grad,
        downward_grad.T,
        small_grad[:heads_size].reshape(heads_bias.shape),
        small_grad[heads_size : heads_size + hidden_size].reshape(hidden_bias.shape),
        small_grad[heads_size + hidden_size :].reshape(norm_vectors.shape),
    )

    step_value = step_count[0].astype(full)
    correct = 1.0 - jnp.power(0.5, step_value)
    plan = (step_value + 4.0) / 12.0
    rates = (D ** (-0.5), (6 * D // LEN) ** (-0.5), D ** (-0.5), FF ** (-0.5), 0.5, 0.5, 0.3)
    decays = (0.01, 0.01, 0.01, 0.01, 0.0, 0.0, 0.0)
    masters = (
        inward_weight,
        output_weight,
        up_weight,
        down_weight,
        heads_bias,
        hidden_bias,
        norm_vectors,
    )
    results = [output_rows, input_grad]
    for at in range(7):
        results.extend(
            adamw(
                masters[at],
                grads[at],
                moments[at],
                moments[7 + at],
                rates[at] * plan,
                decays[at],
                correct,
            )
        )
    return tuple(results)


def solution(mesh):
    matrices = (
        P(None, "dp", "tensor"),
        P("tensor", "dp"),
        P("dp", "tensor"),
        P("tensor", "dp"),
        P(None, "tensor", "dp"),
        P("tensor", "dp"),
        P(None, "dp"),
    )
    in_specs = (
        (P("dp", None), P("dp", None), P("dp"), P("dp"), P()) + matrices + matrices + matrices
    )
    out_specs = (P("dp", None), P("dp", None)) + tuple(
        spec for spec in matrices for _ in range(3)
    )
    return jax.shard_map(
        per_device, mesh=mesh, in_specs=in_specs, out_specs=out_specs, check_vma=False
    )
```

profile of v0, /device:TPU:0, one launch (start us, length us, event | category | flops | bytes accessed | tf_op | source)
XLA Modules:
  0.0 286.6 jit_solution(551562121244899258)
XLA Ops:
  4.5 3.1 %collective-permute-start = (bf16[48,1280]{1,0:T(8,128)(2,1)S(1)}, bf16[48,1280]{1,0:T(8,128)(2,1)S(1)}, u32[]{:S(2)}, u32[]{:S(2)}) collective-permute-start(bf16[48,1280]{1,0:T(8,128)(2,1)S(1)} %fusion.6), channel_id=1, source_target_pairs={{0,8},{2,10},{4,12},{6,14},{8,0},{10,2},{12,4},{14,6},{16,24},{18,... | collective-permute-start | bytes 368648 | tf_op jit(solution)/shard_map/ppermute | solution.py:85
  7.6 2.6 collective-permute-start.1
  15.6 4.3 %collective-permute-done.1 = bf16[48,1280]{1,0:T(8,128)(2,1)S(1)} collective-permute-done((bf16[48,1280]{1,0:T(8,128)(2,1)S(1)}, bf16[48,1280]{1,0:T(8,128)(2,1)S(1)}, u32[]{:S(2)}, u32[]{:S(2)}) %collective-permute-start.1) | collective-permute-done | bytes 122912 | tf_op jit(solution)/shard_map/ppermute | solution.py:85
  19.9 3.1 %collective-permute-start.7 = (bf16[48,1920]{1,0:T(8,128)(2,1)S(1)}, bf16[48,1920]{1,0:T(8,128)(2,1)S(1)}, u32[]{:S(2)}, u32[]{:S(2)}) collective-permute-start(bf16[48,1920]{1,0:T(8,128)(2,1)S(1)} %pad_maximum_fusion.13), channel_id=1, source_target_pairs={{0,16},{2,18},{4,20},{6,22},{8,24},{10,26},{12,28},{14,30},{16,0},... | collective-permute-start | bytes 552968 | tf_op jit(solution)/shard_map/ppermute | solution.py:85
  23.1 1.6 collective-permute-start.4
  26.2 4.3 %collective-permute-done.7 = bf16[48,1920]{1,0:T(8,128)(2,1)S(1)} collective-permute-done((bf16[48,1920]{1,0:T(8,128)(2,1)S(1)}, bf16[48,1920]{1,0:T(8,128)(2,1)S(1)}, u32[]{:S(2)}, u32[]{:S(2)}) %collective-permute-start.7) | collective-permute-done | bytes 184352 | tf_op jit(solution)/shard_map/ppermute | solution.py:85
  33.9 6.6 %collective-permute-done.8 = bf16[2,48,1920]{2,1,0:T(8,128)(2,1)S(1)} collective-permute-done((bf16[2,48,1920]{2,1,0:T(8,128)(2,1)S(1)}, bf16[2,48,1920]{2,1,0:T(8,128)(2,1)S(1)}, u32[]{:S(2)}, u32[]{:S(2)}) %collective-permute-start.8) | collective-permute-done | bytes 368672 | tf_op jit(solution)/shard_map/ppermute | solution.py:85
  40.8 8.1 %collective-permute-done.11 = bf16[48,1536]{1,0:T(8,128)(2,1)S(1)} collective-permute-done((bf16[48,1536]{1,0:T(8,128)(2,1)S(1)}, bf16[48,1536]{1,0:T(8,128)(2,1)S(1)}, u32[]{:S(2)}, u32[]{:S(2)}) %collective-permute-start.11) | collective-permute-done | bytes 147488 | tf_op jit(solution)/shard_map/ppermute | solution.py:85
  49.8 1.6 collective-permute-start.9
  53.4 8.2 %attend.2 = (bf16[1536,384]{1,0:T(8,128)(2,1)}, bf16[3,2,512,512]{3,2,1,0:T(8,128)(2,1)}, bf16[1536,128]{1,0:T(8,128)(2,1)}) custom-call(s32[3]{0:T(128)S(1)} %copy-done.26, bf16[1536,768]{1,0:T(8,128)(2,1)} %x_ref.4, bf16[768,1280]{1,0:T(8,128)(2,1)S(1)} %place.3.w_ref.refs_3_, f32[2,384]{1,0:T(2,128)S(1)} %reshape.207.bias_ref), custom_call_target="tpu_custom_call" | custom-call | flops 1711276032 | bytes 3145728 | tf_op jit(solution)/shard_map/attend/pallas_call | solution.py:259
  69.6 14.4 %attend.3 = (bf16[1536,768]{1,0:T(8,128)(2,1)}, bf16[6,2,512,512]{3,2,1,0:T(8,128)(2,1)}, bf16[1536,256]{1,0:T(8,128)(2,1)}) custom-call(s32[3]{0:T(128)S(1)} %copy-done.26, bf16[1536,768]{1,0:T(8,128)(2,1)} %x_ref.4, bf16[768,1280]{1,0:T(8,128)(2,1)S(1)} %place.3.w_ref.refs_3_, f32[2,384]{1,0:T(2,128)S(1)} %reshape.207.bias_ref), custom_call_target="tpu_custom_call" | custom-call | flops 3422552064 | bytes 6291456 | tf_op jit(solution)/shard_map/attend/pallas_call | solution.py:259
  83.9 2.2 collective-permute-done.15
  86.1 1.9 collective-permute-done.16
  88.3 4.5 %outward.1.mine_ref = bf16[1536,768]{1,0:T(8,128)(2,1)S(1)} custom-call(bf16[1536,128]{1,0:T(8,128)(2,1)} %get-tuple-element.153.refs_0_, bf16[1536,256]{1,0:T(8,128)(2,1)} %get-tuple-element.164.refs_1_, bf16[768,1920]{1,0:T(8,128)(2,1)S(1)} %place.4.refs_2_.up_ref.down_ref.up_first.down_first.w_ref), custom_call_target="tpu_custom_call" | custom-call | flops 905969664 | bytes 4128768 | tf_op jit(solution)/shard_map/outward/pallas_call | solution.py:368
  94.1 3.4 %collective-permute-done.17.other_ref = bf16[1536,768]{1,0:T(8,128)(2,1)S(1)} collective-permute-done((bf16[1536,768]{1,0:T(8,128)(2,1)S(1)}, bf16[1536,768]{1,0:T(8,128)(2,1)S(1)}, u32[]{:S(2)}, u32[]{:S(2)}) %collective-permute-start.17) | collective-permute-done | bytes 2359328 | tf_op jit(solution)/shard_map/ppermute | solution.py:89
  97.4 10.4 %expand_first.1 = (f32[1536,768]{1,0:T(8,128)}, bf16[1536,768]{1,0:T(8,128)(2,1)}, bf16[1536,768]{1,0:T(8,128)(2,1)}, bf16[1536,768]{1,0:T(8,128)(2,1)}, f32[1536,768]{1,0:T(8,128)}, /*index=5*/f32[1536,1]{1,0:T(8,128)}) custom-call(bf16[1536,768]{1,0:T(8,128)(2,1)S(1)} %outward.1.mine_ref, bf16[1536,768]{1,0:T(8,128)(2,1)S(1)} %collective-permute-done.17.other_ref, ...), custom_call_target="tpu_custom_call" | custom-call | flops 3623878656 | bytes 21233664 | tf_op jit(solution)/shard_map/expand_first/pallas_call | solution.py:411
  109.1 9.9 %expand_last.1 = (bf16[1536,768]{1,0:T(8,128)(2,1)}, bf16[1536,768]{1,0:T(8,128)(2,1)}, bf16[1536,768]{1,0:T(8,128)(2,1)}) custom-call(f32[1536,768]{1,0:T(8,128)} %get-tuple-element.171.total_ref, bf16[1536,768]{1,0:T(8,128)(2,1)} %get-tuple-element.186.middle_ref.left_ref, f32[1,1536]{1,0:T(1,128)S(1)} %reshape.210.bias_ref, ...), custom_call_target="tpu_custom_call" | custom-call | flops 3623878656 | bytes 14155776 | tf_op jit(solution)/shard_map/expand_last/pallas_call | solution.py:453
  119.5 4.5 %collective-permute-done.20.other_ref = bf16[1536,768]{1,0:T(8,128)(2,1)} collective-permute-done((bf16[1536,768]{1,0:T(8,128)(2,1)}, bf16[1536,768]{1,0:T(8,128)(2,1)}, u32[]{:S(2)}, u32[]{:S(2)}) %collective-permute-start.20) | collective-permute-done | bytes 2359328 | tf_op jit(solution)/shard_map/ppermute | solution.py:89
  124.0 1.7 copy-done.3
  125.6 18.1 %contract.1 = (bf16[1536,768]{1,0:T(8,128)(2,1)}, f32[3,768]{1,0:T(4,128)S(1)}, f32[1,1536]{1,0:T(1,128)S(1)}, bf16[1536,768]{1,0:T(8,128)(2,1)}, f32[1536,768]{...) custom-call(bf16[1536,768]{1,0:T(8,128)(2,1)} %get-tuple-element.175.mine_ref, ...), custom_call_target="tpu_custom_call" | custom-call | flops 7247757312 | bytes 14155776 | tf_op jit(solution)/shard_map/contract/pallas_call | solution.py:513
  143.9 1.7 copy-done.29
  145.6 5.4 %weight_grad.6 = (bf16[2,4,48,1536]{3,2,1,0:T(8,128)(2,1)}, bf16[2,4,48,1536]{3,2,1,0:T(8,128)(2,1)S(1)}) custom-call(s32[1]{0:T(128)} %bitcast.me_ref, bf16[1536,768]{1,0:T(8,128)(2,1)S(1)} %copy-done.29, bf16[1536,768]{1,0:T(8,128)(2,1)S(1)} %copy-done.33, bf16[1536,768]{1,0:T(8,128)(2,1)S(1)} %copy-done.34), custom_call_target="tpu_custom_call" | custom-call | flops 3623878656 | bytes 7077888 | tf_op jit(solution)/shard_map/weight_grad/pallas_call | solution.py:720
  153.5 5.4 %weight_grad.7 = (bf16[2,4,48,1536]{3,2,1,0:T(8,128)(2,1)}, bf16[2,4,48,1536]{3,2,1,0:T(8,128)(2,1)S(1)}) custom-call(s32[1]{0:T(128)} %bitcast.me_ref, bf16[1536,768]{1,0:T(8,128)(2,1)S(1)} %copy-done.32, bf16[1536,768]{1,0:T(8,128)(2,1)S(1)} %copy-done.27, bf16[1536,768]{1,0:T(8,128)(2,1)S(1)} %copy-done.28), custom_call_target="tpu_custom_call" | custom-call | flops 3623878656 | bytes 7077888 | tf_op jit(solution)/shard_map/weight_grad/pallas_call | solution.py:720
  161.8 10.9 %first_back.1 = (f32[3,768]{1,0:T(4,128)S(1)}, f32[1536,768]{1,0:T(8,128)}, bf16[1536,768]{1,0:T(8,128)(2,1)}, bf16[1536,384]{1,0:T(8,128)(2,1)}) custom-call(bf16[1536,768]{1,0:T(8,128)(2,1)} %get-tuple-element.190.mine_ref, bf16[1536,768]{1,0:T(8,128)(2,1)} %collective-permute-done.21.other_ref, f32[1536,768]{1,0:T(8,128)} %get-tuple-element.191.second_ref, ...), custom_call_target="tpu_custom_call" | custom-call | flops 905969664 | bytes 23592960 | tf_op jit(solution)/shard_map/first_back/pallas_call | solution.py:579
  172.6 7.9 %collective-permute-done.22.refs_1_ = bf16[2,4,48,1536]{3,2,1,0:T(8,128)(2,1)} collective-permute-done((bf16[2,4,48,1536]{3,2,1,0:T(8,128)(2,1)}, bf16[2,4,48,1536]{3,2,1,0:T(8,128)(2,1)}, u32[]{:S(2)}, u32[]{:S(2)}) %collective-permute-start.22) | collective-permute-done | bytes 1179680 | tf_op jit(solution)/shard_map/ppermute | solution.py:85
  180.6 1.9 add_bitcast_fusion.1
  183.0 1.7 copy-done.13
  184.7 2.4 weight_grad.8
  188.6 6.7 %attend_back.3 = (bf16[1536,384]{1,0:T(8,128)(2,1)}, f32[2,128]{1,0:T(2,128)S(1)}) custom-call(bf16[1536,384]{1,0:T(8,128)(2,1)} %get-tuple-element.198.qkv_ref, bf16[3,2,512,512]{3,2,1,0:T(8,128)(2,1)} %get-tuple-element.199.weight_ref, bf16[1536,384]{1,0:T(8,128)(2,1)} %get-tuple-element.200.grad_ref), custom_call_target="tpu_custom_call" | custom-call | flops 1610612736 | bytes 5505024 | tf_op jit(solution)/shard_map/attend_back/pallas_call | solution.py:330
  196.6 2.3 weight_grad.9
  200.5 2.0 add_bitcast_fusion
  203.0 6.6 %attend_back.4 = (bf16[1536,384]{1,0:T(8,128)(2,1)}, f32[2,128]{1,0:T(2,128)S(1)}) custom-call(bf16[1536,768]{1,0:T(8,128)(2,1)} %get-tuple-element.219.qkv_ref, bf16[6,2,512,512]{3,2,1,0:T(8,128)(2,1)} %get-tuple-element.207.weight_ref, bf16[1536,384]{1,0:T(8,128)(2,1)} %get-tuple-element.200.grad_ref), custom_call_target="tpu_custom_call" | custom-call | flops 1610612736 | bytes 5505024 | tf_op jit(solution)/shard_map/attend_back/pallas_call | solution.py:330
  214.2 1.7 add_bitcast_fusion.4
  215.8 1.7 add_bitcast_fusion.5
  220.8 2.2 combine.4
  223.8 1.7 collective-permute-start.28
  225.5 1.6 weight_grad.10
  227.2 6.8 %attend_back.5 = (bf16[1536,384]{1,0:T(8,128)(2,1)}, f32[2,128]{1,0:T(2,128)S(1)}) custom-call(bf16[1536,768]{1,0:T(8,128)(2,1)} %get-tuple-element.219.qkv_ref, bf16[6,2,512,512]{3,2,1,0:T(8,128)(2,1)} %get-tuple-element.207.weight_ref, bf16[1536,384]{1,0:T(8,128)(2,1)} %get-tuple-element.200.grad_ref), custom_call_target="tpu_custom_call" | custom-call | flops 1610612736 | bytes 5505024 | tf_op jit(solution)/shard_map/attend_back/pallas_call | solution.py:330
  241.6 1.7 weight_grad.11
  243.2 1.6 collective-permute-start.34
  246.4 1.8 collective-permute-start.37
  248.2 6.6 %source.1.mine_ref = bf16[1536,768]{1,0:T(8,128)(2,1)S(1)} custom-call(bf16[1536,384]{1,0:T(8,128)(2,1)} %get-tuple-element.236.refs_0_, bf16[1536,384]{1,0:T(8,128)(2,1)} %get-tuple-element.208.refs_0_.refs_1_, bf16[1536,384]{1,0:T(8,128)(2,1)} %get-tuple-element.220.refs_0_.refs_2_, bf16[768,1280]{1,0:T(8,128)(2,1)S(1)} %copy-done.11), custom_call_target="tpu_custom_call" | custom-call | flops 2717908992 | bytes 5308416 | tf_op jit(solution)/shard_map/source/pallas_call | solution.py:614
  256.0 1.9 collective-permute-start.42
  261.3 2.0 multiply_subtract_fusion
  263.2 5.2 %collective-permute-done.39 = bf16[48,768]{1,0:T(8,128)(2,1)S(1)} collective-permute-done((bf16[48,768]{1,0:T(8,128)(2,1)S(1)}, bf16[48,768]{1,0:T(8,128)(2,1)S(1)}, u32[]{:S(2)}, u32[]{:S(2)}) %collective-permute-start.39) | collective-permute-done | bytes 73760 | tf_op jit(solution)/shard_map/ppermute | solution.py:85
  269.5 6.2 %finish.1 = f32[1536,768]{1,0:T(8,128)} custom-call(bf16[1536,768]{1,0:T(8,128)(2,1)S(1)} %source.1.mine_ref, bf16[1536,768]{1,0:T(8,128)(2,1)S(1)} %collective-permute-done.31.other_ref, f32[1536,768]{1,0:T(8,128)} %get-tuple-element.253.first_ref), custom_call_target="tpu_custom_call" | custom-call | flops 2359296 | bytes 14155776 | tf_op jit(solution)/shard_map/finish/pallas_call | solution.py:632
  275.8 3.2 %collective-permute-start.41 = (bf16[48,896]{1,0:T(8,128)(2,1)S(1)}, bf16[48,896]{1,0:T(8,128)(2,1)S(1)}, u32[]{:S(2)}, u32[]{:S(2)}) collective-permute-start(bf16[48,896]{1,0:T(8,128)(2,1)S(1)} %fusion.7), channel_id=1, source_target_pairs={{0,16},{2,18},{4,20},{6,22},{8,24},{10,26},{12,28},{14,30},{16,0},... | collective-permute-start | bytes 258056 | tf_op jit(solution)/shard_map/ppermute | solution.py:85
  280.2 3.2 %collective-permute-done.41 = bf16[48,896]{1,0:T(8,128)(2,1)S(1)} collective-permute-done((bf16[48,896]{1,0:T(8,128)(2,1)S(1)}, bf16[48,896]{1,0:T(8,128)(2,1)S(1)}, u32[]{:S(2)}, u32[]{:S(2)}) %collective-permute-start.41) | collective-permute-done | bytes 86048 | tf_op jit(solution)/shard_map/ppermute | solution.py:85
  (283 shorter events, 66.1 us)
Async XLA Ops:
  4.5 11.1 %collective-permute-start = (bf16[48,1280]{1,0:T(8,128)(2,1)S(1)}, bf16[48,1280]{1,0:T(8,128)(2,1)S(1)}, u32[]{:S(2)}, u32[]{:S(2)}) collective-permute-start(bf16[48,1280]{1,0:T(8,128)(2,1)S(1)} %fusion.6), channel_id=1, source_target_pairs={{0,8},{2,10},{4,12},{6,14},{8,0},{10,2},{12,4},{14,6},{16,24},{18,... | collective-permute-start | bytes 368648 | tf_op jit(solution)/shard_map/ppermute | solution.py:85
  7.6 12.3 %collective-permute-start.1 = (bf16[48,1280]{1,0:T(8,128)(2,1)S(1)}, bf16[48,1280]{1,0:T(8,128)(2,1)S(1)}, u32[]{:S(2)}, u32[]{:S(2)}) collective-permute-start(bf16[48,1280]{1,0:T(8,128)(2,1)S(1)} %fusion.6), channel_id=1, source_target_pairs={{0,16},{2,18},{4,20},{6,22},{8,24},{10,26},{12,28},{14,30},{16,0},... | collective-permute-start | bytes 368648 | tf_op jit(solution)/shard_map/ppermute | solution.py:85
  10.2 9.7 %collective-permute-start.2 = (bf16[48,1280]{1,0:T(8,128)(2,1)S(1)}, bf16[48,1280]{1,0:T(8,128)(2,1)S(1)}, u32[]{:S(2)}, u32[]{:S(2)}) collective-permute-start(bf16[48,1280]{1,0:T(8,128)(2,1)S(1)} %fusion.6), channel_id=1, source_target_pairs={{0,24},{2,26},{4,28},{6,30},{8,16},{10,18},{12,20},{14,22},{16,8},... | collective-permute-start | bytes 368648 | tf_op jit(solution)/shard_map/ppermute | solution.py:85
  19.9 10.6 %collective-permute-start.7 = (bf16[48,1920]{1,0:T(8,128)(2,1)S(1)}, bf16[48,1920]{1,0:T(8,128)(2,1)S(1)}, u32[]{:S(2)}, u32[]{:S(2)}) collective-permute-start(bf16[48,1920]{1,0:T(8,128)(2,1)S(1)} %pad_maximum_fusion.13), channel_id=1, source_target_pairs={{0,16},{2,18},{4,20},{6,22},{8,24},{10,26},{12,28},{14,30},{16,0},... | collective-permute-start | bytes 552968 | tf_op jit(solution)/shard_map/ppermute | solution.py:85
  23.1 7.5 %collective-permute-start.4 = (bf16[4,48,640]{2,1,0:T(8,128)(2,1)S(1)}, bf16[4,48,640]{2,1,0:T(8,128)(2,1)S(1)}, u32[]{:S(2)}, u32[]{:S(2)}) collective-permute-start(bf16[4,48,640]{2,1,0:T(8,128)(2,1)S(1)} %get-tuple-element.142), channel_id=1, source_target_pairs={{0,2},{2,0},{4,6},{6,4},{8,10},{10,8},{12,14},{14,12},{16,18},{18,... | collective-permute-start | bytes 737288 | tf_op jit(solution)/shard_map/ppermute | solution.py:85
  24.7 6.2 %collective-permute-start.3 = (bf16[4,48,640]{2,1,0:T(8,128)(2,1)S(1)}, bf16[4,48,640]{2,1,0:T(8,128)(2,1)S(1)}, u32[]{:S(2)}, u32[]{:S(2)}) collective-permute-start(bf16[4,48,640]{2,1,0:T(8,128)(2,1)S(1)} %get-tuple-element.141), channel_id=1, source_target_pairs={{0,4},{2,6},{4,0},{6,2},{8,12},{10,14},{12,8},{14,10},{16,20},{18,... | collective-permute-start | bytes 737288 | tf_op jit(solution)/shard_map/ppermute | solution.py:85
  30.6 10.0 %collective-permute-start.8 = (bf16[2,48,1920]{2,1,0:T(8,128)(2,1)S(1)}, bf16[2,48,1920]{2,1,0:T(8,128)(2,1)S(1)}, u32[]{:S(2)}, u32[]{:S(2)}) collective-permute-start(bf16[2,48,1920]{2,1,0:T(8,128)(2,1)S(1)} %pad_maximum_fusion.9), channel_id=1, source_target_pairs={{0,8},{2,10},{4,12},{6,14},{8,0},{10,2},{12,4},{14,6},{16,24},{18,... | collective-permute-start | bytes 1105928 | tf_op jit(solution)/shard_map/ppermute | solution.py:85
  30.9 18.7 %collective-permute-start.5 = (bf16[8,48,640]{2,1,0:T(8,128)(2,1)S(1)}, bf16[8,48,640]{2,1,0:T(8,128)(2,1)S(1)}, u32[]{:S(2)}, u32[]{:S(2)}) collective-permute-start(bf16[8,48,640]{2,1,0:T(8,128)(2,1)S(1)} %pad_maximum_fusion.7.pair_a), channel_id=1, source_target_pairs={{0,2},{2,0},{4,6},{6,4},{8,10},{10,8},{12,14},{14,12},{16,18},{18,... | collective-permute-start | bytes 1474568 | tf_op jit(solution)/shard_map/ppermute | solution.py:85
  32.4 17.3 %collective-permute-start.6 = (bf16[8,48,640]{2,1,0:T(8,128)(2,1)S(1)}, bf16[8,48,640]{2,1,0:T(8,128)(2,1)S(1)}, u32[]{:S(2)}, u32[]{:S(2)}) collective-permute-start(bf16[8,48,640]{2,1,0:T(8,128)(2,1)S(1)} %pad_maximum_fusion.8.pair_b), channel_id=1, source_target_pairs={{0,4},{2,6},{4,0},{6,2},{8,12},{10,14},{12,8},{14,10},{16,20},{18,... | collective-permute-start | bytes 1474568 | tf_op jit(solution)/shard_map/ppermute | solution.py:85
  40.5 8.4 %collective-permute-start.11 = (bf16[48,1536]{1,0:T(8,128)(2,1)S(1)}, bf16[48,1536]{1,0:T(8,128)(2,1)S(1)}, u32[]{:S(2)}, u32[]{:S(2)}) collective-permute-start(bf16[48,1536]{1,0:T(8,128)(2,1)S(1)} %pad_maximum_fusion.14), channel_id=1, source_target_pairs={{0,16},{2,18},{4,20},{6,22},{8,24},{10,26},{12,28},{14,30},{16,0},... | collective-permute-start | bytes 442376 | tf_op jit(solution)/shard_map/ppermute | solution.py:85
  49.6 15.0 %collective-permute-start.12 = (bf16[2,48,1536]{2,1,0:T(8,128)(2,1)}, bf16[2,48,1536]{2,1,0:T(8,128)(2,1)}, u32[]{:S(2)}, u32[]{:S(2)}) collective-permute-start(bf16[2,48,1536]{2,1,0:T(8,128)(2,1)} %pad_maximum_fusion.11), channel_id=1, source_target_pairs={{0,8},{2,10},{4,12},{6,14},{8,0},{10,2},{12,4},{14,6},{16,24},{18,... | collective-permute-start | bytes 884744 | tf_op jit(solution)/shard_map/ppermute | solution.py:85
  49.8 19.7 %copy-start.10 = (bf16[768,1280]{1,0:T(8,128)(2,1)}, bf16[768,1280]{1,0:T(8,128)(2,1)S(1)}, u32[]{:S(2)}) copy-start(bf16[768,1280]{1,0:T(8,128)(2,1)S(1)} %place.3.w_ref.refs_3_) | copy-start | bytes 5898244
  49.8 12.3 %collective-permute-start.9 = (bf16[4,48,1024]{2,1,0:T(8,128)(2,1)S(1)}, bf16[4,48,1024]{2,1,0:T(8,128)(2,1)S(1)}, u32[]{:S(2)}, u32[]{:S(2)}) collective-permute-start(bf16[4,48,1024]{2,1,0:T(8,128)(2,1)S(1)} %slice.273), channel_id=1, source_target_pairs={{0,4},{2,6},{4,0},{6,2},{8,12},{10,14},{12,8},{14,10},{16,20},{18,... | collective-permute-start | bytes 1179656 | tf_op jit(solution)/shard_map/ppermute | solution.py:85
  51.4 10.7 %collective-permute-start.10 = (bf16[4,48,896]{2,1,0:T(8,128)(2,1)S(1)}, bf16[4,48,896]{2,1,0:T(8,128)(2,1)}, u32[]{:S(2)}, u32[]{:S(2)}) collective-permute-start(bf16[4,48,896]{2,1,0:T(8,128)(2,1)S(1)} %pad_maximum_fusion.10), channel_id=1, source_target_pairs={{0,2},{2,0},{4,6},{6,4},{8,10},{10,8},{12,14},{14,12},{16,18},{18,... | collective-permute-start | bytes 1032200 | tf_op jit(solution)/shard_map/ppermute | solution.py:85
  63.2 24.8 %collective-permute-start.13 = (bf16[8,48,1024]{2,1,0:T(8,128)(2,1)S(1)}, bf16[8,48,1024]{2,1,0:T(8,128)(2,1)S(1)}, u32[]{:S(2)}, u32[]{:S(2)}) collective-permute-start(bf16[8,48,1024]{2,1,0:T(8,128)(2,1)S(1)} %pad_maximum_fusion.pair_a), channel_id=1, source_target_pairs={{0,2},{2,0},{4,6},{6,4},{8,10},{10,8},{12,14},{14,12},{16,18},{18,... | collective-permute-start | bytes 2359304 | tf_op jit(solution)/shard_map/ppermute | solution.py:85
  63.8 24.2 %collective-permute-start.14 = (bf16[8,48,896]{2,1,0:T(8,128)(2,1)S(1)}, bf16[8,48,896]{2,1,0:T(8,128)(2,1)S(1)}, u32[]{:S(2)}, u32[]{:S(2)}) collective-permute-start(bf16[8,48,896]{2,1,0:T(8,128)(2,1)S(1)} %pad_maximum_fusion.2.pair_b), channel_id=1, source_target_pairs={{0,4},{2,6},{4,0},{6,2},{8,12},{10,14},{12,8},{14,10},{16,20},{18,... | collective-permute-start | bytes 2064392 | tf_op jit(solution)/shard_map/ppermute | solution.py:85
  66.7 19.4 %collective-permute-start.15 = (bf16[4,48,768]{2,1,0:T(8,128)(2,1)S(1)}, bf16[4,48,768]{2,1,0:T(8,128)(2,1)S(1)}, u32[]{:S(2)}, u32[]{:S(2)}) collective-permute-start(bf16[4,48,768]{2,1,0:T(8,128)(2,1)S(1)} %get-tuple-element.161), channel_id=1, source_target_pairs={{0,4},{2,6},{4,0},{6,2},{8,12},{10,14},{12,8},{14,10},{16,20},{18,... | collective-permute-start | bytes 884744 | tf_op jit(solution)/shard_map/ppermute | solution.py:85
  68.1 19.9 %collective-permute-start.16 = (bf16[4,48,768]{2,1,0:T(8,128)(2,1)S(1)}, bf16[4,48,768]{2,1,0:T(8,128)(2,1)S(1)}, u32[]{:S(2)}, u32[]{:S(2)}) collective-permute-start(bf16[4,48,768]{2,1,0:T(8,128)(2,1)S(1)} %get-tuple-element.162), channel_id=1, source_target_pairs={{0,2},{2,0},{4,6},{6,4},{8,10},{10,8},{12,14},{14,12},{16,18},{18,... | collective-permute-start | bytes 884744 | tf_op jit(solution)/shard_map/ppermute | solution.py:85
  92.8 4.6 %collective-permute-start.17 = (bf16[1536,768]{1,0:T(8,128)(2,1)S(1)}, bf16[1536,768]{1,0:T(8,128)(2,1)S(1)}, u32[]{:S(2)}, u32[]{:S(2)}) collective-permute-start(bf16[1536,768]{1,0:T(8,128)(2,1)S(1)} %outward.1.mine_ref), channel_id=1, source_target_pairs={{0,1},{1,0},{2,3},{3,2},{4,5},{5,4},{6,7},{7,6},{8,9},{9,8},{10,11... | collective-permute-start | bytes 7077896 | tf_op jit(solution)/shard_map/ppermute | solution.py:89
  92.9 15.7 %collective-permute-start.18 = (bf16[8,48,768]{2,1,0:T(8,128)(2,1)S(1)}, bf16[8,48,768]{2,1,0:T(8,128)(2,1)S(1)}, u32[]{:S(2)}, u32[]{:S(2)}) collective-permute-start(bf16[8,48,768]{2,1,0:T(8,128)(2,1)S(1)} %pad_maximum_fusion.4.pair_a), channel_id=1, source_target_pairs={{0,2},{2,0},{4,6},{6,4},{8,10},{10,8},{12,14},{14,12},{16,18},{18,... | collective-permute-start | bytes 1769480 | tf_op jit(solution)/shard_map/ppermute | solution.py:85
  93.5 15.4 %collective-permute-start.19 = (bf16[8,48,768]{2,1,0:T(8,128)(2,1)S(1)}, bf16[8,48,768]{2,1,0:T(8,128)(2,1)S(1)}, u32[]{:S(2)}, u32[]{:S(2)}) collective-permute-start(bf16[8,48,768]{2,1,0:T(8,128)(2,1)S(1)} %pad_maximum_fusion.5.pair_b), channel_id=1, source_target_pairs={{0,4},{2,6},{4,0},{6,2},{8,12},{10,14},{12,8},{14,10},{16,20},{18,... | collective-permute-start | bytes 1769480 | tf_op jit(solution)/shard_map/ppermute | solution.py:85
  119.0 4.9 %collective-permute-start.20 = (bf16[1536,768]{1,0:T(8,128)(2,1)}, bf16[1536,768]{1,0:T(8,128)(2,1)}, u32[]{:S(2)}, u32[]{:S(2)}) collective-permute-start(bf16[1536,768]{1,0:T(8,128)(2,1)} %get-tuple-element.175.mine_ref), channel_id=1, source_target_pairs={{0,1},{1,0},{2,3},{3,2},{4,5},{5,4},{6,7},{7,6},{8,9},{9,8},{10,11... | collective-permute-start | bytes 7077896 | tf_op jit(solution)/shard_map/ppermute | solution.py:89
  125.6 18.3 %copy-start.34 = (bf16[1536,768]{1,0:T(8,128)(2,1)S(1)}, bf16[1536,768]{1,0:T(8,128)(2,1)}, u32[]{:S(2)}) copy-start(bf16[1536,768]{1,0:T(8,128)(2,1)} %get-tuple-element.184.refs_1_) | copy-start | bytes 7077892
  143.7 18.0 %collective-permute-start.21 = (bf16[1536,768]{1,0:T(8,128)(2,1)}, bf16[1536,768]{1,0:T(8,128)(2,1)}, u32[]{:S(2)}, u32[]{:S(2)}) collective-permute-start(bf16[1536,768]{1,0:T(8,128)(2,1)} %get-tuple-element.190.mine_ref), channel_id=1, source_target_pairs={{0,1},{1,0},{2,3},{3,2},{4,5},{5,4},{6,7},{7,6},{8,9},{9,8},{10,11... | collective-permute-start | bytes 7077896 | tf_op jit(solution)/shard_map/ppermute | solution.py:89
  152.0 28.6 %collective-permute-start.22 = (bf16[2,4,48,1536]{3,2,1,0:T(8,128)(2,1)}, bf16[2,4,48,1536]{3,2,1,0:T(8,128)(2,1)}, u32[]{:S(2)}, u32[]{:S(2)}) collective-permute-start(bf16[2,4,48,1536]{3,2,1,0:T(8,128)(2,1)} %get-tuple-element.185), channel_id=1, source_target_pairs={{0,2},{2,0},{4,6},{6,4},{8,10},{10,8},{12,14},{14,12},{16,18},{18,... | collective-permute-start | bytes 3538952 | tf_op jit(solution)/shard_map/ppermute | solution.py:85
  159.8 40.7 %collective-permute-start.23 = (bf16[2,4,48,1536]{3,2,1,0:T(8,128)(2,1)}, bf16[2,4,48,1536]{3,2,1,0:T(8,128)(2,1)}, u32[]{:S(2)}, u32[]{:S(2)}) collective-permute-start(bf16[2,4,48,1536]{3,2,1,0:T(8,128)(2,1)} %get-tuple-element.189), channel_id=1, source_target_pairs={{0,4},{2,6},{4,0},{6,2},{8,12},{10,14},{12,8},{14,10},{16,20},{18,... | collective-permute-start | bytes 3538952 | tf_op jit(solution)/shard_map/ppermute | solution.py:85
  161.7 18.8 %copy-start.8 = (bf16[2,4,48,1536]{3,2,1,0:T(8,128)(2,1)S(1)}, bf16[2,4,48,1536]{3,2,1,0:T(8,128)(2,1)}, u32[]{:S(2)}) copy-start(bf16[2,4,48,1536]{3,2,1,0:T(8,128)(2,1)} %copy-done.7) | copy-start | bytes 3538948
  161.7 21.3 %copy-start.4 = (bf16[1536,256]{1,0:T(8,128)(2,1)S(1)}, bf16[1536,256]{1,0:T(8,128)(2,1)}, u32[]{:S(2)}) copy-start(bf16[1536,256]{1,0:T(8,128)(2,1)} %get-tuple-element.164.refs_1_) | copy-start | bytes 2359300
  161.7 21.3 %copy-start.14 = (bf16[1536,128]{1,0:T(8,128)(2,1)S(1)}, bf16[1536,128]{1,0:T(8,128)(2,1)}, u32[]{:S(2)}) copy-start(bf16[1536,128]{1,0:T(8,128)(2,1)} %get-tuple-element.153.refs_0_) | copy-start | bytes 1179652
  182.5 31.7 %collective-permute-start.27 = (bf16[4,48,1536]{2,1,0:T(8,128)(2,1)}, bf16[4,48,1536]{2,1,0:T(8,128)(2,1)}, u32[]{:S(2)}, u32[]{:S(2)}) collective-permute-start(bf16[4,48,1536]{2,1,0:T(8,128)(2,1)} %add_bitcast_fusion.1), channel_id=1, source_target_pairs={{0,4},{2,6},{4,0},{6,2},{8,12},{10,14},{12,8},{14,10},{16,20},{18,... | collective-permute-start | bytes 1769480 | tf_op jit(solution)/shard_map/ppermute | solution.py:85
  187.1 27.1 %collective-permute-start.25 = (bf16[2,4,48,384]{3,2,1,0:T(8,128)(2,1)}, bf16[2,4,48,384]{3,2,1,0:T(8,128)(2,1)}, u32[]{:S(2)}, u32[]{:S(2)}) collective-permute-start(bf16[2,4,48,384]{3,2,1,0:T(8,128)(2,1)} %get-tuple-element.197), channel_id=1, source_target_pairs={{0,2},{2,0},{4,6},{6,4},{8,10},{10,8},{12,14},{14,12},{16,18},{18,... | collective-permute-start | bytes 884744 | tf_op jit(solution)/shard_map/ppermute | solution.py:85
  199.0 15.2 %collective-permute-start.26 = (bf16[2,4,48,384]{3,2,1,0:T(8,128)(2,1)}, bf16[2,4,48,384]{3,2,1,0:T(8,128)(2,1)}, u32[]{:S(2)}, u32[]{:S(2)}) collective-permute-start(bf16[2,4,48,384]{3,2,1,0:T(8,128)(2,1)} %get-tuple-element.203), channel_id=1, source_target_pairs={{0,4},{2,6},{4,0},{6,2},{8,12},{10,14},{12,8},{14,10},{16,20},{18,... | collective-permute-start | bytes 884744 | tf_op jit(solution)/shard_map/ppermute | solution.py:85
  202.5 35.1 %collective-permute-start.24 = (bf16[4,48,1536]{2,1,0:T(8,128)(2,1)}, bf16[4,48,1536]{2,1,0:T(8,128)(2,1)}, u32[]{:S(2)}, u32[]{:S(2)}) collective-permute-start(bf16[4,48,1536]{2,1,0:T(8,128)(2,1)} %add_bitcast_fusion), channel_id=1, source_target_pairs={{0,2},{2,0},{4,6},{6,4},{8,10},{10,8},{12,14},{14,12},{16,18},{18,... | collective-permute-start | bytes 1769480 | tf_op jit(solution)/shard_map/ppermute | solution.py:85
  217.5 20.1 %collective-permute-start.29 = (bf16[4,48,384]{2,1,0:T(8,128)(2,1)}, bf16[4,48,384]{2,1,0:T(8,128)(2,1)}, u32[]{:S(2)}, u32[]{:S(2)}) collective-permute-start(bf16[4,48,384]{2,1,0:T(8,128)(2,1)} %add_bitcast_fusion.5), channel_id=1, source_target_pairs={{0,4},{2,6},{4,0},{6,2},{8,12},{10,14},{12,8},{14,10},{16,20},{18,... | collective-permute-start | bytes 442376 | tf_op jit(solution)/shard_map/ppermute | solution.py:85
  218.0 19.5 %collective-permute-start.30 = (bf16[4,48,384]{2,1,0:T(8,128)(2,1)}, bf16[4,48,384]{2,1,0:T(8,128)(2,1)}, u32[]{:S(2)}, u32[]{:S(2)}) collective-permute-start(bf16[4,48,384]{2,1,0:T(8,128)(2,1)} %add_bitcast_fusion.4), channel_id=1, source_target_pairs={{0,2},{2,0},{4,6},{6,4},{8,10},{10,8},{12,14},{14,12},{16,18},{18,... | collective-permute-start | bytes 442376 | tf_op jit(solution)/shard_map/ppermute | solution.py:85
  223.8 13.8 %collective-permute-start.28 = (bf16[2,48,1536]{2,1,0:T(8,128)(2,1)}, bf16[2,48,1536]{2,1,0:T(8,128)(2,1)}, u32[]{:S(2)}, u32[]{:S(2)}) collective-permute-start(bf16[2,48,1536]{2,1,0:T(8,128)(2,1)} %get-tuple-element.210), channel_id=1, source_target_pairs={{0,8},{2,10},{4,12},{6,14},{8,0},{10,2},{12,4},{14,6},{16,24},{18,... | collective-permute-start | bytes 884744 | tf_op jit(solution)/shard_map/ppermute | solution.py:85
  243.2 12.8 %collective-permute-start.34 = (bf16[2,4,48,512]{3,2,1,0:T(8,128)(2,1)S(1)}, bf16[2,4,48,512]{3,2,1,0:T(8,128)(2,1)S(1)}, u32[]{:S(2)}, u32[]{:S(2)}) collective-permute-start(bf16[2,4,48,512]{3,2,1,0:T(8,128)(2,1)S(1)} %get-tuple-element.235), channel_id=1, source_target_pairs={{0,4},{2,6},{4,0},{6,2},{8,12},{10,14},{12,8},{14,10},{16,20},{18,... | collective-permute-start | bytes 1179656 | tf_op jit(solution)/shard_map/ppermute | solution.py:85
  244.8 10.0 %collective-permute-start.33 = (bf16[2,4,48,384]{3,2,1,0:T(8,128)(2,1)S(1)}, bf16[2,4,48,384]{3,2,1,0:T(8,128)(2,1)S(1)}, u32[]{:S(2)}, u32[]{:S(2)}) collective-permute-start(bf16[2,4,48,384]{3,2,1,0:T(8,128)(2,1)S(1)} %copy-done.31), channel_id=1, source_target_pairs={{0,2},{2,0},{4,6},{6,4},{8,10},{10,8},{12,14},{14,12},{16,18},{18,... | collective-permute-start | bytes 884744 | tf_op jit(solution)/shard_map/ppermute | solution.py:85
  245.3 10.6 %collective-permute-start.32 = (bf16[2,48,1536]{2,1,0:T(8,128)(2,1)S(1)}, bf16[2,48,1536]{2,1,0:T(8,128)(2,1)S(1)}, u32[]{:S(2)}, u32[]{:S(2)}) collective-permute-start(bf16[2,48,1536]{2,1,0:T(8,128)(2,1)S(1)} %get-tuple-element.222), channel_id=1, source_target_pairs={{0,8},{2,10},{4,12},{6,14},{8,0},{10,2},{12,4},{14,6},{16,24},{18,... | collective-permute-start | bytes 884744 | tf_op jit(solution)/shard_map/ppermute | solution.py:85
  246.4 13.2 %collective-permute-start.37 = (bf16[2,48,768]{2,1,0:T(8,128)(2,1)S(1)}, bf16[2,48,768]{2,1,0:T(8,128)(2,1)S(1)}, u32[]{:S(2)}, u32[]{:S(2)}) collective-permute-start(bf16[2,48,768]{2,1,0:T(8,128)(2,1)S(1)} %get-tuple-element.227), channel_id=1, source_target_pairs={{0,8},{2,10},{4,12},{6,14},{8,0},{10,2},{12,4},{14,6},{16,24},{18,... | collective-permute-start | bytes 442376 | tf_op jit(solution)/shard_map/ppermute | solution.py:85
  248.2 11.9 %collective-permute-start.38 = (bf16[48,1536]{1,0:T(8,128)(2,1)S(1)}, bf16[48,1536]{1,0:T(8,128)(2,1)S(1)}, u32[]{:S(2)}, u32[]{:S(2)}) collective-permute-start(bf16[48,1536]{1,0:T(8,128)(2,1)S(1)} %fusion.4), channel_id=1, source_target_pairs={{0,16},{2,18},{4,20},{6,22},{8,24},{10,26},{12,28},{14,30},{16,0},... | collective-permute-start | bytes 442376 | tf_op jit(solution)/shard_map/ppermute | solution.py:85
  254.8 14.7 %collective-permute-start.31 = (bf16[1536,768]{1,0:T(8,128)(2,1)S(1)}, bf16[1536,768]{1,0:T(8,128)(2,1)S(1)}, u32[]{:S(2)}, u32[]{:S(2)}) collective-permute-start(bf16[1536,768]{1,0:T(8,128)(2,1)S(1)} %source.1.mine_ref), channel_id=1, source_target_pairs={{0,1},{1,0},{2,3},{3,2},{4,5},{5,4},{6,7},{7,6},{8,9},{9,8},{10,11... | collective-permute-start | bytes 7077896 | tf_op jit(solution)/shard_map/ppermute | solution.py:89
  256.0 23.1 %collective-permute-start.42 = (bf16[48,1536]{1,0:T(8,128)(2,1)S(1)}, bf16[48,1536]{1,0:T(8,128)(2,1)S(1)}, u32[]{:S(2)}, u32[]{:S(2)}) collective-permute-start(bf16[48,1536]{1,0:T(8,128)(2,1)S(1)} %fusion.5), channel_id=1, source_target_pairs={{0,16},{2,18},{4,20},{6,22},{8,24},{10,26},{12,28},{14,30},{16,0},... | collective-permute-start | bytes 442376 | tf_op jit(solution)/shard_map/ppermute | solution.py:85
  258.0 11.2 %collective-permute-start.36 = (bf16[4,48,512]{2,1,0:T(8,128)(2,1)S(1)}, bf16[4,48,512]{2,1,0:T(8,128)(2,1)S(1)}, u32[]{:S(2)}, u32[]{:S(2)}) collective-permute-start(bf16[4,48,512]{2,1,0:T(8,128)(2,1)S(1)} %add_bitcast_fusion.2), channel_id=1, source_target_pairs={{0,2},{2,0},{4,6},{6,4},{8,10},{10,8},{12,14},{14,12},{16,18},{18,... | collective-permute-start | bytes 589832 | tf_op jit(solution)/shard_map/ppermute | solution.py:85
  259.5 9.7 %collective-permute-start.35 = (bf16[4,48,384]{2,1,0:T(8,128)(2,1)S(1)}, bf16[4,48,384]{2,1,0:T(8,128)(2,1)S(1)}, u32[]{:S(2)}, u32[]{:S(2)}) collective-permute-start(bf16[4,48,384]{2,1,0:T(8,128)(2,1)S(1)} %add_bitcast_fusion.3), channel_id=1, source_target_pairs={{0,4},{2,6},{4,0},{6,2},{8,12},{10,14},{12,8},{14,10},{16,20},{18,... | collective-permute-start | bytes 442376 | tf_op jit(solution)/shard_map/ppermute | solution.py:85
  260.1 8.4 %collective-permute-start.39 = (bf16[48,768]{1,0:T(8,128)(2,1)S(1)}, bf16[48,768]{1,0:T(8,128)(2,1)S(1)}, u32[]{:S(2)}, u32[]{:S(2)}) collective-permute-start(bf16[48,768]{1,0:T(8,128)(2,1)S(1)} %fusion.9), channel_id=1, source_target_pairs={{0,16},{2,18},{4,20},{6,22},{8,24},{10,26},{12,28},{14,30},{16,0},... | collective-permute-start | bytes 221192 | tf_op jit(solution)/shard_map/ppermute | solution.py:85
  269.3 6.5 %collective-permute-start.40 = (bf16[2,48,896]{2,1,0:T(8,128)(2,1)S(1)}, bf16[2,48,896]{2,1,0:T(8,128)(2,1)S(1)}, u32[]{:S(2)}, u32[]{:S(2)}) collective-permute-start(bf16[2,48,896]{2,1,0:T(8,128)(2,1)S(1)} %get-tuple-element.251), channel_id=1, source_target_pairs={{0,8},{2,10},{4,12},{6,14},{8,0},{10,2},{12,4},{14,6},{16,24},{18,... | collective-permute-start | bytes 516104 | tf_op jit(solution)/shard_map/ppermute | solution.py:85
  275.8 7.5 %collective-permute-start.41 = (bf16[48,896]{1,0:T(8,128)(2,1)S(1)}, bf16[48,896]{1,0:T(8,128)(2,1)S(1)}, u32[]{:S(2)}, u32[]{:S(2)}) collective-permute-start(bf16[48,896]{1,0:T(8,128)(2,1)S(1)} %fusion.7), channel_id=1, source_target_pairs={{0,16},{2,18},{4,20},{6,22},{8,24},{10,26},{12,28},{14,30},{16,0},... | collective-permute-start | bytes 258056 | tf_op jit(solution)/shard_map/ppermute | solution.py:85
  (55 other events, 416.3 us)
where the time goes:
time: 288 us; the launch traced here: 287 us
  Pallas kernels  135 us (47%)
  waiting for transfers between devices  53.9 us (19%)
  starting transfers between devices  46.1 us (16%)
  other arithmetic  26.2 us (9%)
  local copies, waits for them, and re-layouts  23.4 us (8%)
    ppermute x39, waiting for transfers between devices, hop(): return lax.ppermute(value, 'dp', [(d, d ^ offset) for d in range(size)])  46 us
    ppermute x39, starting transfers between devices, hop(): return lax.ppermute(value, 'dp', [(d, d ^ offset) for d in range(size)])  45.7 us
    pallas_call x2, Pallas kernels, attend(): pl.pallas_call(attend_kernel, out_shape=(main((rows, groups * width), low...  22.6 us
    pallas_call x3, Pallas kernels, attend_back(): pl.pallas_call(attend_back_kernel, out_shape=(main((rows, width), low), s...  20.1 us
    pallas_call x6, Pallas kernels, weight_grad(): pl.pallas_call(partial(weight_grad_kernel, bit, len(rights), turned, extr...  18.7 us
    pallas_call x1, Pallas kernels, contract(): pl.pallas_call(contract_kernel, out_shape=(shape((rows, D), low), shape((...  18.1 us
    unnamed x120, local copies, waits for them, and re-layouts  12.2 us
    pallas_call x1, Pallas kernels, first_back(): pl.pallas_call(first_back_kernel, out_shape=(shape((3, D), full), main((r...  10.9 us
  transfers between devices with their start and end apart: 43, of which 15 were waited for; matrix products, arithmetic and copies ran while one was open for 10% of the time, Pallas kernels for 34%

commit v1 on v0

--- a/solution.py
+++ b/solution.py
@@ -13,9 +13,9 @@
 FF = 3072
 LEN = 512
 LANES = 128
-ROWS = 256
+ROWS = 384
 COST_SHARE = 1
-ATTEND, BACK, EXPAND, CONTRACT, GRADS = 12, 12, 16, 24, 20
+ATTEND, BACK, EXPAND, CONTRACT, GRADS = 12, 20, 28, 40, 20
 
 norm_epsilon = 1e-12
 low = jnp.bfloat16
@@ -889,10 +889,7 @@
         got_up = hop(sent_up, 2, size)
         first_sums, first_grad, first_low, context_grad = back_first(sent_up)
 
-        got_down = after(got_down, first_low)
-        next_down = kept_down[1] + got_down[1]
-        more_down = hop(next_down, 2, size)
-        sent_out, kept_out = weight_grad(after(first_low, next_down), contexts, me, size, 0)
+        sent_out, kept_out = weight_grad(first_low, contexts, me, size, 0)
         got_out = hop(sent_out, 1, size)
 
         def attention(group, *gates):
@@ -901,7 +898,11 @@
             head_sums.append(sums)
 
         attention(0, sent_out)
-        sent_0, kept_0 = weight_grad(turned, [stacked[0]], me, size, 1, True)
+        got_down = after(got_down, stacked[0])
+        next_down = kept_down[1] + got_down[1]
+        more_down = hop(next_down, 2, size)
+        gated = after(turned, next_down)
+        sent_0, kept_0 = weight_grad(gated, [stacked[0]], me, size, 1, True)
         got_0 = hop(sent_0, 2, size)
         got_up = after(got_up, sent_0)
         next_up = kept_up[1] + got_up[1]

time: 288 us -> 277 us (0.962)
  waiting for transfers between devices: 53.9 us -> 47.8 us
  Pallas kernels: 135 us -> 130 us
    ppermute x39, waiting for transfers between devices: 46 us -> 39.9 us  [hop(): return lax.ppermute(value, 'dp', [(d, d ^ offset) for d in range(size)])]
  transfers between devices with their start and end apart: 43 -> 43, of which waited for: 15 -> 16; matrix products, arithmetic and copies ran while one was open for 10% -> 11% of each run, Pallas kernels for 34% -> 34%
where the time goes in v1:
time: 277 us; the launch traced here: 276 us
  Pallas kernels  130 us (47%)
  waiting for transfers between devices  47.8 us (17%)
  starting transfers between devices  44.5 us (16%)
  other arithmetic  26.2 us (9%)
  local copies, waits for them, and re-layouts  24.9 us (9%)
    ppermute x39, starting transfers between devices, hop(): return lax.ppermute(value, 'dp', [(d, d ^ offset) for d in range(size)])  44.1 us
    ppermute x39, waiting for transfers between devices, hop(): return lax.ppermute(value, 'dp', [(d, d ^ offset) for d in range(size)])  39.9 us
    pallas_call x2, Pallas kernels, attend(): pl.pallas_call(attend_kernel, out_shape=(main((rows, groups * width), low...  22.6 us
    pallas_call x3, Pallas kernels, attend_back(): pl.pallas_call(attend_back_kernel, out_shape=(main((rows, width), low), s...  20.4 us
    pallas_call x6, Pallas kernels, weight_grad(): pl.pallas_call(partial(weight_grad_kernel, bit, len(rights), turned, extr...  18.7 us
    pallas_call x1, Pallas kernels, contract(): pl.pallas_call(contract_kernel, out_shape=(shape((rows, D), low), shape((...  17.9 us
    unnamed x120, local copies, waits for them, and re-layouts  13.7 us
    pallas_call x1, Pallas kernels, expand_first(): pl.pallas_call(expand_first_kernel, out_shape=(main((rows, D), full), mai...  10 us
  transfers between devices with their start and end apart: 43, of which 16 were waited for; matrix products, arithmetic and copies ran while one was open for 11% of the time, Pallas kernels for 34%

profile of v1, /device:TPU:0, one launch (start us, length us, event | category | flops | bytes accessed | tf_op | source)
XLA Modules:
  0.0 275.6 jit_solution(3332439830227423391)
XLA Ops:
  4.5 3.1 %collective-permute-start = (bf16[48,1280]{1,0:T(8,128)(2,1)S(1)}, bf16[48,1280]{1,0:T(8,128)(2,1)S(1)}, u32[]{:S(2)}, u32[]{:S(2)}) collective-permute-start(bf16[48,1280]{1,0:T(8,128)(2,1)S(1)} %fusion.6), channel_id=1, source_target_pairs={{0,8},{2,10},{4,12},{6,14},{8,0},{10,2},{12,4},{14,6},{16,24},{18,... | collective-permute-start | bytes 368648 | tf_op jit(solution)/shard_map/ppermute | solution.py:85
  7.6 2.6 collective-permute-start.1
  15.6 4.3 %collective-permute-done.1 = bf16[48,1280]{1,0:T(8,128)(2,1)S(1)} collective-permute-done((bf16[48,1280]{1,0:T(8,128)(2,1)S(1)}, bf16[48,1280]{1,0:T(8,128)(2,1)S(1)}, u32[]{:S(2)}, u32[]{:S(2)}) %collective-permute-start.1) | collective-permute-done | bytes 122912 | tf_op jit(solution)/shard_map/ppermute | solution.py:85
  19.9 3.1 %collective-permute-start.7 = (bf16[48,1920]{1,0:T(8,128)(2,1)S(1)}, bf16[48,1920]{1,0:T(8,128)(2,1)S(1)}, u32[]{:S(2)}, u32[]{:S(2)}) collective-permute-start(bf16[48,1920]{1,0:T(8,128)(2,1)S(1)} %pad_maximum_fusion.13), channel_id=1, source_target_pairs={{0,16},{2,18},{4,20},{6,22},{8,24},{10,26},{12,28},{14,30},{16,0},... | collective-permute-start | bytes 552968 | tf_op jit(solution)/shard_map/ppermute | solution.py:85
  23.1 1.6 collective-permute-start.4
  26.2 4.3 %collective-permute-done.7 = bf16[48,1920]{1,0:T(8,128)(2,1)S(1)} collective-permute-done((bf16[48,1920]{1,0:T(8,128)(2,1)S(1)}, bf16[48,1920]{1,0:T(8,128)(2,1)S(1)}, u32[]{:S(2)}, u32[]{:S(2)}) %collective-permute-start.7) | collective-permute-done | bytes 184352 | tf_op jit(solution)/shard_map/ppermute | solution.py:85
  33.9 6.6 %collective-permute-done.8 = bf16[2,48,1920]{2,1,0:T(8,128)(2,1)S(1)} collective-permute-done((bf16[2,48,1920]{2,1,0:T(8,128)(2,1)S(1)}, bf16[2,48,1920]{2,1,0:T(8,128)(2,1)S(1)}, u32[]{:S(2)}, u32[]{:S(2)}) %collective-permute-start.8) | collective-permute-done | bytes 368672 | tf_op jit(solution)/shard_map/ppermute | solution.py:85
  40.8 8.1 %collective-permute-done.11 = bf16[48,1536]{1,0:T(8,128)(2,1)S(1)} collective-permute-done((bf16[48,1536]{1,0:T(8,128)(2,1)S(1)}, bf16[48,1536]{1,0:T(8,128)(2,1)S(1)}, u32[]{:S(2)}, u32[]{:S(2)}) %collective-permute-start.11) | collective-permute-done | bytes 147488 | tf_op jit(solution)/shard_map/ppermute | solution.py:85
  49.8 1.6 collective-permute-start.9
  53.4 8.2 %attend.2 = (bf16[1536,384]{1,0:T(8,128)(2,1)}, bf16[3,2,512,512]{3,2,1,0:T(8,128)(2,1)}, bf16[1536,128]{1,0:T(8,128)(2,1)}) custom-call(s32[3]{0:T(128)S(1)} %copy-done.26, bf16[1536,768]{1,0:T(8,128)(2,1)} %x_ref.4, bf16[768,1280]{1,0:T(8,128)(2,1)S(1)} %place.3.w_ref.refs_3_, f32[2,384]{1,0:T(2,128)S(1)} %reshape.207.bias_ref), custom_call_target="tpu_custom_call" | custom-call | flops 1711276032 | bytes 3145728 | tf_op jit(solution)/shard_map/attend/pallas_call | solution.py:259
  69.6 14.4 %attend.3 = (bf16[1536,768]{1,0:T(8,128)(2,1)}, bf16[6,2,512,512]{3,2,1,0:T(8,128)(2,1)}, bf16[1536,256]{1,0:T(8,128)(2,1)}) custom-call(s32[3]{0:T(128)S(1)} %copy-done.26, bf16[1536,768]{1,0:T(8,128)(2,1)} %x_ref.4, bf16[768,1280]{1,0:T(8,128)(2,1)S(1)} %place.3.w_ref.refs_3_, f32[2,384]{1,0:T(2,128)S(1)} %reshape.207.bias_ref), custom_call_target="tpu_custom_call" | custom-call | flops 3422552064 | bytes 6291456 | tf_op jit(solution)/shard_map/attend/pallas_call | solution.py:259
  83.9 2.2 collective-permute-done.15
  86.1 1.9 collective-permute-done.16
  88.3 3.5 %outward.1.mine_ref = bf16[1536,768]{1,0:T(8,128)(2,1)S(1)} custom-call(bf16[1536,128]{1,0:T(8,128)(2,1)} %get-tuple-element.153.refs_0_, bf16[1536,256]{1,0:T(8,128)(2,1)} %get-tuple-element.164.refs_1_, bf16[768,1920]{1,0:T(8,128)(2,1)S(1)} %place.4.refs_2_.up_ref.down_ref.up_first.down_first.w_ref), custom_call_target="tpu_custom_call" | custom-call | flops 905969664 | bytes 4128768 | tf_op jit(solution)/shard_map/outward/pallas_call | solution.py:368
  93.1 3.4 %collective-permute-done.17.other_ref = bf16[1536,768]{1,0:T(8,128)(2,1)S(1)} collective-permute-done((bf16[1536,768]{1,0:T(8,128)(2,1)S(1)}, bf16[1536,768]{1,0:T(8,128)(2,1)S(1)}, u32[]{:S(2)}, u32[]{:S(2)}) %collective-permute-start.17) | collective-permute-done | bytes 2359328 | tf_op jit(solution)/shard_map/ppermute | solution.py:89
  96.5 10.0 %expand_first.1 = (f32[1536,768]{1,0:T(8,128)}, bf16[1536,768]{1,0:T(8,128)(2,1)}, bf16[1536,768]{1,0:T(8,128)(2,1)}, bf16[1536,768]{1,0:T(8,128)(2,1)}, f32[1536,768]{1,0:T(8,128)}, /*index=5*/f32[1536,1]{1,0:T(8,128)}) custom-call(bf16[1536,768]{1,0:T(8,128)(2,1)S(1)} %outward.1.mine_ref, bf16[1536,768]{1,0:T(8,128)(2,1)S(1)} %collective-permute-done.17.other_ref, ...), custom_call_target="tpu_custom_call" | custom-call | flops 3623878656 | bytes 21233664 | tf_op jit(solution)/shard_map/expand_first/pallas_call | solution.py:411
  108.1 9.1 %expand_last.1 = (bf16[1536,768]{1,0:T(8,128)(2,1)}, bf16[1536,768]{1,0:T(8,128)(2,1)}, bf16[1536,768]{1,0:T(8,128)(2,1)}) custom-call(f32[1536,768]{1,0:T(8,128)} %get-tuple-element.171.total_ref, bf16[1536,768]{1,0:T(8,128)(2,1)} %get-tuple-element.186.middle_ref.left_ref, f32[1,1536]{1,0:T(1,128)S(1)} %reshape.210.bias_ref, ...), custom_call_target="tpu_custom_call" | custom-call | flops 3623878656 | bytes 14155776 | tf_op jit(solution)/shard_map/expand_last/pallas_call | solution.py:453
  117.7 4.5 %collective-permute-done.20.other_ref = bf16[1536,768]{1,0:T(8,128)(2,1)} collective-permute-done((bf16[1536,768]{1,0:T(8,128)(2,1)}, bf16[1536,768]{1,0:T(8,128)(2,1)}, u32[]{:S(2)}, u32[]{:S(2)}) %collective-permute-start.20) | collective-permute-done | bytes 2359328 | tf_op jit(solution)/shard_map/ppermute | solution.py:89
  122.2 1.7 copy-done.3
  123.8 17.9 %contract.1 = (bf16[1536,768]{1,0:T(8,128)(2,1)}, f32[3,768]{1,0:T(4,128)S(1)}, f32[1,1536]{1,0:T(1,128)S(1)}, bf16[1536,768]{1,0:T(8,128)(2,1)}, f32[1536,768]{...) custom-call(bf16[1536,768]{1,0:T(8,128)(2,1)} %get-tuple-element.175.mine_ref, ...), custom_call_target="tpu_custom_call" | custom-call | flops 7247757312 | bytes 14155776 | tf_op jit(solution)/shard_map/contract/pallas_call | solution.py:513
  141.9 1.7 copy-done.29
  143.6 1.7 copy-done.34
  145.3 5.3 %weight_grad.6 = (bf16[2,4,48,1536]{3,2,1,0:T(8,128)(2,1)}, bf16[2,4,48,1536]{3,2,1,0:T(8,128)(2,1)S(1)}) custom-call(s32[1]{0:T(128)} %bitcast.me_ref, bf16[1536,768]{1,0:T(8,128)(2,1)S(1)} %copy-done.29, bf16[1536,768]{1,0:T(8,128)(2,1)S(1)} %copy-done.33, bf16[1536,768]{1,0:T(8,128)(2,1)S(1)} %copy-done.34), custom_call_target="tpu_custom_call" | custom-call | flops 3623878656 | bytes 7077888 | tf_op jit(solution)/shard_map/weight_grad/pallas_call | solution.py:720
  153.1 5.3 %weight_grad.7 = (bf16[2,4,48,1536]{3,2,1,0:T(8,128)(2,1)}, bf16[2,4,48,1536]{3,2,1,0:T(8,128)(2,1)S(1)}) custom-call(s32[1]{0:T(128)} %bitcast.me_ref, bf16[1536,768]{1,0:T(8,128)(2,1)S(1)} %copy-done.32, bf16[1536,768]{1,0:T(8,128)(2,1)S(1)} %copy-done.27, bf16[1536,768]{1,0:T(8,128)(2,1)S(1)} %copy-done.28), custom_call_target="tpu_custom_call" | custom-call | flops 3623878656 | bytes 7077888 | tf_op jit(solution)/shard_map/weight_grad/pallas_call | solution.py:720
  161.3 10.0 %first_back.1 = (f32[3,768]{1,0:T(4,128)S(1)}, f32[1536,768]{1,0:T(8,128)}, bf16[1536,768]{1,0:T(8,128)(2,1)}, bf16[1536,384]{1,0:T(8,128)(2,1)}) custom-call(bf16[1536,768]{1,0:T(8,128)(2,1)} %get-tuple-element.190.mine_ref, bf16[1536,768]{1,0:T(8,128)(2,1)} %collective-permute-done.21.other_ref, f32[1536,768]{1,0:T(8,128)} %get-tuple-element.191.second_ref, ...), custom_call_target="tpu_custom_call" | custom-call | flops 905969664 | bytes 23592960 | tf_op jit(solution)/shard_map/first_back/pallas_call | solution.py:579
  171.4 1.7 copy-done.13
  173.0 2.4 weight_grad.8
  175.5 7.0 %attend_back.3 = (bf16[1536,384]{1,0:T(8,128)(2,1)}, f32[2,128]{1,0:T(2,128)S(1)}) custom-call(bf16[1536,384]{1,0:T(8,128)(2,1)} %get-tuple-element.195.qkv_ref, bf16[3,2,512,512]{3,2,1,0:T(8,128)(2,1)} %get-tuple-element.196.weight_ref, bf16[1536,384]{1,0:T(8,128)(2,1)} %get-tuple-element.197.grad_ref), custom_call_target="tpu_custom_call" | custom-call | flops 1610612736 | bytes 5505024 | tf_op jit(solution)/shard_map/attend_back/pallas_call | solution.py:330
  182.5 2.0 add_bitcast_fusion.1
  187.8 2.3 weight_grad.9
  190.7 2.0 add_bitcast_fusion
  194.1 6.6 %attend_back.4 = (bf16[1536,384]{1,0:T(8,128)(2,1)}, f32[2,128]{1,0:T(2,128)S(1)}) custom-call(bf16[1536,768]{1,0:T(8,128)(2,1)} %get-tuple-element.219.qkv_ref, bf16[6,2,512,512]{3,2,1,0:T(8,128)(2,1)} %get-tuple-element.207.weight_ref, bf16[1536,384]{1,0:T(8,128)(2,1)} %get-tuple-element.197.grad_ref), custom_call_target="tpu_custom_call" | custom-call | flops 1610612736 | bytes 5505024 | tf_op jit(solution)/shard_map/attend_back/pallas_call | solution.py:330
  206.7 1.7 add_bitcast_fusion.4
  208.3 1.7 add_bitcast_fusion.5
  212.9 2.2 combine.4
  215.8 1.7 collective-permute-start.28
  217.6 1.6 weight_grad.10
  219.3 6.8 %attend_back.5 = (bf16[1536,384]{1,0:T(8,128)(2,1)}, f32[2,128]{1,0:T(2,128)S(1)}) custom-call(bf16[1536,768]{1,0:T(8,128)(2,1)} %get-tuple-element.219.qkv_ref, bf16[6,2,512,512]{3,2,1,0:T(8,128)(2,1)} %get-tuple-element.207.weight_ref, bf16[1536,384]{1,0:T(8,128)(2,1)} %get-tuple-element.197.grad_ref), custom_call_target="tpu_custom_call" | custom-call | flops 1610612736 | bytes 5505024 | tf_op jit(solution)/shard_map/attend_back/pallas_call | solution.py:330
  229.7 1.5 combine.5
  233.6 1.7 weight_grad.11
  238.9 1.8 collective-permute-start.37
  240.7 5.6 %source.1.mine_ref = bf16[1536,768]{1,0:T(8,128)(2,1)S(1)} custom-call(bf16[1536,384]{1,0:T(8,128)(2,1)} %get-tuple-element.236.refs_0_, bf16[1536,384]{1,0:T(8,128)(2,1)} %get-tuple-element.208.refs_0_.refs_1_, bf16[1536,384]{1,0:T(8,128)(2,1)} %get-tuple-element.220.refs_0_.refs_2_, bf16[768,1280]{1,0:T(8,128)(2,1)S(1)} %copy-done.11), custom_call_target="tpu_custom_call" | custom-call | flops 2717908992 | bytes 5308416 | tf_op jit(solution)/shard_map/source/pallas_call | solution.py:614
  246.4 3.1 %collective-permute-done.32 = bf16[2,48,1536]{2,1,0:T(8,128)(2,1)S(1)} collective-permute-done((bf16[2,48,1536]{2,1,0:T(8,128)(2,1)S(1)}, bf16[2,48,1536]{2,1,0:T(8,128)(2,1)S(1)}, u32[]{:S(2)}, u32[]{:S(2)}) %collective-permute-start.32) | collective-permute-done | bytes 294944 | tf_op jit(solution)/shard_map/ppermute | solution.py:85
  251.7 2.2 collective-permute-start.39
  253.9 2.0 multiply_subtract_fusion
  255.9 4.1 %collective-permute-done.39 = bf16[48,768]{1,0:T(8,128)(2,1)S(1)} collective-permute-done((bf16[48,768]{1,0:T(8,128)(2,1)S(1)}, bf16[48,768]{1,0:T(8,128)(2,1)S(1)}, u32[]{:S(2)}, u32[]{:S(2)}) %collective-permute-start.39) | collective-permute-done | bytes 73760 | tf_op jit(solution)/shard_map/ppermute | solution.py:85
  261.0 5.2 %finish.1 = f32[1536,768]{1,0:T(8,128)} custom-call(bf16[1536,768]{1,0:T(8,128)(2,1)S(1)} %source.1.mine_ref, bf16[1536,768]{1,0:T(8,128)(2,1)S(1)} %collective-permute-done.31.other_ref, f32[1536,768]{1,0:T(8,128)} %get-tuple-element.253.first_ref), custom_call_target="tpu_custom_call" | custom-call | flops 2359296 | bytes 14155776 | tf_op jit(solution)/shard_map/finish/pallas_call | solution.py:632
  266.4 3.3 %collective-permute-start.41 = (bf16[48,896]{1,0:T(8,128)(2,1)S(1)}, bf16[48,896]{1,0:T(8,128)(2,1)S(1)}, u32[]{:S(2)}, u32[]{:S(2)}) collective-permute-start(bf16[48,896]{1,0:T(8,128)(2,1)S(1)} %fusion.7), channel_id=1, source_target_pairs={{0,16},{2,18},{4,20},{6,22},{8,24},{10,26},{12,28},{14,30},{16,0},... | collective-permute-start | bytes 258056 | tf_op jit(solution)/shard_map/ppermute | solution.py:85
  (283 shorter events, 67.0 us)
Async XLA Ops:
  4.5 11.1 %collective-permute-start = (bf16[48,1280]{1,0:T(8,128)(2,1)S(1)}, bf16[48,1280]{1,0:T(8,128)(2,1)S(1)}, u32[]{:S(2)}, u32[]{:S(2)}) collective-permute-start(bf16[48,1280]{1,0:T(8,128)(2,1)S(1)} %fusion.6), channel_id=1, source_target_pairs={{0,8},{2,10},{4,12},{6,14},{8,0},{10,2},{12,4},{14,6},{16,24},{18,... | collective-permute-start | bytes 368648 | tf_op jit(solution)/shard_map/ppermute | solution.py:85
  7.6 12.3 %collective-permute-start.1 = (bf16[48,1280]{1,0:T(8,128)(2,1)S(1)}, bf16[48,1280]{1,0:T(8,128)(2,1)S(1)}, u32[]{:S(2)}, u32[]{:S(2)}) collective-permute-start(bf16[48,1280]{1,0:T(8,128)(2,1)S(1)} %fusion.6), channel_id=1, source_target_pairs={{0,16},{2,18},{4,20},{6,22},{8,24},{10,26},{12,28},{14,30},{16,0},... | collective-permute-start | bytes 368648 | tf_op jit(solution)/shard_map/ppermute | solution.py:85
  10.2 9.7 %collective-permute-start.2 = (bf16[48,1280]{1,0:T(8,128)(2,1)S(1)}, bf16[48,1280]{1,0:T(8,128)(2,1)S(1)}, u32[]{:S(2)}, u32[]{:S(2)}) collective-permute-start(bf16[48,1280]{1,0:T(8,128)(2,1)S(1)} %fusion.6), channel_id=1, source_target_pairs={{0,24},{2,26},{4,28},{6,30},{8,16},{10,18},{12,20},{14,22},{16,8},... | collective-permute-start | bytes 368648 | tf_op jit(solution)/shard_map/ppermute | solution.py:85
  19.9 10.6 %collective-permute-start.7 = (bf16[48,1920]{1,0:T(8,128)(2,1)S(1)}, bf16[48,1920]{1,0:T(8,128)(2,1)S(1)}, u32[]{:S(2)}, u32[]{:S(2)}) collective-permute-start(bf16[48,1920]{1,0:T(8,128)(2,1)S(1)} %pad_maximum_fusion.13), channel_id=1, source_target_pairs={{0,16},{2,18},{4,20},{6,22},{8,24},{10,26},{12,28},{14,30},{16,0},... | collective-permute-start | bytes 552968 | tf_op jit(solution)/shard_map/ppermute | solution.py:85
  23.1 7.5 %collective-permute-start.4 = (bf16[4,48,640]{2,1,0:T(8,128)(2,1)S(1)}, bf16[4,48,640]{2,1,0:T(8,128)(2,1)S(1)}, u32[]{:S(2)}, u32[]{:S(2)}) collective-permute-start(bf16[4,48,640]{2,1,0:T(8,128)(2,1)S(1)} %get-tuple-element.142), channel_id=1, source_target_pairs={{0,2},{2,0},{4,6},{6,4},{8,10},{10,8},{12,14},{14,12},{16,18},{18,... | collective-permute-start | bytes 737288 | tf_op jit(solution)/shard_map/ppermute | solution.py:85
  24.7 6.2 %collective-permute-start.3 = (bf16[4,48,640]{2,1,0:T(8,128)(2,1)S(1)}, bf16[4,48,640]{2,1,0:T(8,128)(2,1)S(1)}, u32[]{:S(2)}, u32[]{:S(2)}) collective-permute-start(bf16[4,48,640]{2,1,0:T(8,128)(2,1)S(1)} %get-tuple-element.141), channel_id=1, source_target_pairs={{0,4},{2,6},{4,0},{6,2},{8,12},{10,14},{12,8},{14,10},{16,20},{18,... | collective-permute-start | bytes 737288 | tf_op jit(solution)/shard_map/ppermute | solution.py:85
  30.6 10.0 %collective-permute-start.8 = (bf16[2,48,1920]{2,1,0:T(8,128)(2,1)S(1)}, bf16[2,48,1920]{2,1,0:T(8,128)(2,1)S(1)}, u32[]{:S(2)}, u32[]{:S(2)}) collective-permute-start(bf16[2,48,1920]{2,1,0:T(8,128)(2,1)S(1)} %pad_maximum_fusion.9), channel_id=1, source_target_pairs={{0,8},{2,10},{4,12},{6,14},{8,0},{10,2},{12,4},{14,6},{16,24},{18,... | collective-permute-start | bytes 1105928 | tf_op jit(solution)/shard_map/ppermute | solution.py:85
  30.9 18.7 %collective-permute-start.5 = (bf16[8,48,640]{2,1,0:T(8,128)(2,1)S(1)}, bf16[8,48,640]{2,1,0:T(8,128)(2,1)S(1)}, u32[]{:S(2)}, u32[]{:S(2)}) collective-permute-start(bf16[8,48,640]{2,1,0:T(8,128)(2,1)S(1)} %pad_maximum_fusion.7.pair_a), channel_id=1, source_target_pairs={{0,2},{2,0},{4,6},{6,4},{8,10},{10,8},{12,14},{14,12},{16,18},{18,... | collective-permute-start | bytes 1474568 | tf_op jit(solution)/shard_map/ppermute | solution.py:85
  32.4 17.3 %collective-permute-start.6 = (bf16[8,48,640]{2,1,0:T(8,128)(2,1)S(1)}, bf16[8,48,640]{2,1,0:T(8,128)(2,1)S(1)}, u32[]{:S(2)}, u32[]{:S(2)}) collective-permute-start(bf16[8,48,640]{2,1,0:T(8,128)(2,1)S(1)} %pad_maximum_fusion.8.pair_b), channel_id=1, source_target_pairs={{0,4},{2,6},{4,0},{6,2},{8,12},{10,14},{12,8},{14,10},{16,20},{18,... | collective-permute-start | bytes 1474568 | tf_op jit(solution)/shard_map/ppermute | solution.py:85
  40.5 8.4 %collective-permute-start.11 = (bf16[48,1536]{1,0:T(8,128)(2,1)S(1)}, bf16[48,1536]{1,0:T(8,128)(2,1)S(1)}, u32[]{:S(2)}, u32[]{:S(2)}) collective-permute-start(bf16[48,1536]{1,0:T(8,128)(2,1)S(1)} %pad_maximum_fusion.14), channel_id=1, source_target_pairs={{0,16},{2,18},{4,20},{6,22},{8,24},{10,26},{12,28},{14,30},{16,0},... | collective-permute-start | bytes 442376 | tf_op jit(solution)/shard_map/ppermute | solution.py:85
  49.6 15.0 %collective-permute-start.12 = (bf16[2,48,1536]{2,1,0:T(8,128)(2,1)}, bf16[2,48,1536]{2,1,0:T(8,128)(2,1)}, u32[]{:S(2)}, u32[]{:S(2)}) collective-permute-start(bf16[2,48,1536]{2,1,0:T(8,128)(2,1)} %pad_maximum_fusion.11), channel_id=1, source_target_pairs={{0,8},{2,10},{4,12},{6,14},{8,0},{10,2},{12,4},{14,6},{16,24},{18,... | collective-permute-start | bytes 884744 | tf_op jit(solution)/shard_map/ppermute | solution.py:85
  49.8 19.7 %copy-start.10 = (bf16[768,1280]{1,0:T(8,128)(2,1)}, bf16[768,1280]{1,0:T(8,128)(2,1)S(1)}, u32[]{:S(2)}) copy-start(bf16[768,1280]{1,0:T(8,128)(2,1)S(1)} %place.3.w_ref.refs_3_) | copy-start | bytes 5898244
  49.8 12.3 %collective-permute-start.9 = (bf16[4,48,1024]{2,1,0:T(8,128)(2,1)S(1)}, bf16[4,48,1024]{2,1,0:T(8,128)(2,1)S(1)}, u32[]{:S(2)}, u32[]{:S(2)}) collective-permute-start(bf16[4,48,1024]{2,1,0:T(8,128)(2,1)S(1)} %slice.273), channel_id=1, source_target_pairs={{0,4},{2,6},{4,0},{6,2},{8,12},{10,14},{12,8},{14,10},{16,20},{18,... | collective-permute-start | bytes 1179656 | tf_op jit(solution)/shard_map/ppermute | solution.py:85
  51.4 10.7 %collective-permute-start.10 = (bf16[4,48,896]{2,1,0:T(8,128)(2,1)S(1)}, bf16[4,48,896]{2,1,0:T(8,128)(2,1)}, u32[]{:S(2)}, u32[]{:S(2)}) collective-permute-start(bf16[4,48,896]{2,1,0:T(8,128)(2,1)S(1)} %pad_maximum_fusion.10), channel_id=1, source_target_pairs={{0,2},{2,0},{4,6},{6,4},{8,10},{10,8},{12,14},{14,12},{16,18},{18,... | collective-permute-start | bytes 1032200 | tf_op jit(solution)/shard_map/ppermute | solution.py:85
  63.2 24.8 %collective-permute-start.13 = (bf16[8,48,1024]{2,1,0:T(8,128)(2,1)S(1)}, bf16[8,48,1024]{2,1,0:T(8,128)(2,1)S(1)}, u32[]{:S(2)}, u32[]{:S(2)}) collective-permute-start(bf16[8,48,1024]{2,1,0:T(8,128)(2,1)S(1)} %pad_maximum_fusion.pair_a), channel_id=1, source_target_pairs={{0,2},{2,0},{4,6},{6,4},{8,10},{10,8},{12,14},{14,12},{16,18},{18,... | collective-permute-start | bytes 2359304 | tf_op jit(solution)/shard_map/ppermute | solution.py:85
  63.8 24.2 %collective-permute-start.14 = (bf16[8,48,896]{2,1,0:T(8,128)(2,1)S(1)}, bf16[8,48,896]{2,1,0:T(8,128)(2,1)S(1)}, u32[]{:S(2)}, u32[]{:S(2)}) collective-permute-start(bf16[8,48,896]{2,1,0:T(8,128)(2,1)S(1)} %pad_maximum_fusion.2.pair_b), channel_id=1, source_target_pairs={{0,4},{2,6},{4,0},{6,2},{8,12},{10,14},{12,8},{14,10},{16,20},{18,... | collective-permute-start | bytes 2064392 | tf_op jit(solution)/shard_map/ppermute | solution.py:85
  66.7 19.4 %collective-permute-start.15 = (bf16[4,48,768]{2,1,0:T(8,128)(2,1)S(1)}, bf16[4,48,768]{2,1,0:T(8,128)(2,1)S(1)}, u32[]{:S(2)}, u32[]{:S(2)}) collective-permute-start(bf16[4,48,768]{2,1,0:T(8,128)(2,1)S(1)} %get-tuple-element.161), channel_id=1, source_target_pairs={{0,4},{2,6},{4,0},{6,2},{8,12},{10,14},{12,8},{14,10},{16,20},{18,... | collective-permute-start | bytes 884744 | tf_op jit(solution)/shard_map/ppermute | solution.py:85
  68.1 19.9 %collective-permute-start.16 = (bf16[4,48,768]{2,1,0:T(8,128)(2,1)S(1)}, bf16[4,48,768]{2,1,0:T(8,128)(2,1)S(1)}, u32[]{:S(2)}, u32[]{:S(2)}) collective-permute-start(bf16[4,48,768]{2,1,0:T(8,128)(2,1)S(1)} %get-tuple-element.162), channel_id=1, source_target_pairs={{0,2},{2,0},{4,6},{6,4},{8,10},{10,8},{12,14},{14,12},{16,18},{18,... | collective-permute-start | bytes 884744 | tf_op jit(solution)/shard_map/ppermute | solution.py:85
  91.9 4.6 %collective-permute-start.17 = (bf16[1536,768]{1,0:T(8,128)(2,1)S(1)}, bf16[1536,768]{1,0:T(8,128)(2,1)S(1)}, u32[]{:S(2)}, u32[]{:S(2)}) collective-permute-start(bf16[1536,768]{1,0:T(8,128)(2,1)S(1)} %outward.1.mine_ref), channel_id=1, source_target_pairs={{0,1},{1,0},{2,3},{3,2},{4,5},{5,4},{6,7},{7,6},{8,9},{9,8},{10,11... | collective-permute-start | bytes 7077896 | tf_op jit(solution)/shard_map/ppermute | solution.py:89
  91.9 15.7 %collective-permute-start.18 = (bf16[8,48,768]{2,1,0:T(8,128)(2,1)S(1)}, bf16[8,48,768]{2,1,0:T(8,128)(2,1)S(1)}, u32[]{:S(2)}, u32[]{:S(2)}) collective-permute-start(bf16[8,48,768]{2,1,0:T(8,128)(2,1)S(1)} %pad_maximum_fusion.4.pair_a), channel_id=1, source_target_pairs={{0,2},{2,0},{4,6},{6,4},{8,10},{10,8},{12,14},{14,12},{16,18},{18,... | collective-permute-start | bytes 1769480 | tf_op jit(solution)/shard_map/ppermute | solution.py:85
  92.5 15.4 %collective-permute-start.19 = (bf16[8,48,768]{2,1,0:T(8,128)(2,1)S(1)}, bf16[8,48,768]{2,1,0:T(8,128)(2,1)S(1)}, u32[]{:S(2)}, u32[]{:S(2)}) collective-permute-start(bf16[8,48,768]{2,1,0:T(8,128)(2,1)S(1)} %pad_maximum_fusion.5.pair_b), channel_id=1, source_target_pairs={{0,4},{2,6},{4,0},{6,2},{8,12},{10,14},{12,8},{14,10},{16,20},{18,... | collective-permute-start | bytes 1769480 | tf_op jit(solution)/shard_map/ppermute | solution.py:85
  117.2 4.9 %collective-permute-start.20 = (bf16[1536,768]{1,0:T(8,128)(2,1)}, bf16[1536,768]{1,0:T(8,128)(2,1)}, u32[]{:S(2)}, u32[]{:S(2)}) collective-permute-start(bf16[1536,768]{1,0:T(8,128)(2,1)} %get-tuple-element.175.mine_ref), channel_id=1, source_target_pairs={{0,1},{1,0},{2,3},{3,2},{4,5},{5,4},{6,7},{7,6},{8,9},{9,8},{10,11... | collective-permute-start | bytes 7077896 | tf_op jit(solution)/shard_map/ppermute | solution.py:89
  123.8 18.1 %copy-start.33 = (bf16[1536,768]{1,0:T(8,128)(2,1)S(1)}, bf16[1536,768]{1,0:T(8,128)(2,1)}, u32[]{:S(2)}) copy-start(bf16[1536,768]{1,0:T(8,128)(2,1)} %get-tuple-element.183.refs_0_) | copy-start | bytes 7077892
  141.7 19.6 %collective-permute-start.21 = (bf16[1536,768]{1,0:T(8,128)(2,1)}, bf16[1536,768]{1,0:T(8,128)(2,1)}, u32[]{:S(2)}, u32[]{:S(2)}) collective-permute-start(bf16[1536,768]{1,0:T(8,128)(2,1)} %get-tuple-element.190.mine_ref), channel_id=1, source_target_pairs={{0,1},{1,0},{2,3},{3,2},{4,5},{5,4},{6,7},{7,6},{8,9},{9,8},{10,11... | collective-permute-start | bytes 7077896 | tf_op jit(solution)/shard_map/ppermute | solution.py:89
  151.6 30.8 %collective-permute-start.23 = (bf16[2,4,48,1536]{3,2,1,0:T(8,128)(2,1)}, bf16[2,4,48,1536]{3,2,1,0:T(8,128)(2,1)}, u32[]{:S(2)}, u32[]{:S(2)}) collective-permute-start(bf16[2,4,48,1536]{3,2,1,0:T(8,128)(2,1)} %get-tuple-element.185), channel_id=1, source_target_pairs={{0,2},{2,0},{4,6},{6,4},{8,10},{10,8},{12,14},{14,12},{16,18},{18,... | collective-permute-start | bytes 3538952 | tf_op jit(solution)/shard_map/ppermute | solution.py:85
  159.4 31.3 %collective-permute-start.22 = (bf16[2,4,48,1536]{3,2,1,0:T(8,128)(2,1)}, bf16[2,4,48,1536]{3,2,1,0:T(8,128)(2,1)}, u32[]{:S(2)}, u32[]{:S(2)}) collective-permute-start(bf16[2,4,48,1536]{3,2,1,0:T(8,128)(2,1)} %get-tuple-element.189), channel_id=1, source_target_pairs={{0,4},{2,6},{4,0},{6,2},{8,12},{10,14},{12,8},{14,10},{16,20},{18,... | collective-permute-start | bytes 3538952 | tf_op jit(solution)/shard_map/ppermute | solution.py:85
  184.5 22.2 %collective-permute-start.27 = (bf16[4,48,1536]{2,1,0:T(8,128)(2,1)}, bf16[4,48,1536]{2,1,0:T(8,128)(2,1)}, u32[]{:S(2)}, u32[]{:S(2)}) collective-permute-start(bf16[4,48,1536]{2,1,0:T(8,128)(2,1)} %add_bitcast_fusion.1), channel_id=1, source_target_pairs={{0,4},{2,6},{4,0},{6,2},{8,12},{10,14},{12,8},{14,10},{16,20},{18,... | collective-permute-start | bytes 1769480 | tf_op jit(solution)/shard_map/ppermute | solution.py:85
  186.0 20.6 %collective-permute-start.25 = (bf16[2,4,48,384]{3,2,1,0:T(8,128)(2,1)}, bf16[2,4,48,384]{3,2,1,0:T(8,128)(2,1)}, u32[]{:S(2)}, u32[]{:S(2)}) collective-permute-start(bf16[2,4,48,384]{3,2,1,0:T(8,128)(2,1)} %get-tuple-element.194), channel_id=1, source_target_pairs={{0,2},{2,0},{4,6},{6,4},{8,10},{10,8},{12,14},{14,12},{16,18},{18,... | collective-permute-start | bytes 884744 | tf_op jit(solution)/shard_map/ppermute | solution.py:85
  190.2 16.5 %collective-permute-start.26 = (bf16[2,4,48,384]{3,2,1,0:T(8,128)(2,1)}, bf16[2,4,48,384]{3,2,1,0:T(8,128)(2,1)}, u32[]{:S(2)}, u32[]{:S(2)}) collective-permute-start(bf16[2,4,48,384]{3,2,1,0:T(8,128)(2,1)} %get-tuple-element.203), channel_id=1, source_target_pairs={{0,4},{2,6},{4,0},{6,2},{8,12},{10,14},{12,8},{14,10},{16,20},{18,... | collective-permute-start | bytes 884744 | tf_op jit(solution)/shard_map/ppermute | solution.py:85
  192.7 36.9 %collective-permute-start.24 = (bf16[4,48,1536]{2,1,0:T(8,128)(2,1)}, bf16[4,48,1536]{2,1,0:T(8,128)(2,1)}, u32[]{:S(2)}, u32[]{:S(2)}) collective-permute-start(bf16[4,48,1536]{2,1,0:T(8,128)(2,1)} %add_bitcast_fusion), channel_id=1, source_target_pairs={{0,2},{2,0},{4,6},{6,4},{8,10},{10,8},{12,14},{14,12},{16,18},{18,... | collective-permute-start | bytes 1769480 | tf_op jit(solution)/shard_map/ppermute | solution.py:85
  210.0 19.6 %collective-permute-start.29 = (bf16[4,48,384]{2,1,0:T(8,128)(2,1)}, bf16[4,48,384]{2,1,0:T(8,128)(2,1)}, u32[]{:S(2)}, u32[]{:S(2)}) collective-permute-start(bf16[4,48,384]{2,1,0:T(8,128)(2,1)} %add_bitcast_fusion.5), channel_id=1, source_target_pairs={{0,4},{2,6},{4,0},{6,2},{8,12},{10,14},{12,8},{14,10},{16,20},{18,... | collective-permute-start | bytes 442376 | tf_op jit(solution)/shard_map/ppermute | solution.py:85
  211.1 18.6 %collective-permute-start.30 = (bf16[4,48,384]{2,1,0:T(8,128)(2,1)}, bf16[4,48,384]{2,1,0:T(8,128)(2,1)}, u32[]{:S(2)}, u32[]{:S(2)}) collective-permute-start(bf16[4,48,384]{2,1,0:T(8,128)(2,1)} %add_bitcast_fusion.4), channel_id=1, source_target_pairs={{0,2},{2,0},{4,6},{6,4},{8,10},{10,8},{12,14},{14,12},{16,18},{18,... | collective-permute-start | bytes 442376 | tf_op jit(solution)/shard_map/ppermute | solution.py:85
  215.8 13.8 %collective-permute-start.28 = (bf16[2,48,1536]{2,1,0:T(8,128)(2,1)}, bf16[2,48,1536]{2,1,0:T(8,128)(2,1)}, u32[]{:S(2)}, u32[]{:S(2)}) collective-permute-start(bf16[2,48,1536]{2,1,0:T(8,128)(2,1)} %get-tuple-element.210), channel_id=1, source_target_pairs={{0,8},{2,10},{4,12},{6,14},{8,0},{10,2},{12,4},{14,6},{16,24},{18,... | collective-permute-start | bytes 884744 | tf_op jit(solution)/shard_map/ppermute | solution.py:85
  235.3 14.2 %collective-permute-start.34 = (bf16[2,4,48,512]{3,2,1,0:T(8,128)(2,1)S(1)}, bf16[2,4,48,512]{3,2,1,0:T(8,128)(2,1)S(1)}, u32[]{:S(2)}, u32[]{:S(2)}) collective-permute-start(bf16[2,4,48,512]{3,2,1,0:T(8,128)(2,1)S(1)} %get-tuple-element.235), channel_id=1, source_target_pairs={{0,4},{2,6},{4,0},{6,2},{8,12},{10,14},{12,8},{14,10},{16,20},{18,... | collective-permute-start | bytes 1179656 | tf_op jit(solution)/shard_map/ppermute | solution.py:85
  236.3 10.0 %collective-permute-start.33 = (bf16[2,4,48,384]{3,2,1,0:T(8,128)(2,1)S(1)}, bf16[2,4,48,384]{3,2,1,0:T(8,128)(2,1)S(1)}, u32[]{:S(2)}, u32[]{:S(2)}) collective-permute-start(bf16[2,4,48,384]{3,2,1,0:T(8,128)(2,1)S(1)} %copy-done.31), channel_id=1, source_target_pairs={{0,2},{2,0},{4,6},{6,4},{8,10},{10,8},{12,14},{14,12},{16,18},{18,... | collective-permute-start | bytes 884744 | tf_op jit(solution)/shard_map/ppermute | solution.py:85
  237.8 11.7 %collective-permute-start.32 = (bf16[2,48,1536]{2,1,0:T(8,128)(2,1)S(1)}, bf16[2,48,1536]{2,1,0:T(8,128)(2,1)S(1)}, u32[]{:S(2)}, u32[]{:S(2)}) collective-permute-start(bf16[2,48,1536]{2,1,0:T(8,128)(2,1)S(1)} %get-tuple-element.222), channel_id=1, source_target_pairs={{0,8},{2,10},{4,12},{6,14},{8,0},{10,2},{12,4},{14,6},{16,24},{18,... | collective-permute-start | bytes 884744 | tf_op jit(solution)/shard_map/ppermute | solution.py:85
  238.8 15.1 %copy-start.35 = (f32[1536,48]{0,1:T(8,128)S(1)}, f32[1536,48]{0,1:T(8,128)}, u32[]{:S(2)}) copy-start(f32[1536,48]{0,1:T(8,128)} %param.34) | copy-start | bytes 884740
  238.8 15.1 %copy-start.39 = (f32[1536,48]{0,1:T(8,128)S(1)}, f32[1536,48]{0,1:T(8,128)}, u32[]{:S(2)}) copy-start(f32[1536,48]{0,1:T(8,128)} %param.48) | copy-start | bytes 884740
  238.8 15.0 %copy-start.40 = (f32[1536,48]{0,1:T(8,128)S(1)}, f32[1536,48]{0,1:T(8,128)}, u32[]{:S(2)}) copy-start(f32[1536,48]{0,1:T(8,128)} %param.41) | copy-start | bytes 884740
  238.9 12.3 %collective-permute-start.37 = (bf16[2,48,768]{2,1,0:T(8,128)(2,1)S(1)}, bf16[2,48,768]{2,1,0:T(8,128)(2,1)S(1)}, u32[]{:S(2)}, u32[]{:S(2)}) collective-permute-start(bf16[2,48,768]{2,1,0:T(8,128)(2,1)S(1)} %get-tuple-element.227), channel_id=1, source_target_pairs={{0,8},{2,10},{4,12},{6,14},{8,0},{10,2},{12,4},{14,6},{16,24},{18,... | collective-permute-start | bytes 442376 | tf_op jit(solution)/shard_map/ppermute | solution.py:85
  240.7 11.0 %collective-permute-start.38 = (bf16[48,1536]{1,0:T(8,128)(2,1)S(1)}, bf16[48,1536]{1,0:T(8,128)(2,1)S(1)}, u32[]{:S(2)}, u32[]{:S(2)}) collective-permute-start(bf16[48,1536]{1,0:T(8,128)(2,1)S(1)} %fusion.4), channel_id=1, source_target_pairs={{0,16},{2,18},{4,20},{6,22},{8,24},{10,26},{12,28},{14,30},{16,0},... | collective-permute-start | bytes 442376 | tf_op jit(solution)/shard_map/ppermute | solution.py:85
  246.3 14.7 %collective-permute-start.31 = (bf16[1536,768]{1,0:T(8,128)(2,1)S(1)}, bf16[1536,768]{1,0:T(8,128)(2,1)S(1)}, u32[]{:S(2)}, u32[]{:S(2)}) collective-permute-start(bf16[1536,768]{1,0:T(8,128)(2,1)S(1)} %source.1.mine_ref), channel_id=1, source_target_pairs={{0,1},{1,0},{2,3},{3,2},{4,5},{5,4},{6,7},{7,6},{8,9},{9,8},{10,11... | collective-permute-start | bytes 7077896 | tf_op jit(solution)/shard_map/ppermute | solution.py:89
  249.6 20.2 %collective-permute-start.42 = (bf16[48,1536]{1,0:T(8,128)(2,1)S(1)}, bf16[48,1536]{1,0:T(8,128)(2,1)S(1)}, u32[]{:S(2)}, u32[]{:S(2)}) collective-permute-start(bf16[48,1536]{1,0:T(8,128)(2,1)S(1)} %fusion.5), channel_id=1, source_target_pairs={{0,16},{2,18},{4,20},{6,22},{8,24},{10,26},{12,28},{14,30},{16,0},... | collective-permute-start | bytes 442376 | tf_op jit(solution)/shard_map/ppermute | solution.py:85
  249.7 11.0 %collective-permute-start.36 = (bf16[4,48,512]{2,1,0:T(8,128)(2,1)S(1)}, bf16[4,48,512]{2,1,0:T(8,128)(2,1)S(1)}, u32[]{:S(2)}, u32[]{:S(2)}) collective-permute-start(bf16[4,48,512]{2,1,0:T(8,128)(2,1)S(1)} %add_bitcast_fusion.2), channel_id=1, source_target_pairs={{0,2},{2,0},{4,6},{6,4},{8,10},{10,8},{12,14},{14,12},{16,18},{18,... | collective-permute-start | bytes 589832 | tf_op jit(solution)/shard_map/ppermute | solution.py:85
  251.1 9.6 %collective-permute-start.35 = (bf16[4,48,384]{2,1,0:T(8,128)(2,1)S(1)}, bf16[4,48,384]{2,1,0:T(8,128)(2,1)S(1)}, u32[]{:S(2)}, u32[]{:S(2)}) collective-permute-start(bf16[4,48,384]{2,1,0:T(8,128)(2,1)S(1)} %add_bitcast_fusion.3), channel_id=1, source_target_pairs={{0,4},{2,6},{4,0},{6,2},{8,12},{10,14},{12,8},{14,10},{16,20},{18,... | collective-permute-start | bytes 442376 | tf_op jit(solution)/shard_map/ppermute | solution.py:85
  251.7 8.3 %collective-permute-start.39 = (bf16[48,768]{1,0:T(8,128)(2,1)S(1)}, bf16[48,768]{1,0:T(8,128)(2,1)S(1)}, u32[]{:S(2)}, u32[]{:S(2)}) collective-permute-start(bf16[48,768]{1,0:T(8,128)(2,1)S(1)} %fusion.9), channel_id=1, source_target_pairs={{0,16},{2,18},{4,20},{6,22},{8,24},{10,26},{12,28},{14,30},{16,0},... | collective-permute-start | bytes 221192 | tf_op jit(solution)/shard_map/ppermute | solution.py:85
  260.9 5.5 %collective-permute-start.40 = (bf16[2,48,896]{2,1,0:T(8,128)(2,1)S(1)}, bf16[2,48,896]{2,1,0:T(8,128)(2,1)S(1)}, u32[]{:S(2)}, u32[]{:S(2)}) collective-permute-start(bf16[2,48,896]{2,1,0:T(8,128)(2,1)S(1)} %get-tuple-element.251), channel_id=1, source_target_pairs={{0,8},{2,10},{4,12},{6,14},{8,0},{10,2},{12,4},{14,6},{16,24},{18,... | collective-permute-start | bytes 516104 | tf_op jit(solution)/shard_map/ppermute | solution.py:85
  266.4 5.9 %collective-permute-start.41 = (bf16[48,896]{1,0:T(8,128)(2,1)S(1)}, bf16[48,896]{1,0:T(8,128)(2,1)S(1)}, u32[]{:S(2)}, u32[]{:S(2)}) collective-permute-start(bf16[48,896]{1,0:T(8,128)(2,1)S(1)} %fusion.7), channel_id=1, source_target_pairs={{0,16},{2,18},{4,20},{6,22},{8,24},{10,26},{12,28},{14,30},{16,0},... | collective-permute-start | bytes 258056 | tf_op jit(solution)/shard_map/ppermute | solution.py:85
  (55 other events, 357.6 us)

commit v2 on v1

--- a/solution.py
+++ b/solution.py
@@ -15,7 +15,7 @@
 LANES = 128
 ROWS = 384
 COST_SHARE = 1
-ATTEND, BACK, EXPAND, CONTRACT, GRADS = 12, 20, 28, 40, 20
+ATTEND, BACK, EXPAND, CONTRACT, GRADS = 12, 16, 22, 26, 16
 
 norm_epsilon = 1e-12
 low = jnp.bfloat16
@@ -644,7 +644,13 @@
 def weight_grad_kernel(bit, count, turned, extra, me_ref, left_ref, *refs):
     rights, refs = refs[:count], refs[count:]
     if extra:
-        extra_ref, refs = refs[0], refs[1:]
+        small_refs, refs = refs[:extra], refs[extra:]
+        small, refs = refs[-1], refs[:-1]
+        small[...] = jnp.zeros_like(small)
+        at = 0
+        for small_ref in small_refs:
+            small[at : at + small_ref.shape[0], :] = small_ref[...]
+            at += small_ref.shape[0]
     left = left_ref
     if not turned:
         left, refs = refs[-1], refs[:-1]
@@ -657,10 +663,12 @@
 
         lax.fori_loop(0, left_ref.shape[0] // ROWS, turn_block, 0, unroll=True)
     total_ref = refs[-1] if bit is not None else refs[0]
+    if extra:
+        total_ref[:, total_ref.shape[1] - LANES :] = small[...].T
     block = 2 * ROWS if rights[0].shape[1] % D else D
     if rights[0].shape[1] % block:
         right = jnp.concatenate([piece[...] for piece in rights], axis=1)
-        total_ref[...] = dot_nn(left[...], right)
+        total_ref[:, : right.shape[1]] = dot_nn(left[...], right)
     else:
         for at, piece in enumerate(rights):
             steps = piece.shape[1] // block
@@ -680,7 +688,6 @@
     if bit is None:
         return
     layers, rows = refs[0].shape[1:3]
-    width = total_ref.shape[1]
     for target, far in ((refs[0], 1), (refs[1], 0)):
 
         def spread(i, carry, target=target, far=far):
@@ -688,23 +695,20 @@
             plane = 2 * other + far if bit == 0 else other + 2 * far
             owner = me_ref[0] ^ (4 * k + plane)
             start = pl.multiple_of(owner * rows, 8)
-            target[other, k, :, :width] = total_ref[pl.ds(start, rows), :].astype(low)
-            if extra:
-                target[other, k, :, width:] = extra_ref[owner]
+            target[other, k] = total_ref[pl.ds(start, rows), :].astype(low)
             return carry
 
         lax.fori_loop(0, 2 * layers, spread, 0)
 
 
-def weight_grad(left, rights, me, size, bit, turned=False, extra=None):
+def weight_grad(left, rights, me, size, bit, turned=False, extras=()):
     tokens = rights[0].shape[0]
     width = sum(right.shape[1] for right in rights)
     layers, rows = size // 4, D // size
-    extras = () if extra is None else (extra,)
     if me is not None:
-        total = width + (0 if extra is None else LANES)
+        total = width + (LANES if extras else 0)
         outs = (shape((2, layers, rows, total), low),) * 2
-        scratch = [pltpu.VMEM((D, width), full)]
+        scratch = [pltpu.VMEM((D, total), full)]
     else:
         outs = (shape((D, width), full),)
         scratch = []
@@ -712,13 +716,15 @@
         bit = None
     if not turned:
         scratch.append(pltpu.VMEM((D, tokens), low))
+    if extras:
+        scratch.append(pltpu.VMEM((LANES, D), full))
 
     def whole(array):
         return pl.BlockSpec(array.shape, lambda j, m: (0,) * len(array.shape))
 
     flat = (left, *rights, *extras)
     return pl.pallas_call(
-        partial(weight_grad_kernel, bit, len(rights), turned, extra is not None),
+        partial(weight_grad_kernel, bit, len(rights), turned, len(extras)),
         out_shape=outs,
         grid_spec=pltpu.PrefetchScalarGridSpec(
             num_scalar_prefetch=1,
@@ -909,35 +915,40 @@
         more_up = hop(next_up, 1, size)
 
         attention(1, next_up)
-        got_out, got_0, more_down = after_all((got_out, got_0, more_down), stacked[1])
+        more_down = after(more_down, stacked[1])
+        own_down, out_down = combine([(kept_down, got_down, more_down)])
+        near_down = hop(out_down, 4, size)
+        gated = after(turned, out_down)
+        sent_1, kept_1 = weight_grad(gated, [stacked[1]], me, size, 0, True)
+        got_1 = hop(sent_1, 1, size)
+
+        attention(2, sent_1)
+        extras = (
+            first_sums,
+            second_sums,
+            hidden_sums.reshape(2, rows, size).transpose(0, 2, 1).reshape(2, D),
+            jnp.concatenate(head_sums, axis=1).reshape(rows, size).T.reshape(1, D),
+        )
+        got_out, got_0, more_up = after_all((got_out, got_0, more_up), stacked[2])
         next_out, next_0 = after_all((kept_out[1] + got_out[1], kept_0[1] + got_0[1]))
         more_out, more_0 = hop(next_out, 2, size), hop(next_0, 1, size)
-        own_down, out_down = combine([(kept_down, got_down, more_down)])
-        near_down = hop(out_down, 4, size)
-        gated = after(turned, next_out, next_0, out_down)
-        sent_1, kept_1 = weight_grad(gated, [stacked[1]], me, size, 0, True)
-        got_1 = hop(sent_1, 1, size)
-
-        attention(2, sent_1)
-        extra = small_outgoing(first_sums, head_sums).reshape(size, rows, per_row)
-        extra = jnp.pad(extra, ((0, 0), (0, 0), (0, LANES - per_row))).astype(low)
-        more_up, near_down, more_out, more_0 = after_all(
-            (more_up, near_down, more_out, more_0), stacked[2]
+        own_up, out_up = combine([(kept_up, got_up, after(more_up, next_out, next_0))])
+        near_up = hop(out_up, 4, size)
+        near_down = after(near_down, out_up)
+        next_far = far_half(own_down, near_down)
+        gated = after(turned, out_up, next_far)
+        sent_2, kept_2 = weight_grad(gated, [stacked[2]], me, size, 1, True, extras)
+        got_2 = hop(sent_2, 2, size)
+
+        mine_source = source_part([after(stacked[0], sent_2)] + stacked[1:], inward)
+        other_source = swap_cores(mine_source)
+        far_down = hop(after(next_far, mine_source), 8, size)
+        near_up, more_out, more_0, got_1, got_2 = after_all(
+            (near_up, more_out, more_0, got_1, got_2), mine_source
         )
-        own_up, out_up = combine([(kept_up, got_up, more_up)])
-        near_up = hop(out_up, 4, size)
-        next_far = far_half(own_down, near_down)
-        far_down = hop(next_far, 8, size)
         own_near, out_near = combine([(kept_out, got_out, more_out), (kept_0, got_0, more_0)])
         near_near = hop(out_near, 4, size)
-        gated = after(turned, out_up, next_far, out_near)
-        sent_2, kept_2 = weight_grad(gated, [stacked[2]], me, size, 1, True, extra)
-        got_2 = hop(sent_2, 2, size)
-
-        mine_source = source_part([after(stacked[0], sent_2)] + stacked[1:], inward)
-        other_source = swap_cores(mine_source)
-        near_up, got_1, got_2 = after_all((near_up, got_1, got_2), mine_source)
-        next_far = far_half(own_up, near_up)
+        next_far = far_half(own_up, after(near_up, out_near))
         far_up = hop(next_far, 8, size)
         got_1, got_2 = after_all((got_1, got_2), next_far)
         next_1, next_2 = after_all((kept_1[1] + got_1[1], kept_2[1] + got_2[1]))
@@ -958,7 +969,12 @@
         outward_grad = near_grad[:, :width]
         cut = 3 * LANES
         inward_grads = [near_grad[:, width:], far_grad[:, :cut], far_grad[:, cut : 2 * cut]]
-        small_grad = far_grad[:, 2 * cut : 2 * cut + per_row].reshape(-1)
+        small_grad = far_grad[:, 2 * cut :]
+        small_grads = (
+            small_grad[:, 8].reshape(heads_bias.shape),
+            small_grad[:, 6:8].T.reshape(hidden_bias.shape),
+            small_grad[:, :6].T,
+        )
     else:
 
         def reduced(left, rights, turned=False):
@@ -979,6 +995,11 @@
         small_grad = lax.psum_scatter(
             small_outgoing(first_sums, head_sums), "dp", scatter_dimension=0, tiled=True
         ).reshape(-1)
+        small_grads = (
+            small_grad[:heads_size].reshape(heads_bias.shape),
+            small_grad[heads_size : heads_size + hidden_size].reshape(hidden_bias.shape),
+            small_grad[heads_size + hidden_size :].reshape(norm_vectors.shape),
+        )
         input_grad = finish(mine_source, swap_cores(mine_source), first_grad)
 
     inward_grad = jnp.stack(
@@ -994,9 +1015,7 @@
         outward_grad.T,
         upward_grad,
         downward_grad.T,
-        small_grad[:heads_size].reshape(heads_bias.shape),
-        small_grad[heads_size : heads_size + hidden_size].reshape(hidden_bias.shape),
-        small_grad[heads_size + hidden_size :].reshape(norm_vectors.shape),
+        *small_grads,
     )
 
     step_value = step_count[0].astype(full)

time: 277 us -> 273 us (0.986)
  waiting for transfers between devices: 47.8 us -> 52.9 us
  Pallas kernels: 130 us -> 126 us
    ppermute x39, waiting for transfers between devices: 39.9 us -> 45.1 us  [hop(): return lax.ppermute(value, 'dp', [(d, d ^ offset) for d in range(size)])]
    reshape x9 -> x5, local copies, waits for them, and re-layouts: 5.47 us -> 2.39 us  [the longest x2 2.14 us: per_device(): jnp.concatenate(head_sums, axis=1).reshape(rows, size).T.reshape(1, D)]
    unnamed x120 -> x148, local copies, waits for them, and re-layouts: 13.7 us -> 13.8 us
  transfers between devices with their start and end apart: 43 -> 43, of which waited for: 16 -> 18; matrix products, arithmetic and copies ran while one was open for 11% -> 10% of each run, Pallas kernels for 34% -> 35%
where the time goes in v2:
time: 273 us; the launch traced here: 272 us
  Pallas kernels  126 us (46%)
  waiting for transfers between devices  52.9 us (19%)
  starting transfers between devices  44.2 us (16%)
  other arithmetic  23.8 us (9%)
  local copies, waits for them, and re-layouts  22.2 us (8%)
    ppermute x39, waiting for transfers between devices, hop(): return lax.ppermute(value, 'dp', [(d, d ^ offset) for d in range(size)])  45.1 us
    ppermute x39, starting transfers between devices, hop(): return lax.ppermute(value, 'dp', [(d, d ^ offset) for d in range(size)])  43.9 us
    pallas_call x2, Pallas kernels, attend(): pl.pallas_call(attend_kernel, out_shape=(main((rows, groups * width), low...  22.6 us
    pallas_call x3, Pallas kernels, attend_back(): pl.pallas_call(attend_back_kernel, out_shape=(main((rows, width), low), s...  20 us
    pallas_call x1, Pallas kernels, contract(): pl.pallas_call(contract_kernel, out_shape=(shape((rows, D), low), shape((...  17.5 us
    pallas_call x6, Pallas kernels, weight_grad(): pl.pallas_call(partial(weight_grad_kernel, bit, len(rights), turned, len(...  17.4 us
    unnamed x148, local copies, waits for them, and re-layouts  13.8 us
    pallas_call x1, Pallas kernels, expand_first(): pl.pallas_call(expand_first_kernel, out_shape=(main((rows, D), full), mai...  10 us
  transfers between devices with their start and end apart: 43, of which 18 were waited for; matrix products, arithmetic and copies ran while one was open for 10% of the time, Pallas kernels for 35%

profile of v2, /device:TPU:0, one launch (start us, length us, event | category | flops | bytes accessed | tf_op | source)
XLA Modules:
  0.0 271.6 jit_solution(5834748381617433237)
XLA Ops:
  4.5 3.1 %collective-permute-start = (bf16[48,1280]{1,0:T(8,128)(2,1)S(1)}, bf16[48,1280]{1,0:T(8,128)(2,1)S(1)}, u32[]{:S(2)}, u32[]{:S(2)}) collective-permute-start(bf16[48,1280]{1,0:T(8,128)(2,1)S(1)} %fusion.6), channel_id=1, source_target_pairs={{0,8},{2,10},{4,12},{6,14},{8,0},{10,2},{12,4},{14,6},{16,24},{18,... | collective-permute-start | bytes 368648 | tf_op jit(solution)/shard_map/ppermute | solution.py:85
  7.6 2.6 collective-permute-start.1
  15.6 4.3 %collective-permute-done.1 = bf16[48,1280]{1,0:T(8,128)(2,1)S(1)} collective-permute-done((bf16[48,1280]{1,0:T(8,128)(2,1)S(1)}, bf16[48,1280]{1,0:T(8,128)(2,1)S(1)}, u32[]{:S(2)}, u32[]{:S(2)}) %collective-permute-start.1) | collective-permute-done | bytes 122912 | tf_op jit(solution)/shard_map/ppermute | solution.py:85
  20.0 3.1 %collective-permute-start.7 = (bf16[48,1920]{1,0:T(8,128)(2,1)S(1)}, bf16[48,1920]{1,0:T(8,128)(2,1)S(1)}, u32[]{:S(2)}, u32[]{:S(2)}) collective-permute-start(bf16[48,1920]{1,0:T(8,128)(2,1)S(1)} %pad_maximum_fusion.13), channel_id=1, source_target_pairs={{0,16},{2,18},{4,20},{6,22},{8,24},{10,26},{12,28},{14,30},{16,0},... | collective-permute-start | bytes 552968 | tf_op jit(solution)/shard_map/ppermute | solution.py:85
  23.1 1.6 collective-permute-start.4
  24.7 1.5 collective-permute-start.3
  26.2 4.3 %collective-permute-done.7 = bf16[48,1920]{1,0:T(8,128)(2,1)S(1)} collective-permute-done((bf16[48,1920]{1,0:T(8,128)(2,1)S(1)}, bf16[48,1920]{1,0:T(8,128)(2,1)S(1)}, u32[]{:S(2)}, u32[]{:S(2)}) %collective-permute-start.7) | collective-permute-done | bytes 184352 | tf_op jit(solution)/shard_map/ppermute | solution.py:85
  32.4 1.5 collective-permute-start.6
  33.9 6.6 %collective-permute-done.8 = bf16[2,48,1920]{2,1,0:T(8,128)(2,1)S(1)} collective-permute-done((bf16[2,48,1920]{2,1,0:T(8,128)(2,1)S(1)}, bf16[2,48,1920]{2,1,0:T(8,128)(2,1)S(1)}, u32[]{:S(2)}, u32[]{:S(2)}) %collective-permute-start.8) | collective-permute-done | bytes 368672 | tf_op jit(solution)/shard_map/ppermute | solution.py:85
  40.8 8.1 %collective-permute-done.11 = bf16[48,1536]{1,0:T(8,128)(2,1)S(1)} collective-permute-done((bf16[48,1536]{1,0:T(8,128)(2,1)S(1)}, bf16[48,1536]{1,0:T(8,128)(2,1)S(1)}, u32[]{:S(2)}, u32[]{:S(2)}) %collective-permute-start.11) | collective-permute-done | bytes 147488 | tf_op jit(solution)/shard_map/ppermute | solution.py:85
  49.8 1.6 collective-permute-start.9
  53.4 8.2 %attend.2 = (bf16[1536,384]{1,0:T(8,128)(2,1)}, bf16[3,2,512,512]{3,2,1,0:T(8,128)(2,1)}, bf16[1536,128]{1,0:T(8,128)(2,1)}) custom-call(s32[3]{0:T(128)S(1)} %copy-done.41, bf16[1536,768]{1,0:T(8,128)(2,1)} %x_ref.4, bf16[768,1280]{1,0:T(8,128)(2,1)S(1)} %place.3.w_ref.refs_3_, f32[2,384]{1,0:T(2,128)S(1)} %reshape.234.bias_ref), custom_call_target="tpu_custom_call" | custom-call | flops 1711276032 | bytes 3145728 | tf_op jit(solution)/shard_map/attend/pallas_call | solution.py:259
  70.5 14.4 %attend.3 = (bf16[1536,768]{1,0:T(8,128)(2,1)}, bf16[6,2,512,512]{3,2,1,0:T(8,128)(2,1)}, bf16[1536,256]{1,0:T(8,128)(2,1)}) custom-call(s32[3]{0:T(128)S(1)} %copy-done.41, bf16[1536,768]{1,0:T(8,128)(2,1)} %x_ref.4, bf16[768,1280]{1,0:T(8,128)(2,1)S(1)} %place.3.w_ref.refs_3_, f32[2,384]{1,0:T(2,128)S(1)} %reshape.234.bias_ref), custom_call_target="tpu_custom_call" | custom-call | flops 3422552064 | bytes 6291456 | tf_op jit(solution)/shard_map/attend/pallas_call | solution.py:259
  84.9 2.2 collective-permute-done.15
  87.1 1.8 collective-permute-done.16
  89.3 3.5 %outward.1.mine_ref = bf16[1536,768]{1,0:T(8,128)(2,1)S(1)} custom-call(bf16[1536,128]{1,0:T(8,128)(2,1)} %get-tuple-element.156.refs_0_, bf16[1536,256]{1,0:T(8,128)(2,1)} %get-tuple-element.167.refs_1_, bf16[768,1920]{1,0:T(8,128)(2,1)S(1)} %place.4.refs_2_.up_ref.down_ref.up_first.down_first.w_ref), custom_call_target="tpu_custom_call" | custom-call | flops 905969664 | bytes 4128768 | tf_op jit(solution)/shard_map/outward/pallas_call | solution.py:368
  94.1 3.3 %collective-permute-done.17.other_ref = bf16[1536,768]{1,0:T(8,128)(2,1)S(1)} collective-permute-done((bf16[1536,768]{1,0:T(8,128)(2,1)S(1)}, bf16[1536,768]{1,0:T(8,128)(2,1)S(1)}, u32[]{:S(2)}, u32[]{:S(2)}) %collective-permute-start.17) | collective-permute-done | bytes 2359328 | tf_op jit(solution)/shard_map/ppermute | solution.py:89
  97.4 10.0 %expand_first.1 = (f32[1536,768]{1,0:T(8,128)}, bf16[1536,768]{1,0:T(8,128)(2,1)}, bf16[1536,768]{1,0:T(8,128)(2,1)}, bf16[1536,768]{1,0:T(8,128)(2,1)}, f32[1536,768]{1,0:T(8,128)}, /*index=5*/f32[1536,1]{1,0:T(8,128)}) custom-call(bf16[1536,768]{1,0:T(8,128)(2,1)S(1)} %outward.1.mine_ref, bf16[1536,768]{1,0:T(8,128)(2,1)S(1)} %collective-permute-done.17.other_ref, ...), custom_call_target="tpu_custom_call" | custom-call | flops 3623878656 | bytes 21233664 | tf_op jit(solution)/shard_map/expand_first/pallas_call | solution.py:411
  109.1 9.1 %expand_last.1 = (bf16[1536,768]{1,0:T(8,128)(2,1)}, bf16[1536,768]{1,0:T(8,128)(2,1)}, bf16[1536,768]{1,0:T(8,128)(2,1)}) custom-call(f32[1536,768]{1,0:T(8,128)} %get-tuple-element.174.total_ref, bf16[1536,768]{1,0:T(8,128)(2,1)} %get-tuple-element.189.middle_ref.left_ref, f32[1,1536]{1,0:T(1,128)S(1)} %reshape.237.bias_ref, ...), custom_call_target="tpu_custom_call" | custom-call | flops 3623878656 | bytes 14155776 | tf_op jit(solution)/shard_map/expand_last/pallas_call | solution.py:453
  118.7 4.5 %collective-permute-done.20.other_ref = bf16[1536,768]{1,0:T(8,128)(2,1)} collective-permute-done((bf16[1536,768]{1,0:T(8,128)(2,1)}, bf16[1536,768]{1,0:T(8,128)(2,1)}, u32[]{:S(2)}, u32[]{:S(2)}) %collective-permute-start.20) | collective-permute-done | bytes 2359328 | tf_op jit(solution)/shard_map/ppermute | solution.py:89
  123.2 1.7 copy-done.3
  124.8 17.5 %contract.1 = (bf16[1536,768]{1,0:T(8,128)(2,1)S(1)}, f32[3,768]{1,0:T(4,128)S(1)}, f32[1,1536]{1,0:T(1,128)S(1)}, bf16[1536,768]{1,0:T(8,128)(2,1)}, f32[1536,7...) custom-call(bf16[1536,768]{1,0:T(8,128)(2,1)} %get-tuple-element.178.mine_ref, ...), custom_call_target="tpu_custom_call" | custom-call | flops 7247757312 | bytes 14155776 | tf_op jit(solution)/shard_map/contract/pallas_call | solution.py:513
  142.6 1.7 copy-done.44
  144.2 4.3 %weight_grad.6 = (bf16[2,4,48,1536]{3,2,1,0:T(8,128)(2,1)S(1)}, bf16[2,4,48,1536]{3,2,1,0:T(8,128)(2,1)S(1)}) custom-call(s32[1]{0:T(128)} %bitcast.me_ref, bf16[1536,768]{1,0:T(8,128)(2,1)S(1)} %copy-done.44, bf16[1536,768]{1,0:T(8,128)(2,1)S(1)} %copy-done.46, bf16[1536,768]{1,0:T(8,128)(2,1)S(1)} %copy-done.47), custom_call_target="tpu_custom_call" | custom-call | flops 3623878656 | bytes 7077888 | tf_op jit(solution)/shard_map/weight_grad/pallas_call | solution.py:726
  148.6 1.5 collective-permute-start.23
  150.2 4.3 %weight_grad.7 = (bf16[2,4,48,1536]{3,2,1,0:T(8,128)(2,1)S(1)}, bf16[2,4,48,1536]{3,2,1,0:T(8,128)(2,1)S(1)}) custom-call(s32[1]{0:T(128)} %bitcast.me_ref, bf16[1536,768]{1,0:T(8,128)(2,1)S(1)} %copy-done.45, bf16[1536,768]{1,0:T(8,128)(2,1)S(1)} %copy-done.42, bf16[1536,768]{1,0:T(8,128)(2,1)S(1)} %copy-done.43), custom_call_target="tpu_custom_call" | custom-call | flops 3623878656 | bytes 7077888 | tf_op jit(solution)/shard_map/weight_grad/pallas_call | solution.py:726
  155.1 9.3 %first_back.1 = (f32[3,768]{1,0:T(4,128)S(1)}, f32[1536,768]{1,0:T(8,128)}, bf16[1536,768]{1,0:T(8,128)(2,1)}, bf16[1536,384]{1,0:T(8,128)(2,1)}) custom-call(bf16[1536,768]{1,0:T(8,128)(2,1)S(1)} %get-tuple-element.193.mine_ref, bf16[1536,768]{1,0:T(8,128)(2,1)S(1)} %collective-permute-done.21.other_ref, f32[1536,768]{1,0:T(8,128)} %get-tuple-element.194.second_ref, ...), custom_call_target="tpu_custom_call" | custom-call | flops 905969664 | bytes 23592960 | tf_op jit(solution)/shard_map/first_back/pallas_call | solution.py:579
  165.0 1.7 copy-done.16
  166.6 2.4 weight_grad.8
  169.0 6.7 %attend_back.3 = (bf16[1536,384]{1,0:T(8,128)(2,1)}, f32[2,128]{1,0:T(2,128)S(1)}) custom-call(bf16[1536,384]{1,0:T(8,128)(2,1)} %get-tuple-element.198.qkv_ref, bf16[3,2,512,512]{3,2,1,0:T(8,128)(2,1)} %get-tuple-element.199.weight_ref, bf16[1536,384]{1,0:T(8,128)(2,1)} %get-tuple-element.200.grad_ref), custom_call_target="tpu_custom_call" | custom-call | flops 1610612736 | bytes 5505024 | tf_op jit(solution)/shard_map/attend_back/pallas_call | solution.py:330
  179.7 2.3 weight_grad.9
  188.2 6.7 %attend_back.4 = (bf16[1536,384]{1,0:T(8,128)(2,1)}, f32[2,128]{1,0:T(2,128)S(1)}) custom-call(bf16[1536,768]{1,0:T(8,128)(2,1)} %get-tuple-element.216.qkv_ref, bf16[6,2,512,512]{3,2,1,0:T(8,128)(2,1)} %get-tuple-element.210.weight_ref, bf16[1536,384]{1,0:T(8,128)(2,1)} %get-tuple-element.200.grad_ref), custom_call_target="tpu_custom_call" | custom-call | flops 1610612736 | bytes 5505024 | tf_op jit(solution)/shard_map/attend_back/pallas_call | solution.py:330
  196.9 1.7 collective-permute-start.28
  198.6 2.3 weight_grad.10
  201.5 6.6 %attend_back.5 = (bf16[1536,384]{1,0:T(8,128)(2,1)}, f32[2,128]{1,0:T(2,128)S(1)}) custom-call(bf16[1536,768]{1,0:T(8,128)(2,1)} %get-tuple-element.216.qkv_ref, bf16[6,2,512,512]{3,2,1,0:T(8,128)(2,1)} %get-tuple-element.210.weight_ref, bf16[1536,384]{1,0:T(8,128)(2,1)} %get-tuple-element.200.grad_ref), custom_call_target="tpu_custom_call" | custom-call | flops 1610612736 | bytes 5505024 | tf_op jit(solution)/shard_map/attend_back/pallas_call | solution.py:330
  213.1 1.7 add_bitcast_fusion.5
  216.1 2.1 combine.5
  219.1 1.6 fusion.4
  220.7 1.6 weight_grad.11
  226.4 1.5 copy-done.14
  228.0 5.8 %source.1.mine_ref = bf16[1536,768]{1,0:T(8,128)(2,1)S(1)} custom-call(bf16[1536,384]{1,0:T(8,128)(2,1)} %get-tuple-element.237.refs_0_, bf16[1536,384]{1,0:T(8,128)(2,1)} %get-tuple-element.211.refs_0_.refs_1_, bf16[1536,384]{1,0:T(8,128)(2,1)} %get-tuple-element.217.refs_0_.refs_2_, bf16[768,1280]{1,0:T(8,128)(2,1)S(1)} %copy-done.14), custom_call_target="tpu_custom_call" | custom-call | flops 2717908992 | bytes 5308416 | tf_op jit(solution)/shard_map/source/pallas_call | solution.py:614
  234.4 1.6 collective-permute-start.37
  236.1 3.0 %collective-permute-start.42 = (bf16[48,1536]{1,0:T(8,128)(2,1)S(1)}, bf16[48,1536]{1,0:T(8,128)(2,1)S(1)}, u32[]{:S(2)}, u32[]{:S(2)}) collective-permute-start(bf16[48,1536]{1,0:T(8,128)(2,1)S(1)} %fusion.5), channel_id=1, source_target_pairs={{0,16},{2,18},{4,20},{6,22},{8,24},{10,26},{12,28},{14,30},{16,0},... | collective-permute-start | bytes 442376 | tf_op jit(solution)/shard_map/ppermute | solution.py:85
  241.3 3.7 %collective-permute-done.38 = bf16[48,1536]{1,0:T(8,128)(2,1)S(1)} collective-permute-done((bf16[48,1536]{1,0:T(8,128)(2,1)S(1)}, bf16[48,1536]{1,0:T(8,128)(2,1)S(1)}, u32[]{:S(2)}, u32[]{:S(2)}) %collective-permute-start.38) | collective-permute-done | bytes 147488 | tf_op jit(solution)/shard_map/ppermute | solution.py:85
  246.7 2.0 multiply_subtract_fusion
  248.6 4.2 %collective-permute-done.42 = bf16[48,1536]{1,0:T(8,128)(2,1)S(1)} collective-permute-done((bf16[48,1536]{1,0:T(8,128)(2,1)S(1)}, bf16[48,1536]{1,0:T(8,128)(2,1)S(1)}, u32[]{:S(2)}, u32[]{:S(2)}) %collective-permute-start.42) | collective-permute-done | bytes 147488 | tf_op jit(solution)/shard_map/ppermute | solution.py:85
  255.9 5.3 %finish.1 = f32[1536,768]{1,0:T(8,128)} custom-call(bf16[1536,768]{1,0:T(8,128)(2,1)S(1)} %source.1.mine_ref, bf16[1536,768]{1,0:T(8,128)(2,1)S(1)} %collective-permute-done.29.other_ref, f32[1536,768]{1,0:T(8,128)} %get-tuple-element.259.first_ref), custom_call_target="tpu_custom_call" | custom-call | flops 2359296 | bytes 14155776 | tf_op jit(solution)/shard_map/finish/pallas_call | solution.py:632
  262.5 4.3 %collective-permute-done.41 = bf16[48,896]{1,0:T(8,128)(2,1)S(1)} collective-permute-done((bf16[48,896]{1,0:T(8,128)(2,1)S(1)}, bf16[48,896]{1,0:T(8,128)(2,1)S(1)}, u32[]{:S(2)}, u32[]{:S(2)}) %collective-permute-start.41) | collective-permute-done | bytes 86048 | tf_op jit(solution)/shard_map/ppermute | solution.py:85
  (306 shorter events, 64.8 us)
Async XLA Ops:
  4.5 11.1 %collective-permute-start = (bf16[48,1280]{1,0:T(8,128)(2,1)S(1)}, bf16[48,1280]{1,0:T(8,128)(2,1)S(1)}, u32[]{:S(2)}, u32[]{:S(2)}) collective-permute-start(bf16[48,1280]{1,0:T(8,128)(2,1)S(1)} %fusion.6), channel_id=1, source_target_pairs={{0,8},{2,10},{4,12},{6,14},{8,0},{10,2},{12,4},{14,6},{16,24},{18,... | collective-permute-start | bytes 368648 | tf_op jit(solution)/shard_map/ppermute | solution.py:85
  7.6 12.3 %collective-permute-start.1 = (bf16[48,1280]{1,0:T(8,128)(2,1)S(1)}, bf16[48,1280]{1,0:T(8,128)(2,1)S(1)}, u32[]{:S(2)}, u32[]{:S(2)}) collective-permute-start(bf16[48,1280]{1,0:T(8,128)(2,1)S(1)} %fusion.6), channel_id=1, source_target_pairs={{0,16},{2,18},{4,20},{6,22},{8,24},{10,26},{12,28},{14,30},{16,0},... | collective-permute-start | bytes 368648 | tf_op jit(solution)/shard_map/ppermute | solution.py:85
  10.2 9.7 %collective-permute-start.2 = (bf16[48,1280]{1,0:T(8,128)(2,1)S(1)}, bf16[48,1280]{1,0:T(8,128)(2,1)S(1)}, u32[]{:S(2)}, u32[]{:S(2)}) collective-permute-start(bf16[48,1280]{1,0:T(8,128)(2,1)S(1)} %fusion.6), channel_id=1, source_target_pairs={{0,24},{2,26},{4,28},{6,30},{8,16},{10,18},{12,20},{14,22},{16,8},... | collective-permute-start | bytes 368648 | tf_op jit(solution)/shard_map/ppermute | solution.py:85
  20.0 10.6 %collective-permute-start.7 = (bf16[48,1920]{1,0:T(8,128)(2,1)S(1)}, bf16[48,1920]{1,0:T(8,128)(2,1)S(1)}, u32[]{:S(2)}, u32[]{:S(2)}) collective-permute-start(bf16[48,1920]{1,0:T(8,128)(2,1)S(1)} %pad_maximum_fusion.13), channel_id=1, source_target_pairs={{0,16},{2,18},{4,20},{6,22},{8,24},{10,26},{12,28},{14,30},{16,0},... | collective-permute-start | bytes 552968 | tf_op jit(solution)/shard_map/ppermute | solution.py:85
  23.1 7.5 %collective-permute-start.4 = (bf16[4,48,640]{2,1,0:T(8,128)(2,1)S(1)}, bf16[4,48,640]{2,1,0:T(8,128)(2,1)S(1)}, u32[]{:S(2)}, u32[]{:S(2)}) collective-permute-start(bf16[4,48,640]{2,1,0:T(8,128)(2,1)S(1)} %get-tuple-element.145), channel_id=1, source_target_pairs={{0,2},{2,0},{4,6},{6,4},{8,10},{10,8},{12,14},{14,12},{16,18},{18,... | collective-permute-start | bytes 737288 | tf_op jit(solution)/shard_map/ppermute | solution.py:85
  24.7 6.2 %collective-permute-start.3 = (bf16[4,48,640]{2,1,0:T(8,128)(2,1)S(1)}, bf16[4,48,640]{2,1,0:T(8,128)(2,1)S(1)}, u32[]{:S(2)}, u32[]{:S(2)}) collective-permute-start(bf16[4,48,640]{2,1,0:T(8,128)(2,1)S(1)} %get-tuple-element.144), channel_id=1, source_target_pairs={{0,4},{2,6},{4,0},{6,2},{8,12},{10,14},{12,8},{14,10},{16,20},{18,... | collective-permute-start | bytes 737288 | tf_op jit(solution)/shard_map/ppermute | solution.py:85
  30.6 10.0 %collective-permute-start.8 = (bf16[2,48,1920]{2,1,0:T(8,128)(2,1)S(1)}, bf16[2,48,1920]{2,1,0:T(8,128)(2,1)S(1)}, u32[]{:S(2)}, u32[]{:S(2)}) collective-permute-start(bf16[2,48,1920]{2,1,0:T(8,128)(2,1)S(1)} %pad_maximum_fusion.9), channel_id=1, source_target_pairs={{0,8},{2,10},{4,12},{6,14},{8,0},{10,2},{12,4},{14,6},{16,24},{18,... | collective-permute-start | bytes 1105928 | tf_op jit(solution)/shard_map/ppermute | solution.py:85
  31.0 18.7 %collective-permute-start.5 = (bf16[8,48,640]{2,1,0:T(8,128)(2,1)S(1)}, bf16[8,48,640]{2,1,0:T(8,128)(2,1)S(1)}, u32[]{:S(2)}, u32[]{:S(2)}) collective-permute-start(bf16[8,48,640]{2,1,0:T(8,128)(2,1)S(1)} %pad_maximum_fusion.7.pair_a), channel_id=1, source_target_pairs={{0,2},{2,0},{4,6},{6,4},{8,10},{10,8},{12,14},{14,12},{16,18},{18,... | collective-permute-start | bytes 1474568 | tf_op jit(solution)/shard_map/ppermute | solution.py:85
  32.4 17.3 %collective-permute-start.6 = (bf16[8,48,640]{2,1,0:T(8,128)(2,1)S(1)}, bf16[8,48,640]{2,1,0:T(8,128)(2,1)S(1)}, u32[]{:S(2)}, u32[]{:S(2)}) collective-permute-start(bf16[8,48,640]{2,1,0:T(8,128)(2,1)S(1)} %pad_maximum_fusion.8.pair_b), channel_id=1, source_target_pairs={{0,4},{2,6},{4,0},{6,2},{8,12},{10,14},{12,8},{14,10},{16,20},{18,... | collective-permute-start | bytes 1474568 | tf_op jit(solution)/shard_map/ppermute | solution.py:85
  40.5 8.4 %collective-permute-start.11 = (bf16[48,1536]{1,0:T(8,128)(2,1)S(1)}, bf16[48,1536]{1,0:T(8,128)(2,1)S(1)}, u32[]{:S(2)}, u32[]{:S(2)}) collective-permute-start(bf16[48,1536]{1,0:T(8,128)(2,1)S(1)} %pad_maximum_fusion.14), channel_id=1, source_target_pairs={{0,16},{2,18},{4,20},{6,22},{8,24},{10,26},{12,28},{14,30},{16,0},... | collective-permute-start | bytes 442376 | tf_op jit(solution)/shard_map/ppermute | solution.py:85
  49.6 16.1 %collective-permute-start.12 = (bf16[2,48,1536]{2,1,0:T(8,128)(2,1)}, bf16[2,48,1536]{2,1,0:T(8,128)(2,1)}, u32[]{:S(2)}, u32[]{:S(2)}) collective-permute-start(bf16[2,48,1536]{2,1,0:T(8,128)(2,1)} %pad_maximum_fusion.11), channel_id=1, source_target_pairs={{0,8},{2,10},{4,12},{6,14},{8,0},{10,2},{12,4},{14,6},{16,24},{18,... | collective-permute-start | bytes 884744 | tf_op jit(solution)/shard_map/ppermute | solution.py:85
  49.8 20.7 %copy-start.13 = (bf16[768,1280]{1,0:T(8,128)(2,1)}, bf16[768,1280]{1,0:T(8,128)(2,1)S(1)}, u32[]{:S(2)}) copy-start(bf16[768,1280]{1,0:T(8,128)(2,1)S(1)} %place.3.w_ref.refs_3_) | copy-start | bytes 5898244
  49.8 12.2 %collective-permute-start.9 = (bf16[4,48,1024]{2,1,0:T(8,128)(2,1)S(1)}, bf16[4,48,1024]{2,1,0:T(8,128)(2,1)}, u32[]{:S(2)}, u32[]{:S(2)}) collective-permute-start(bf16[4,48,1024]{2,1,0:T(8,128)(2,1)S(1)} %slice.266), channel_id=1, source_target_pairs={{0,4},{2,6},{4,0},{6,2},{8,12},{10,14},{12,8},{14,10},{16,20},{18,... | collective-permute-start | bytes 1179656 | tf_op jit(solution)/shard_map/ppermute | solution.py:85
  51.4 10.6 %collective-permute-start.10 = (bf16[4,48,896]{2,1,0:T(8,128)(2,1)S(1)}, bf16[4,48,896]{2,1,0:T(8,128)(2,1)}, u32[]{:S(2)}, u32[]{:S(2)}) collective-permute-start(bf16[4,48,896]{2,1,0:T(8,128)(2,1)S(1)} %pad_maximum_fusion.10), channel_id=1, source_target_pairs={{0,2},{2,0},{4,6},{6,4},{8,10},{10,8},{12,14},{14,12},{16,18},{18,... | collective-permute-start | bytes 1032200 | tf_op jit(solution)/shard_map/ppermute | solution.py:85
  64.2 24.8 %collective-permute-start.13 = (bf16[8,48,1024]{2,1,0:T(8,128)(2,1)S(1)}, bf16[8,48,1024]{2,1,0:T(8,128)(2,1)S(1)}, u32[]{:S(2)}, u32[]{:S(2)}) collective-permute-start(bf16[8,48,1024]{2,1,0:T(8,128)(2,1)S(1)} %pad_maximum_fusion.pair_a), channel_id=1, source_target_pairs={{0,2},{2,0},{4,6},{6,4},{8,10},{10,8},{12,14},{14,12},{16,18},{18,... | collective-permute-start | bytes 2359304 | tf_op jit(solution)/shard_map/ppermute | solution.py:85
  64.8 24.2 %collective-permute-start.14 = (bf16[8,48,896]{2,1,0:T(8,128)(2,1)S(1)}, bf16[8,48,896]{2,1,0:T(8,128)(2,1)S(1)}, u32[]{:S(2)}, u32[]{:S(2)}) collective-permute-start(bf16[8,48,896]{2,1,0:T(8,128)(2,1)S(1)} %pad_maximum_fusion.2.pair_b), channel_id=1, source_target_pairs={{0,4},{2,6},{4,0},{6,2},{8,12},{10,14},{12,8},{14,10},{16,20},{18,... | collective-permute-start | bytes 2064392 | tf_op jit(solution)/shard_map/ppermute | solution.py:85
  67.8 19.2 %collective-permute-start.15 = (bf16[4,48,768]{2,1,0:T(8,128)(2,1)S(1)}, bf16[4,48,768]{2,1,0:T(8,128)(2,1)S(1)}, u32[]{:S(2)}, u32[]{:S(2)}) collective-permute-start(bf16[4,48,768]{2,1,0:T(8,128)(2,1)S(1)} %get-tuple-element.164), channel_id=1, source_target_pairs={{0,4},{2,6},{4,0},{6,2},{8,12},{10,14},{12,8},{14,10},{16,20},{18,... | collective-permute-start | bytes 884744 | tf_op jit(solution)/shard_map/ppermute | solution.py:85
  69.1 19.9 %collective-permute-start.16 = (bf16[4,48,768]{2,1,0:T(8,128)(2,1)S(1)}, bf16[4,48,768]{2,1,0:T(8,128)(2,1)S(1)}, u32[]{:S(2)}, u32[]{:S(2)}) collective-permute-start(bf16[4,48,768]{2,1,0:T(8,128)(2,1)S(1)} %get-tuple-element.165), channel_id=1, source_target_pairs={{0,2},{2,0},{4,6},{6,4},{8,10},{10,8},{12,14},{14,12},{16,18},{18,... | collective-permute-start | bytes 884744 | tf_op jit(solution)/shard_map/ppermute | solution.py:85
  92.8 4.6 %collective-permute-start.17 = (bf16[1536,768]{1,0:T(8,128)(2,1)S(1)}, bf16[1536,768]{1,0:T(8,128)(2,1)S(1)}, u32[]{:S(2)}, u32[]{:S(2)}) collective-permute-start(bf16[1536,768]{1,0:T(8,128)(2,1)S(1)} %outward.1.mine_ref), channel_id=1, source_target_pairs={{0,1},{1,0},{2,3},{3,2},{4,5},{5,4},{6,7},{7,6},{8,9},{9,8},{10,11... | collective-permute-start | bytes 7077896 | tf_op jit(solution)/shard_map/ppermute | solution.py:89
  92.9 15.7 %collective-permute-start.18 = (bf16[8,48,768]{2,1,0:T(8,128)(2,1)S(1)}, bf16[8,48,768]{2,1,0:T(8,128)(2,1)S(1)}, u32[]{:S(2)}, u32[]{:S(2)}) collective-permute-start(bf16[8,48,768]{2,1,0:T(8,128)(2,1)S(1)} %pad_maximum_fusion.4.pair_a), channel_id=1, source_target_pairs={{0,2},{2,0},{4,6},{6,4},{8,10},{10,8},{12,14},{14,12},{16,18},{18,... | collective-permute-start | bytes 1769480 | tf_op jit(solution)/shard_map/ppermute | solution.py:85
  93.5 15.4 %collective-permute-start.19 = (bf16[8,48,768]{2,1,0:T(8,128)(2,1)S(1)}, bf16[8,48,768]{2,1,0:T(8,128)(2,1)S(1)}, u32[]{:S(2)}, u32[]{:S(2)}) collective-permute-start(bf16[8,48,768]{2,1,0:T(8,128)(2,1)S(1)} %pad_maximum_fusion.5.pair_b), channel_id=1, source_target_pairs={{0,4},{2,6},{4,0},{6,2},{8,12},{10,14},{12,8},{14,10},{16,20},{18,... | collective-permute-start | bytes 1769480 | tf_op jit(solution)/shard_map/ppermute | solution.py:85
  118.2 4.9 %collective-permute-start.20 = (bf16[1536,768]{1,0:T(8,128)(2,1)}, bf16[1536,768]{1,0:T(8,128)(2,1)}, u32[]{:S(2)}, u32[]{:S(2)}) collective-permute-start(bf16[1536,768]{1,0:T(8,128)(2,1)} %get-tuple-element.178.mine_ref), channel_id=1, source_target_pairs={{0,1},{1,0},{2,3},{3,2},{4,5},{5,4},{6,7},{7,6},{8,9},{9,8},{10,11... | collective-permute-start | bytes 7077896 | tf_op jit(solution)/shard_map/ppermute | solution.py:89
  142.4 12.7 %collective-permute-start.21 = (bf16[1536,768]{1,0:T(8,128)(2,1)S(1)}, bf16[1536,768]{1,0:T(8,128)(2,1)S(1)}, u32[]{:S(2)}, u32[]{:S(2)}) collective-permute-start(bf16[1536,768]{1,0:T(8,128)(2,1)S(1)} %get-tuple-element.193.mine_ref), channel_id=1, source_target_pairs={{0,1},{1,0},{2,3},{3,2},{4,5},{5,4},{6,7},{7,6},{8,9},{9,8},{10,11... | collective-permute-start | bytes 7077896 | tf_op jit(solution)/shard_map/ppermute | solution.py:89
  148.6 28.3 %copy-start.9 = (bf16[2,4,48,1536]{3,2,1,0:T(8,128)(2,1)}, bf16[2,4,48,1536]{3,2,1,0:T(8,128)(2,1)S(1)}, u32[]{:S(2)}) copy-start(bf16[2,4,48,1536]{3,2,1,0:T(8,128)(2,1)S(1)} %get-tuple-element.203.refs_0_) | copy-start | bytes 3538948
  148.6 28.3 %collective-permute-start.23 = (bf16[2,4,48,1536]{3,2,1,0:T(8,128)(2,1)S(1)}, bf16[2,4,48,1536]{3,2,1,0:T(8,128)(2,1)S(1)}, u32[]{:S(2)}, u32[]{:S(2)}) collective-permute-start(bf16[2,4,48,1536]{3,2,1,0:T(8,128)(2,1)S(1)} %get-tuple-element.188), channel_id=1, source_target_pairs={{0,2},{2,0},{4,6},{6,4},{8,10},{10,8},{12,14},{14,12},{16,18},{18,... | collective-permute-start | bytes 3538952 | tf_op jit(solution)/shard_map/ppermute | solution.py:85
  154.5 28.9 %copy-start.5 = (bf16[2,4,48,1536]{3,2,1,0:T(8,128)(2,1)}, bf16[2,4,48,1536]{3,2,1,0:T(8,128)(2,1)S(1)}, u32[]{:S(2)}) copy-start(bf16[2,4,48,1536]{3,2,1,0:T(8,128)(2,1)S(1)} %get-tuple-element.202.refs_0_) | copy-start | bytes 3538948
  154.5 28.9 %collective-permute-start.22 = (bf16[2,4,48,1536]{3,2,1,0:T(8,128)(2,1)S(1)}, bf16[2,4,48,1536]{3,2,1,0:T(8,128)(2,1)S(1)}, u32[]{:S(2)}, u32[]{:S(2)}) collective-permute-start(bf16[2,4,48,1536]{3,2,1,0:T(8,128)(2,1)S(1)} %get-tuple-element.192), channel_id=1, source_target_pairs={{0,4},{2,6},{4,0},{6,2},{8,12},{10,14},{12,8},{14,10},{16,20},{18,... | collective-permute-start | bytes 3538952 | tf_op jit(solution)/shard_map/ppermute | solution.py:85
  177.9 18.2 %collective-permute-start.27 = (bf16[4,48,1536]{2,1,0:T(8,128)(2,1)}, bf16[4,48,1536]{2,1,0:T(8,128)(2,1)S(1)}, u32[]{:S(2)}, u32[]{:S(2)}) collective-permute-start(bf16[4,48,1536]{2,1,0:T(8,128)(2,1)} %add_bitcast_fusion.1), channel_id=1, source_target_pairs={{0,4},{2,6},{4,0},{6,2},{8,12},{10,14},{12,8},{14,10},{16,20},{18,... | collective-permute-start | bytes 1769480 | tf_op jit(solution)/shard_map/ppermute | solution.py:85
  184.6 23.5 %collective-permute-start.26 = (bf16[4,48,1536]{2,1,0:T(8,128)(2,1)}, bf16[4,48,1536]{2,1,0:T(8,128)(2,1)}, u32[]{:S(2)}, u32[]{:S(2)}) collective-permute-start(bf16[4,48,1536]{2,1,0:T(8,128)(2,1)} %add_bitcast_fusion), channel_id=1, source_target_pairs={{0,2},{2,0},{4,6},{6,4},{8,10},{10,8},{12,14},{14,12},{16,18},{18,... | collective-permute-start | bytes 1769480 | tf_op jit(solution)/shard_map/ppermute | solution.py:85
  186.1 22.0 %collective-permute-start.25 = (bf16[2,4,48,384]{3,2,1,0:T(8,128)(2,1)}, bf16[2,4,48,384]{3,2,1,0:T(8,128)(2,1)S(1)}, u32[]{:S(2)}, u32[]{:S(2)}) collective-permute-start(bf16[2,4,48,384]{3,2,1,0:T(8,128)(2,1)} %get-tuple-element.206), channel_id=1, source_target_pairs={{0,4},{2,6},{4,0},{6,2},{8,12},{10,14},{12,8},{14,10},{16,20},{18,... | collective-permute-start | bytes 884744 | tf_op jit(solution)/shard_map/ppermute | solution.py:85
  187.3 20.9 %collective-permute-start.24 = (bf16[2,4,48,384]{3,2,1,0:T(8,128)(2,1)}, bf16[2,4,48,384]{3,2,1,0:T(8,128)(2,1)S(1)}, u32[]{:S(2)}, u32[]{:S(2)}) collective-permute-start(bf16[2,4,48,384]{3,2,1,0:T(8,128)(2,1)} %get-tuple-element.197), channel_id=1, source_target_pairs={{0,2},{2,0},{4,6},{6,4},{8,10},{10,8},{12,14},{14,12},{16,18},{18,... | collective-permute-start | bytes 884744 | tf_op jit(solution)/shard_map/ppermute | solution.py:85
  196.9 22.2 %collective-permute-start.28 = (bf16[2,48,1536]{2,1,0:T(8,128)(2,1)}, bf16[2,48,1536]{2,1,0:T(8,128)(2,1)}, u32[]{:S(2)}, u32[]{:S(2)}) collective-permute-start(bf16[2,48,1536]{2,1,0:T(8,128)(2,1)} %get-tuple-element.213), channel_id=1, source_target_pairs={{0,8},{2,10},{4,12},{6,14},{8,0},{10,2},{12,4},{14,6},{16,24},{18,... | collective-permute-start | bytes 884744 | tf_op jit(solution)/shard_map/ppermute | solution.py:85
  201.0 33.3 %collective-permute-start.33 = (bf16[2,4,48,384]{3,2,1,0:T(8,128)(2,1)}, bf16[2,4,48,384]{3,2,1,0:T(8,128)(2,1)}, u32[]{:S(2)}, u32[]{:S(2)}) collective-permute-start(bf16[2,4,48,384]{3,2,1,0:T(8,128)(2,1)} %get-tuple-element.215), channel_id=1, source_target_pairs={{0,2},{2,0},{4,6},{6,4},{8,10},{10,8},{12,14},{14,12},{16,18},{18,... | collective-permute-start | bytes 884744 | tf_op jit(solution)/shard_map/ppermute | solution.py:85
  218.1 16.1 %collective-permute-start.30 = (bf16[2,48,1536]{2,1,0:T(8,128)(2,1)}, bf16[2,48,1536]{2,1,0:T(8,128)(2,1)S(1)}, u32[]{:S(2)}, u32[]{:S(2)}) collective-permute-start(bf16[2,48,1536]{2,1,0:T(8,128)(2,1)} %get-tuple-element.226), channel_id=1, source_target_pairs={{0,8},{2,10},{4,12},{6,14},{8,0},{10,2},{12,4},{14,6},{16,24},{18,... | collective-permute-start | bytes 884744 | tf_op jit(solution)/shard_map/ppermute | solution.py:85
  222.4 11.9 %collective-permute-start.34 = (bf16[2,4,48,512]{3,2,1,0:T(8,128)(2,1)S(1)}, bf16[2,4,48,512]{3,2,1,0:T(8,128)(2,1)S(1)}, u32[]{:S(2)}, u32[]{:S(2)}) collective-permute-start(bf16[2,4,48,512]{3,2,1,0:T(8,128)(2,1)S(1)} %get-tuple-element.236), channel_id=1, source_target_pairs={{0,4},{2,6},{4,0},{6,2},{8,12},{10,14},{12,8},{14,10},{16,20},{18,... | collective-permute-start | bytes 1179656 | tf_op jit(solution)/shard_map/ppermute | solution.py:85
  224.1 9.9 %collective-permute-start.31 = (bf16[4,48,384]{2,1,0:T(8,128)(2,1)}, bf16[4,48,384]{2,1,0:T(8,128)(2,1)S(1)}, u32[]{:S(2)}, u32[]{:S(2)}) collective-permute-start(bf16[4,48,384]{2,1,0:T(8,128)(2,1)} %add_bitcast_fusion.5), channel_id=1, source_target_pairs={{0,4},{2,6},{4,0},{6,2},{8,12},{10,14},{12,8},{14,10},{16,20},{18,... | collective-permute-start | bytes 442376 | tf_op jit(solution)/shard_map/ppermute | solution.py:85
  225.6 8.5 %collective-permute-start.32 = (bf16[4,48,384]{2,1,0:T(8,128)(2,1)}, bf16[4,48,384]{2,1,0:T(8,128)(2,1)S(1)}, u32[]{:S(2)}, u32[]{:S(2)}) collective-permute-start(bf16[4,48,384]{2,1,0:T(8,128)(2,1)} %add_bitcast_fusion.4), channel_id=1, source_target_pairs={{0,2},{2,0},{4,6},{6,4},{8,10},{10,8},{12,14},{14,12},{16,18},{18,... | collective-permute-start | bytes 442376 | tf_op jit(solution)/shard_map/ppermute | solution.py:85
  234.0 21.8 %collective-permute-start.29 = (bf16[1536,768]{1,0:T(8,128)(2,1)S(1)}, bf16[1536,768]{1,0:T(8,128)(2,1)S(1)}, u32[]{:S(2)}, u32[]{:S(2)}) collective-permute-start(bf16[1536,768]{1,0:T(8,128)(2,1)S(1)} %source.1.mine_ref), channel_id=1, source_target_pairs={{0,1},{1,0},{2,3},{3,2},{4,5},{5,4},{6,7},{7,6},{8,9},{9,8},{10,11... | collective-permute-start | bytes 7077896 | tf_op jit(solution)/shard_map/ppermute | solution.py:89
  234.0 10.9 %collective-permute-start.38 = (bf16[48,1536]{1,0:T(8,128)(2,1)S(1)}, bf16[48,1536]{1,0:T(8,128)(2,1)S(1)}, u32[]{:S(2)}, u32[]{:S(2)}) collective-permute-start(bf16[48,1536]{1,0:T(8,128)(2,1)S(1)} %copy-done.58), channel_id=1, source_target_pairs={{0,16},{2,18},{4,20},{6,22},{8,24},{10,26},{12,28},{14,30},{16,0},... | collective-permute-start | bytes 442376 | tf_op jit(solution)/shard_map/ppermute | solution.py:85
  234.4 18.4 %copy-start.49 = (f32[48,1536]{1,0:T(8,128)S(1)}, f32[48,1536]{1,0:T(8,128)}, u32[]{:S(2)}) copy-start(f32[48,1536]{1,0:T(8,128)} %param.33) | copy-start | bytes 884740
  234.4 18.4 %copy-start.54 = (f32[48,1536]{1,0:T(8,128)S(1)}, f32[48,1536]{1,0:T(8,128)}, u32[]{:S(2)}) copy-start(f32[48,1536]{1,0:T(8,128)} %param.47) | copy-start | bytes 884740
  234.4 11.4 %collective-permute-start.37 = (bf16[2,48,768]{2,1,0:T(8,128)(2,1)S(1)}, bf16[2,48,768]{2,1,0:T(8,128)(2,1)S(1)}, u32[]{:S(2)}, u32[]{:S(2)}) collective-permute-start(bf16[2,48,768]{2,1,0:T(8,128)(2,1)S(1)} %get-tuple-element.245), channel_id=1, source_target_pairs={{0,8},{2,10},{4,12},{6,14},{8,0},{10,2},{12,4},{14,6},{16,24},{18,... | collective-permute-start | bytes 442376 | tf_op jit(solution)/shard_map/ppermute | solution.py:85
  236.1 16.8 %collective-permute-start.42 = (bf16[48,1536]{1,0:T(8,128)(2,1)S(1)}, bf16[48,1536]{1,0:T(8,128)(2,1)S(1)}, u32[]{:S(2)}, u32[]{:S(2)}) collective-permute-start(bf16[48,1536]{1,0:T(8,128)(2,1)S(1)} %fusion.5), channel_id=1, source_target_pairs={{0,16},{2,18},{4,20},{6,22},{8,24},{10,26},{12,28},{14,30},{16,0},... | collective-permute-start | bytes 442376 | tf_op jit(solution)/shard_map/ppermute | solution.py:85
  240.0 13.9 %collective-permute-start.36 = (bf16[4,48,512]{2,1,0:T(8,128)(2,1)S(1)}, bf16[4,48,512]{2,1,0:T(8,128)(2,1)S(1)}, u32[]{:S(2)}, u32[]{:S(2)}) collective-permute-start(bf16[4,48,512]{2,1,0:T(8,128)(2,1)S(1)} %add_bitcast_fusion.2), channel_id=1, source_target_pairs={{0,2},{2,0},{4,6},{6,4},{8,10},{10,8},{12,14},{14,12},{16,18},{18,... | collective-permute-start | bytes 589832 | tf_op jit(solution)/shard_map/ppermute | solution.py:85
  245.0 9.0 %collective-permute-start.35 = (bf16[4,48,384]{2,1,0:T(8,128)(2,1)S(1)}, bf16[4,48,384]{2,1,0:T(8,128)(2,1)S(1)}, u32[]{:S(2)}, u32[]{:S(2)}) collective-permute-start(bf16[4,48,384]{2,1,0:T(8,128)(2,1)S(1)} %add_bitcast_fusion.3), channel_id=1, source_target_pairs={{0,4},{2,6},{4,0},{6,2},{8,12},{10,14},{12,8},{14,10},{16,20},{18,... | collective-permute-start | bytes 442376 | tf_op jit(solution)/shard_map/ppermute | solution.py:85
  245.8 9.2 %collective-permute-start.39 = (bf16[48,768]{1,0:T(8,128)(2,1)S(1)}, bf16[48,768]{1,0:T(8,128)(2,1)S(1)}, u32[]{:S(2)}, u32[]{:S(2)}) collective-permute-start(bf16[48,768]{1,0:T(8,128)(2,1)S(1)} %fusion.9), channel_id=1, source_target_pairs={{0,16},{2,18},{4,20},{6,22},{8,24},{10,26},{12,28},{14,30},{16,0},... | collective-permute-start | bytes 221192 | tf_op jit(solution)/shard_map/ppermute | solution.py:85
  255.0 6.2 %collective-permute-start.40 = (bf16[2,48,896]{2,1,0:T(8,128)(2,1)S(1)}, bf16[2,48,896]{2,1,0:T(8,128)(2,1)S(1)}, u32[]{:S(2)}, u32[]{:S(2)}) collective-permute-start(bf16[2,48,896]{2,1,0:T(8,128)(2,1)S(1)} %get-tuple-element.257), channel_id=1, source_target_pairs={{0,8},{2,10},{4,12},{6,14},{8,0},{10,2},{12,4},{14,6},{16,24},{18,... | collective-permute-start | bytes 516104 | tf_op jit(solution)/shard_map/ppermute | solution.py:85
  261.2 5.6 %collective-permute-start.41 = (bf16[48,896]{1,0:T(8,128)(2,1)S(1)}, bf16[48,896]{1,0:T(8,128)(2,1)S(1)}, u32[]{:S(2)}, u32[]{:S(2)}) collective-permute-start(bf16[48,896]{1,0:T(8,128)(2,1)S(1)} %fusion.7), channel_id=1, source_target_pairs={{0,16},{2,18},{4,20},{6,22},{8,24},{10,26},{12,28},{14,30},{16,0},... | collective-permute-start | bytes 258056 | tf_op jit(solution)/shard_map/ppermute | solution.py:85
  (67 other events, 521.1 us)

commit v3 on v2

--- a/solution.py
+++ b/solution.py
@@ -215,6 +215,26 @@
         compiler_params=params(16),
         cost_estimate=cost(3 * layers * rows * width, 8 * layers * rows * width),
         name="combine",
+    )(*flat)
+
+
+def advance_kernel(kept_a, got_a, kept_b, got_b, out_a, out_b):
+    out_a[...] = (kept_a[0].astype(full) + got_a[0].astype(full)).astype(low)
+    out_b[...] = (kept_b[0].astype(full) + got_b[0].astype(full)).astype(low)
+
+
+def advance(kept_a, got_a, kept_b, got_b):
+    flat = (kept_a, got_a, kept_b, got_b)
+    pieces = (kept_a.shape[1:], kept_b.shape[1:])
+    return pl.pallas_call(
+        advance_kernel,
+        out_shape=tuple(shape(piece, low) for piece in pieces),
+        grid=(1,),
+        in_specs=[pl.BlockSpec((1,) + part.shape[1:], lambda i: (1, 0, 0, 0)) for part in flat],
+        out_specs=tuple(pl.BlockSpec(piece, lambda i: (0, 0, 0)) for piece in pieces),
+        compiler_params=params(),
+        cost_estimate=cost(kept_a.size + kept_b.size, 3 * (kept_a.size + kept_b.size)),
+        name="advance",
     )(*flat)
 
 
@@ -930,7 +950,7 @@
             jnp.concatenate(head_sums, axis=1).reshape(rows, size).T.reshape(1, D),
         )
         got_out, got_0, more_up = after_all((got_out, got_0, more_up), stacked[2])
-        next_out, next_0 = after_all((kept_out[1] + got_out[1], kept_0[1] + got_0[1]))
+        next_out, next_0 = advance(kept_out, got_out, kept_0, got_0)
         more_out, more_0 = hop(next_out, 2, size), hop(next_0, 1, size)
         own_up, out_up = combine([(kept_up, got_up, after(more_up, next_out, next_0))])
         near_up = hop(out_up, 4, size)
@@ -951,7 +971,7 @@
         next_far = far_half(own_up, after(near_up, out_near))
         far_up = hop(next_far, 8, size)
         got_1, got_2 = after_all((got_1, got_2), next_far)
-        next_1, next_2 = after_all((kept_1[1] + got_1[1], kept_2[1] + got_2[1]))
+        next_1, next_2 = advance(kept_1, got_1, kept_2, got_2)
         more_1, more_2 = hop(next_1, 2, size), hop(next_2, 1, size)
         near_near, far_down = after_all((near_near, far_down), next_1, next_2)
         next_far = far_half(own_near, near_near)

time: 273 us -> 285 us (1.044)
  local copies, waits for them, and re-layouts: 22.2 us -> 34.5 us
  waiting for transfers between devices: 52.9 us -> 45.3 us
  Pallas kernels: 126 us -> 133 us
    unnamed x148 -> x158, local copies, waits for them, and re-layouts: 13.8 us -> 22.1 us
    ppermute x39, waiting for transfers between devices: 45.1 us -> 37.4 us  [hop(): return lax.ppermute(value, 'dp', [(d, d ^ offset) for d in range(size)])]
    add x4 -> x0, other arithmetic: 3.4 us -> none  [the longest x1 1.67 us: per_device(): kept_out[1] + got_out[1]]
  transfers between devices with their start and end apart: 43 -> 43, of which waited for: 18 -> 15; matrix products, arithmetic and copies ran while one was open for 10% -> 11% of each run, Pallas kernels for 35% -> 36%
where the time goes in v3:
time: 285 us; the launch traced here: 283 us
  Pallas kernels  133 us (47%)
  waiting for transfers between devices  45.3 us (16%)
  starting transfers between devices  44.2 us (16%)
  local copies, waits for them, and re-layouts  34.5 us (12%)
  other arithmetic  24.2 us (8%)
    ppermute x39, starting transfers between devices, hop(): return lax.ppermute(value, 'dp', [(d, d ^ offset) for d in range(size)])  43.9 us
    ppermute x39, waiting for transfers between devices, hop(): return lax.ppermute(value, 'dp', [(d, d ^ offset) for d in range(size)])  37.4 us
    pallas_call x2, Pallas kernels, attend(): pl.pallas_call(attend_kernel, out_shape=(main((rows, groups * width), low...  22.6 us
    unnamed x158, local copies, waits for them, and re-layouts  22.1 us
    pallas_call x3, Pallas kernels, attend_back(): pl.pallas_call(attend_back_kernel, out_shape=(main((rows, width), low), s...  20.4 us
    pallas_call x6, Pallas kernels, weight_grad(): pl.pallas_call(partial(weight_grad_kernel, bit, len(rights), turned, len(...  18.7 us
    pallas_call x1, Pallas kernels, contract(): pl.pallas_call(contract_kernel, out_shape=(shape((rows, D), low), shape((...  17.9 us
    pallas_call x1, Pallas kernels, expand_first(): pl.pallas_call(expand_first_kernel, out_shape=(main((rows, D), full), mai...  10 us
  transfers between devices with their start and end apart: 43, of which 15 were waited for; matrix products, arithmetic and copies ran while one was open for 11% of the time, Pallas kernels for 36%

profile of v3, /device:TPU:0, one launch (start us, length us, event | category | flops | bytes accessed | tf_op | source)
XLA Modules:
  0.0 283.3 jit_solution(15621978753752685025)
XLA Ops:
  4.5 3.1 %collective-permute-start = (bf16[48,1280]{1,0:T(8,128)(2,1)S(1)}, bf16[48,1280]{1,0:T(8,128)(2,1)S(1)}, u32[]{:S(2)}, u32[]{:S(2)}) collective-permute-start(bf16[48,1280]{1,0:T(8,128)(2,1)S(1)} %fusion.6), channel_id=1, source_target_pairs={{0,8},{2,10},{4,12},{6,14},{8,0},{10,2},{12,4},{14,6},{16,24},{18,... | collective-permute-start | bytes 368648 | tf_op jit(solution)/shard_map/ppermute | solution.py:85
  7.6 2.6 collective-permute-start.1
  15.6 4.3 %collective-permute-done.1 = bf16[48,1280]{1,0:T(8,128)(2,1)S(1)} collective-permute-done((bf16[48,1280]{1,0:T(8,128)(2,1)S(1)}, bf16[48,1280]{1,0:T(8,128)(2,1)S(1)}, u32[]{:S(2)}, u32[]{:S(2)}) %collective-permute-start.1) | collective-permute-done | bytes 122912 | tf_op jit(solution)/shard_map/ppermute | solution.py:85
  20.0 3.1 %collective-permute-start.7 = (bf16[48,1920]{1,0:T(8,128)(2,1)S(1)}, bf16[48,1920]{1,0:T(8,128)(2,1)S(1)}, u32[]{:S(2)}, u32[]{:S(2)}) collective-permute-start(bf16[48,1920]{1,0:T(8,128)(2,1)S(1)} %pad_maximum_fusion.13), channel_id=1, source_target_pairs={{0,16},{2,18},{4,20},{6,22},{8,24},{10,26},{12,28},{14,30},{16,0},... | collective-permute-start | bytes 552968 | tf_op jit(solution)/shard_map/ppermute | solution.py:85
  23.1 1.6 collective-permute-start.4
  24.7 1.5 collective-permute-start.3
  26.2 4.3 %collective-permute-done.7 = bf16[48,1920]{1,0:T(8,128)(2,1)S(1)} collective-permute-done((bf16[48,1920]{1,0:T(8,128)(2,1)S(1)}, bf16[48,1920]{1,0:T(8,128)(2,1)S(1)}, u32[]{:S(2)}, u32[]{:S(2)}) %collective-permute-start.7) | collective-permute-done | bytes 184352 | tf_op jit(solution)/shard_map/ppermute | solution.py:85
  32.4 1.5 collective-permute-start.6
  33.9 6.6 %collective-permute-done.8 = bf16[2,48,1920]{2,1,0:T(8,128)(2,1)S(1)} collective-permute-done((bf16[2,48,1920]{2,1,0:T(8,128)(2,1)S(1)}, bf16[2,48,1920]{2,1,0:T(8,128)(2,1)S(1)}, u32[]{:S(2)}, u32[]{:S(2)}) %collective-permute-start.8) | collective-permute-done | bytes 368672 | tf_op jit(solution)/shard_map/ppermute | solution.py:85
  40.8 8.1 %collective-permute-done.11 = bf16[48,1536]{1,0:T(8,128)(2,1)S(1)} collective-permute-done((bf16[48,1536]{1,0:T(8,128)(2,1)S(1)}, bf16[48,1536]{1,0:T(8,128)(2,1)S(1)}, u32[]{:S(2)}, u32[]{:S(2)}) %collective-permute-start.11) | collective-permute-done | bytes 147488 | tf_op jit(solution)/shard_map/ppermute | solution.py:85
  49.8 1.6 collective-permute-start.9
  53.4 8.2 %attend.2 = (bf16[1536,384]{1,0:T(8,128)(2,1)}, bf16[3,2,512,512]{3,2,1,0:T(8,128)(2,1)}, bf16[1536,128]{1,0:T(8,128)(2,1)}) custom-call(s32[3]{0:T(128)S(1)} %copy-done.41, bf16[1536,768]{1,0:T(8,128)(2,1)} %x_ref.4, bf16[768,1280]{1,0:T(8,128)(2,1)S(1)} %place.3.w_ref.refs_3_, f32[2,384]{1,0:T(2,128)S(1)} %reshape.230.bias_ref), custom_call_target="tpu_custom_call" | custom-call | flops 1711276032 | bytes 3145728 | tf_op jit(solution)/shard_map/attend/pallas_call | solution.py:279
  70.6 14.4 %attend.3 = (bf16[1536,768]{1,0:T(8,128)(2,1)}, bf16[6,2,512,512]{3,2,1,0:T(8,128)(2,1)}, bf16[1536,256]{1,0:T(8,128)(2,1)}) custom-call(s32[3]{0:T(128)S(1)} %copy-done.41, bf16[1536,768]{1,0:T(8,128)(2,1)} %x_ref.4, bf16[768,1280]{1,0:T(8,128)(2,1)S(1)} %place.3.w_ref.refs_3_, f32[2,384]{1,0:T(2,128)S(1)} %reshape.230.bias_ref), custom_call_target="tpu_custom_call" | custom-call | flops 3422552064 | bytes 6291456 | tf_op jit(solution)/shard_map/attend/pallas_call | solution.py:279
  85.0 2.1 collective-permute-done.15
  87.1 1.8 collective-permute-done.16
  89.3 3.5 %outward.1.mine_ref = bf16[1536,768]{1,0:T(8,128)(2,1)S(1)} custom-call(bf16[1536,128]{1,0:T(8,128)(2,1)} %get-tuple-element.156.refs_0_, bf16[1536,256]{1,0:T(8,128)(2,1)} %get-tuple-element.167.refs_1_, bf16[768,1920]{1,0:T(8,128)(2,1)S(1)} %place.4.refs_2_.up_ref.down_ref.up_first.down_first.w_ref), custom_call_target="tpu_custom_call" | custom-call | flops 905969664 | bytes 4128768 | tf_op jit(solution)/shard_map/outward/pallas_call | solution.py:388
  94.1 3.4 %collective-permute-done.17.other_ref = bf16[1536,768]{1,0:T(8,128)(2,1)S(1)} collective-permute-done((bf16[1536,768]{1,0:T(8,128)(2,1)S(1)}, bf16[1536,768]{1,0:T(8,128)(2,1)S(1)}, u32[]{:S(2)}, u32[]{:S(2)}) %collective-permute-start.17) | collective-permute-done | bytes 2359328 | tf_op jit(solution)/shard_map/ppermute | solution.py:89
  97.5 10.0 %expand_first.1 = (f32[1536,768]{1,0:T(8,128)}, bf16[1536,768]{1,0:T(8,128)(2,1)}, bf16[1536,768]{1,0:T(8,128)(2,1)}, bf16[1536,768]{1,0:T(8,128)(2,1)}, f32[1536,768]{1,0:T(8,128)}, /*index=5*/f32[1536,1]{1,0:T(8,128)}) custom-call(bf16[1536,768]{1,0:T(8,128)(2,1)S(1)} %outward.1.mine_ref, bf16[1536,768]{1,0:T(8,128)(2,1)S(1)} %collective-permute-done.17.other_ref, ...), custom_call_target="tpu_custom_call" | custom-call | flops 3623878656 | bytes 21233664 | tf_op jit(solution)/shard_map/expand_first/pallas_call | solution.py:431
  109.1 9.1 %expand_last.1 = (bf16[1536,768]{1,0:T(8,128)(2,1)}, bf16[1536,768]{1,0:T(8,128)(2,1)}, bf16[1536,768]{1,0:T(8,128)(2,1)}) custom-call(f32[1536,768]{1,0:T(8,128)} %get-tuple-element.174.total_ref, bf16[1536,768]{1,0:T(8,128)(2,1)} %get-tuple-element.189.middle_ref.left_ref, f32[1,1536]{1,0:T(1,128)S(1)} %reshape.233.bias_ref, ...), custom_call_target="tpu_custom_call" | custom-call | flops 3623878656 | bytes 14155776 | tf_op jit(solution)/shard_map/expand_last/pallas_call | solution.py:473
  118.7 4.5 %collective-permute-done.20.other_ref = bf16[1536,768]{1,0:T(8,128)(2,1)} collective-permute-done((bf16[1536,768]{1,0:T(8,128)(2,1)}, bf16[1536,768]{1,0:T(8,128)(2,1)}, u32[]{:S(2)}, u32[]{:S(2)}) %collective-permute-start.20) | collective-permute-done | bytes 2359328 | tf_op jit(solution)/shard_map/ppermute | solution.py:89
  123.2 1.7 copy-done.3
  124.9 17.9 %contract.1 = (bf16[1536,768]{1,0:T(8,128)(2,1)}, f32[3,768]{1,0:T(4,128)S(1)}, f32[1,1536]{1,0:T(1,128)S(1)}, bf16[1536,768]{1,0:T(8,128)(2,1)}, f32[1536,768]{...) custom-call(bf16[1536,768]{1,0:T(8,128)(2,1)} %get-tuple-element.178.mine_ref, ...), custom_call_target="tpu_custom_call" | custom-call | flops 7247757312 | bytes 14155776 | tf_op jit(solution)/shard_map/contract/pallas_call | solution.py:533
  143.0 1.7 copy-done.44
  144.6 5.3 %weight_grad.6 = (bf16[2,4,48,1536]{3,2,1,0:T(8,128)(2,1)}, bf16[2,4,48,1536]{3,2,1,0:T(8,128)(2,1)S(1)}) custom-call(s32[1]{0:T(128)} %bitcast.me_ref, bf16[1536,768]{1,0:T(8,128)(2,1)S(1)} %copy-done.44, bf16[1536,768]{1,0:T(8,128)(2,1)S(1)} %copy-done.50, bf16[1536,768]{1,0:T(8,128)(2,1)S(1)} %copy-done.51), custom_call_target="tpu_custom_call" | custom-call | flops 3623878656 | bytes 7077888 | tf_op jit(solution)/shard_map/weight_grad/pallas_call | solution.py:746
  152.5 5.3 %weight_grad.7 = (bf16[2,4,48,1536]{3,2,1,0:T(8,128)(2,1)}, bf16[2,4,48,1536]{3,2,1,0:T(8,128)(2,1)S(1)}) custom-call(s32[1]{0:T(128)} %bitcast.me_ref, bf16[1536,768]{1,0:T(8,128)(2,1)S(1)} %copy-done.49, bf16[1536,768]{1,0:T(8,128)(2,1)S(1)} %copy-done.42, bf16[1536,768]{1,0:T(8,128)(2,1)S(1)} %copy-done.43), custom_call_target="tpu_custom_call" | custom-call | flops 3623878656 | bytes 7077888 | tf_op jit(solution)/shard_map/weight_grad/pallas_call | solution.py:746
  161.5 10.0 %first_back.1 = (f32[3,768]{1,0:T(4,128)S(1)}, f32[1536,768]{1,0:T(8,128)}, bf16[1536,768]{1,0:T(8,128)(2,1)}, bf16[1536,384]{1,0:T(8,128)(2,1)}) custom-call(bf16[1536,768]{1,0:T(8,128)(2,1)} %get-tuple-element.193.mine_ref, bf16[1536,768]{1,0:T(8,128)(2,1)} %collective-permute-done.21.other_ref, f32[1536,768]{1,0:T(8,128)} %get-tuple-element.194.second_ref, ...), custom_call_target="tpu_custom_call" | custom-call | flops 905969664 | bytes 23592960 | tf_op jit(solution)/shard_map/first_back/pallas_call | solution.py:599
  172.1 1.7 copy-done.13
  173.8 1.7 weight_grad.8
  175.5 7.1 %attend_back.3 = (bf16[1536,384]{1,0:T(8,128)(2,1)}, f32[2,128]{1,0:T(2,128)S(1)}) custom-call(bf16[1536,384]{1,0:T(8,128)(2,1)} %get-tuple-element.198.qkv_ref, bf16[3,2,512,512]{3,2,1,0:T(8,128)(2,1)} %get-tuple-element.199.weight_ref, bf16[1536,384]{1,0:T(8,128)(2,1)} %get-tuple-element.200.grad_ref), custom_call_target="tpu_custom_call" | custom-call | flops 1610612736 | bytes 5505024 | tf_op jit(solution)/shard_map/attend_back/pallas_call | solution.py:350
  182.7 2.1 add_bitcast_fusion.1
  187.5 1.6 weight_grad.9
  190.6 2.0 add_bitcast_fusion
  200.2 6.7 %attend_back.4 = (bf16[1536,384]{1,0:T(8,128)(2,1)}, f32[2,128]{1,0:T(2,128)S(1)}) custom-call(bf16[1536,768]{1,0:T(8,128)(2,1)} %get-tuple-element.216.qkv_ref, bf16[6,2,512,512]{3,2,1,0:T(8,128)(2,1)} %get-tuple-element.210.weight_ref, bf16[1536,384]{1,0:T(8,128)(2,1)} %get-tuple-element.200.grad_ref), custom_call_target="tpu_custom_call" | custom-call | flops 1610612736 | bytes 5505024 | tf_op jit(solution)/shard_map/attend_back/pallas_call | solution.py:350
  206.8 2.2 combine.4
  209.0 1.7 collective-permute-start.28
  210.7 2.3 weight_grad.10
  213.6 6.6 %attend_back.5 = (bf16[1536,384]{1,0:T(8,128)(2,1)}, f32[2,128]{1,0:T(2,128)S(1)}) custom-call(bf16[1536,768]{1,0:T(8,128)(2,1)} %get-tuple-element.216.qkv_ref, bf16[6,2,512,512]{3,2,1,0:T(8,128)(2,1)} %get-tuple-element.210.weight_ref, bf16[1536,384]{1,0:T(8,128)(2,1)} %get-tuple-element.200.grad_ref), custom_call_target="tpu_custom_call" | custom-call | flops 1610612736 | bytes 5505024 | tf_op jit(solution)/shard_map/attend_back/pallas_call | solution.py:350
  225.2 1.6 collective-permute-start.31
  228.2 2.1 combine.5
  230.6 2.0 fusion.4
  232.6 2.4 weight_grad.11
  235.5 5.6 %source.1.mine_ref = bf16[1536,768]{1,0:T(8,128)(2,1)S(1)} custom-call(bf16[1536,384]{1,0:T(8,128)(2,1)} %get-tuple-element.237.refs_0_, bf16[1536,384]{1,0:T(8,128)(2,1)} %get-tuple-element.211.refs_0_.refs_1_, bf16[1536,384]{1,0:T(8,128)(2,1)} %get-tuple-element.217.refs_0_.refs_2_, bf16[768,1280]{1,0:T(8,128)(2,1)S(1)} %copy-done.11), custom_call_target="tpu_custom_call" | custom-call | flops 2717908992 | bytes 5308416 | tf_op jit(solution)/shard_map/source/pallas_call | solution.py:634
  257.8 2.0 multiply_subtract_fusion
  259.8 3.3 %collective-permute-done.42 = bf16[48,1536]{1,0:T(8,128)(2,1)S(1)} collective-permute-done((bf16[48,1536]{1,0:T(8,128)(2,1)S(1)}, bf16[48,1536]{1,0:T(8,128)(2,1)S(1)}, u32[]{:S(2)}, u32[]{:S(2)}) %collective-permute-start.42) | collective-permute-done | bytes 147488 | tf_op jit(solution)/shard_map/ppermute | solution.py:85
  263.2 2.0 multiply_subtract_fusion.1
  267.2 5.8 %finish.1 = f32[1536,768]{1,0:T(8,128)} custom-call(bf16[1536,768]{1,0:T(8,128)(2,1)S(1)} %source.1.mine_ref, bf16[1536,768]{1,0:T(8,128)(2,1)} %collective-permute-done.29.other_ref, f32[1536,768]{1,0:T(8,128)} %get-tuple-element.259.first_ref), custom_call_target="tpu_custom_call" | custom-call | flops 2359296 | bytes 14155776 | tf_op jit(solution)/shard_map/finish/pallas_call | solution.py:652
  273.0 3.1 %collective-permute-start.41 = (bf16[48,896]{1,0:T(8,128)(2,1)S(1)}, bf16[48,896]{1,0:T(8,128)(2,1)S(1)}, u32[]{:S(2)}, u32[]{:S(2)}) collective-permute-start(bf16[48,896]{1,0:T(8,128)(2,1)S(1)} %fusion.7), channel_id=1, source_target_pairs={{0,16},{2,18},{4,20},{6,22},{8,24},{10,26},{12,28},{14,30},{16,0},... | collective-permute-start | bytes 258056 | tf_op jit(solution)/shard_map/ppermute | solution.py:85
  276.1 2.5 collective-permute-done.41
  (314 shorter events, 75.7 us)
Async XLA Ops:
  4.5 11.1 %collective-permute-start = (bf16[48,1280]{1,0:T(8,128)(2,1)S(1)}, bf16[48,1280]{1,0:T(8,128)(2,1)S(1)}, u32[]{:S(2)}, u32[]{:S(2)}) collective-permute-start(bf16[48,1280]{1,0:T(8,128)(2,1)S(1)} %fusion.6), channel_id=1, source_target_pairs={{0,8},{2,10},{4,12},{6,14},{8,0},{10,2},{12,4},{14,6},{16,24},{18,... | collective-permute-start | bytes 368648 | tf_op jit(solution)/shard_map/ppermute | solution.py:85
  7.6 12.3 %collective-permute-start.1 = (bf16[48,1280]{1,0:T(8,128)(2,1)S(1)}, bf16[48,1280]{1,0:T(8,128)(2,1)S(1)}, u32[]{:S(2)}, u32[]{:S(2)}) collective-permute-start(bf16[48,1280]{1,0:T(8,128)(2,1)S(1)} %fusion.6), channel_id=1, source_target_pairs={{0,16},{2,18},{4,20},{6,22},{8,24},{10,26},{12,28},{14,30},{16,0},... | collective-permute-start | bytes 368648 | tf_op jit(solution)/shard_map/ppermute | solution.py:85
  10.2 9.7 %collective-permute-start.2 = (bf16[48,1280]{1,0:T(8,128)(2,1)S(1)}, bf16[48,1280]{1,0:T(8,128)(2,1)S(1)}, u32[]{:S(2)}, u32[]{:S(2)}) collective-permute-start(bf16[48,1280]{1,0:T(8,128)(2,1)S(1)} %fusion.6), channel_id=1, source_target_pairs={{0,24},{2,26},{4,28},{6,30},{8,16},{10,18},{12,20},{14,22},{16,8},... | collective-permute-start | bytes 368648 | tf_op jit(solution)/shard_map/ppermute | solution.py:85
  20.0 10.6 %collective-permute-start.7 = (bf16[48,1920]{1,0:T(8,128)(2,1)S(1)}, bf16[48,1920]{1,0:T(8,128)(2,1)S(1)}, u32[]{:S(2)}, u32[]{:S(2)}) collective-permute-start(bf16[48,1920]{1,0:T(8,128)(2,1)S(1)} %pad_maximum_fusion.13), channel_id=1, source_target_pairs={{0,16},{2,18},{4,20},{6,22},{8,24},{10,26},{12,28},{14,30},{16,0},... | collective-permute-start | bytes 552968 | tf_op jit(solution)/shard_map/ppermute | solution.py:85
  23.1 7.5 %collective-permute-start.4 = (bf16[4,48,640]{2,1,0:T(8,128)(2,1)S(1)}, bf16[4,48,640]{2,1,0:T(8,128)(2,1)S(1)}, u32[]{:S(2)}, u32[]{:S(2)}) collective-permute-start(bf16[4,48,640]{2,1,0:T(8,128)(2,1)S(1)} %get-tuple-element.145), channel_id=1, source_target_pairs={{0,2},{2,0},{4,6},{6,4},{8,10},{10,8},{12,14},{14,12},{16,18},{18,... | collective-permute-start | bytes 737288 | tf_op jit(solution)/shard_map/ppermute | solution.py:85
  24.7 6.2 %collective-permute-start.3 = (bf16[4,48,640]{2,1,0:T(8,128)(2,1)S(1)}, bf16[4,48,640]{2,1,0:T(8,128)(2,1)S(1)}, u32[]{:S(2)}, u32[]{:S(2)}) collective-permute-start(bf16[4,48,640]{2,1,0:T(8,128)(2,1)S(1)} %get-tuple-element.144), channel_id=1, source_target_pairs={{0,4},{2,6},{4,0},{6,2},{8,12},{10,14},{12,8},{14,10},{16,20},{18,... | collective-permute-start | bytes 737288 | tf_op jit(solution)/shard_map/ppermute | solution.py:85
  30.6 10.0 %collective-permute-start.8 = (bf16[2,48,1920]{2,1,0:T(8,128)(2,1)S(1)}, bf16[2,48,1920]{2,1,0:T(8,128)(2,1)S(1)}, u32[]{:S(2)}, u32[]{:S(2)}) collective-permute-start(bf16[2,48,1920]{2,1,0:T(8,128)(2,1)S(1)} %pad_maximum_fusion.9), channel_id=1, source_target_pairs={{0,8},{2,10},{4,12},{6,14},{8,0},{10,2},{12,4},{14,6},{16,24},{18,... | collective-permute-start | bytes 1105928 | tf_op jit(solution)/shard_map/ppermute | solution.py:85
  31.0 18.7 %collective-permute-start.5 = (bf16[8,48,640]{2,1,0:T(8,128)(2,1)S(1)}, bf16[8,48,640]{2,1,0:T(8,128)(2,1)S(1)}, u32[]{:S(2)}, u32[]{:S(2)}) collective-permute-start(bf16[8,48,640]{2,1,0:T(8,128)(2,1)S(1)} %pad_maximum_fusion.7.pair_a), channel_id=1, source_target_pairs={{0,2},{2,0},{4,6},{6,4},{8,10},{10,8},{12,14},{14,12},{16,18},{18,... | collective-permute-start | bytes 1474568 | tf_op jit(solution)/shard_map/ppermute | solution.py:85
  32.4 17.3 %collective-permute-start.6 = (bf16[8,48,640]{2,1,0:T(8,128)(2,1)S(1)}, bf16[8,48,640]{2,1,0:T(8,128)(2,1)S(1)}, u32[]{:S(2)}, u32[]{:S(2)}) collective-permute-start(bf16[8,48,640]{2,1,0:T(8,128)(2,1)S(1)} %pad_maximum_fusion.8.pair_b), channel_id=1, source_target_pairs={{0,4},{2,6},{4,0},{6,2},{8,12},{10,14},{12,8},{14,10},{16,20},{18,... | collective-permute-start | bytes 1474568 | tf_op jit(solution)/shard_map/ppermute | solution.py:85
  40.5 8.4 %collective-permute-start.11 = (bf16[48,1536]{1,0:T(8,128)(2,1)S(1)}, bf16[48,1536]{1,0:T(8,128)(2,1)S(1)}, u32[]{:S(2)}, u32[]{:S(2)}) collective-permute-start(bf16[48,1536]{1,0:T(8,128)(2,1)S(1)} %pad_maximum_fusion.14), channel_id=1, source_target_pairs={{0,16},{2,18},{4,20},{6,22},{8,24},{10,26},{12,28},{14,30},{16,0},... | collective-permute-start | bytes 442376 | tf_op jit(solution)/shard_map/ppermute | solution.py:85
  49.6 16.1 %collective-permute-start.12 = (bf16[2,48,1536]{2,1,0:T(8,128)(2,1)}, bf16[2,48,1536]{2,1,0:T(8,128)(2,1)}, u32[]{:S(2)}, u32[]{:S(2)}) collective-permute-start(bf16[2,48,1536]{2,1,0:T(8,128)(2,1)} %pad_maximum_fusion.11), channel_id=1, source_target_pairs={{0,8},{2,10},{4,12},{6,14},{8,0},{10,2},{12,4},{14,6},{16,24},{18,... | collective-permute-start | bytes 884744 | tf_op jit(solution)/shard_map/ppermute | solution.py:85
  49.8 20.7 %copy-start.10 = (bf16[768,1280]{1,0:T(8,128)(2,1)}, bf16[768,1280]{1,0:T(8,128)(2,1)S(1)}, u32[]{:S(2)}) copy-start(bf16[768,1280]{1,0:T(8,128)(2,1)S(1)} %place.3.w_ref.refs_3_) | copy-start | bytes 5898244
  49.8 12.3 %collective-permute-start.9 = (bf16[4,48,1024]{2,1,0:T(8,128)(2,1)S(1)}, bf16[4,48,1024]{2,1,0:T(8,128)(2,1)}, u32[]{:S(2)}, u32[]{:S(2)}) collective-permute-start(bf16[4,48,1024]{2,1,0:T(8,128)(2,1)S(1)} %slice.234), channel_id=1, source_target_pairs={{0,4},{2,6},{4,0},{6,2},{8,12},{10,14},{12,8},{14,10},{16,20},{18,... | collective-permute-start | bytes 1179656 | tf_op jit(solution)/shard_map/ppermute | solution.py:85
  51.4 10.7 %collective-permute-start.10 = (bf16[4,48,896]{2,1,0:T(8,128)(2,1)S(1)}, bf16[4,48,896]{2,1,0:T(8,128)(2,1)}, u32[]{:S(2)}, u32[]{:S(2)}) collective-permute-start(bf16[4,48,896]{2,1,0:T(8,128)(2,1)S(1)} %pad_maximum_fusion.10), channel_id=1, source_target_pairs={{0,2},{2,0},{4,6},{6,4},{8,10},{10,8},{12,14},{14,12},{16,18},{18,... | collective-permute-start | bytes 1032200 | tf_op jit(solution)/shard_map/ppermute | solution.py:85
  64.2 24.8 %collective-permute-start.13 = (bf16[8,48,1024]{2,1,0:T(8,128)(2,1)S(1)}, bf16[8,48,1024]{2,1,0:T(8,128)(2,1)S(1)}, u32[]{:S(2)}, u32[]{:S(2)}) collective-permute-start(bf16[8,48,1024]{2,1,0:T(8,128)(2,1)S(1)} %pad_maximum_fusion.pair_a), channel_id=1, source_target_pairs={{0,2},{2,0},{4,6},{6,4},{8,10},{10,8},{12,14},{14,12},{16,18},{18,... | collective-permute-start | bytes 2359304 | tf_op jit(solution)/shard_map/ppermute | solution.py:85
  64.9 24.2 %collective-permute-start.14 = (bf16[8,48,896]{2,1,0:T(8,128)(2,1)S(1)}, bf16[8,48,896]{2,1,0:T(8,128)(2,1)S(1)}, u32[]{:S(2)}, u32[]{:S(2)}) collective-permute-start(bf16[8,48,896]{2,1,0:T(8,128)(2,1)S(1)} %pad_maximum_fusion.2.pair_b), channel_id=1, source_target_pairs={{0,4},{2,6},{4,0},{6,2},{8,12},{10,14},{12,8},{14,10},{16,20},{18,... | collective-permute-start | bytes 2064392 | tf_op jit(solution)/shard_map/ppermute | solution.py:85
  67.8 19.3 %collective-permute-start.15 = (bf16[4,48,768]{2,1,0:T(8,128)(2,1)S(1)}, bf16[4,48,768]{2,1,0:T(8,128)(2,1)S(1)}, u32[]{:S(2)}, u32[]{:S(2)}) collective-permute-start(bf16[4,48,768]{2,1,0:T(8,128)(2,1)S(1)} %get-tuple-element.164), channel_id=1, source_target_pairs={{0,4},{2,6},{4,0},{6,2},{8,12},{10,14},{12,8},{14,10},{16,20},{18,... | collective-permute-start | bytes 884744 | tf_op jit(solution)/shard_map/ppermute | solution.py:85
  69.1 19.9 %collective-permute-start.16 = (bf16[4,48,768]{2,1,0:T(8,128)(2,1)S(1)}, bf16[4,48,768]{2,1,0:T(8,128)(2,1)S(1)}, u32[]{:S(2)}, u32[]{:S(2)}) collective-permute-start(bf16[4,48,768]{2,1,0:T(8,128)(2,1)S(1)} %get-tuple-element.165), channel_id=1, source_target_pairs={{0,2},{2,0},{4,6},{6,4},{8,10},{10,8},{12,14},{14,12},{16,18},{18,... | collective-permute-start | bytes 884744 | tf_op jit(solution)/shard_map/ppermute | solution.py:85
  92.9 4.6 %collective-permute-start.17 = (bf16[1536,768]{1,0:T(8,128)(2,1)S(1)}, bf16[1536,768]{1,0:T(8,128)(2,1)S(1)}, u32[]{:S(2)}, u32[]{:S(2)}) collective-permute-start(bf16[1536,768]{1,0:T(8,128)(2,1)S(1)} %outward.1.mine_ref), channel_id=1, source_target_pairs={{0,1},{1,0},{2,3},{3,2},{4,5},{5,4},{6,7},{7,6},{8,9},{9,8},{10,11... | collective-permute-start | bytes 7077896 | tf_op jit(solution)/shard_map/ppermute | solution.py:89
  92.9 15.7 %collective-permute-start.18 = (bf16[8,48,768]{2,1,0:T(8,128)(2,1)S(1)}, bf16[8,48,768]{2,1,0:T(8,128)(2,1)S(1)}, u32[]{:S(2)}, u32[]{:S(2)}) collective-permute-start(bf16[8,48,768]{2,1,0:T(8,128)(2,1)S(1)} %pad_maximum_fusion.4.pair_a), channel_id=1, source_target_pairs={{0,2},{2,0},{4,6},{6,4},{8,10},{10,8},{12,14},{14,12},{16,18},{18,... | collective-permute-start | bytes 1769480 | tf_op jit(solution)/shard_map/ppermute | solution.py:85
  93.6 15.4 %collective-permute-start.19 = (bf16[8,48,768]{2,1,0:T(8,128)(2,1)S(1)}, bf16[8,48,768]{2,1,0:T(8,128)(2,1)S(1)}, u32[]{:S(2)}, u32[]{:S(2)}) collective-permute-start(bf16[8,48,768]{2,1,0:T(8,128)(2,1)S(1)} %pad_maximum_fusion.5.pair_b), channel_id=1, source_target_pairs={{0,4},{2,6},{4,0},{6,2},{8,12},{10,14},{12,8},{14,10},{16,20},{18,... | collective-permute-start | bytes 1769480 | tf_op jit(solution)/shard_map/ppermute | solution.py:85
  118.2 4.9 %collective-permute-start.20 = (bf16[1536,768]{1,0:T(8,128)(2,1)}, bf16[1536,768]{1,0:T(8,128)(2,1)}, u32[]{:S(2)}, u32[]{:S(2)}) collective-permute-start(bf16[1536,768]{1,0:T(8,128)(2,1)} %get-tuple-element.178.mine_ref), channel_id=1, source_target_pairs={{0,1},{1,0},{2,3},{3,2},{4,5},{5,4},{6,7},{7,6},{8,9},{9,8},{10,11... | collective-permute-start | bytes 7077896 | tf_op jit(solution)/shard_map/ppermute | solution.py:89
  124.9 18.1 %copy-start.50 = (bf16[1536,768]{1,0:T(8,128)(2,1)S(1)}, bf16[1536,768]{1,0:T(8,128)(2,1)}, u32[]{:S(2)}) copy-start(bf16[1536,768]{1,0:T(8,128)(2,1)} %get-tuple-element.186.refs_0_) | copy-start | bytes 7077892
  124.9 18.1 %copy-start.51 = (bf16[1536,768]{1,0:T(8,128)(2,1)S(1)}, bf16[1536,768]{1,0:T(8,128)(2,1)}, u32[]{:S(2)}) copy-start(bf16[1536,768]{1,0:T(8,128)(2,1)} %get-tuple-element.187.refs_1_) | copy-start | bytes 7077892
  142.7 18.7 %collective-permute-start.21 = (bf16[1536,768]{1,0:T(8,128)(2,1)}, bf16[1536,768]{1,0:T(8,128)(2,1)}, u32[]{:S(2)}, u32[]{:S(2)}) collective-permute-start(bf16[1536,768]{1,0:T(8,128)(2,1)} %get-tuple-element.193.mine_ref), channel_id=1, source_target_pairs={{0,1},{1,0},{2,3},{3,2},{4,5},{5,4},{6,7},{7,6},{8,9},{9,8},{10,11... | collective-permute-start | bytes 7077896 | tf_op jit(solution)/shard_map/ppermute | solution.py:89
  151.0 31.6 %collective-permute-start.23 = (bf16[2,4,48,1536]{3,2,1,0:T(8,128)(2,1)}, bf16[2,4,48,1536]{3,2,1,0:T(8,128)(2,1)}, u32[]{:S(2)}, u32[]{:S(2)}) collective-permute-start(bf16[2,4,48,1536]{3,2,1,0:T(8,128)(2,1)} %get-tuple-element.188), channel_id=1, source_target_pairs={{0,2},{2,0},{4,6},{6,4},{8,10},{10,8},{12,14},{14,12},{16,18},{18,... | collective-permute-start | bytes 3538952 | tf_op jit(solution)/shard_map/ppermute | solution.py:85
  158.9 31.0 %collective-permute-start.22 = (bf16[2,4,48,1536]{3,2,1,0:T(8,128)(2,1)}, bf16[2,4,48,1536]{3,2,1,0:T(8,128)(2,1)}, u32[]{:S(2)}, u32[]{:S(2)}) collective-permute-start(bf16[2,4,48,1536]{3,2,1,0:T(8,128)(2,1)} %get-tuple-element.192), channel_id=1, source_target_pairs={{0,4},{2,6},{4,0},{6,2},{8,12},{10,14},{12,8},{14,10},{16,20},{18,... | collective-permute-start | bytes 3538952 | tf_op jit(solution)/shard_map/ppermute | solution.py:85
  184.8 22.1 %collective-permute-start.27 = (bf16[4,48,1536]{2,1,0:T(8,128)(2,1)}, bf16[4,48,1536]{2,1,0:T(8,128)(2,1)}, u32[]{:S(2)}, u32[]{:S(2)}) collective-permute-start(bf16[4,48,1536]{2,1,0:T(8,128)(2,1)} %add_bitcast_fusion.1), channel_id=1, source_target_pairs={{0,4},{2,6},{4,0},{6,2},{8,12},{10,14},{12,8},{14,10},{16,20},{18,... | collective-permute-start | bytes 1769480 | tf_op jit(solution)/shard_map/ppermute | solution.py:85
  192.6 27.7 %collective-permute-start.26 = (bf16[4,48,1536]{2,1,0:T(8,128)(2,1)}, bf16[4,48,1536]{2,1,0:T(8,128)(2,1)}, u32[]{:S(2)}, u32[]{:S(2)}) collective-permute-start(bf16[4,48,1536]{2,1,0:T(8,128)(2,1)} %add_bitcast_fusion), channel_id=1, source_target_pairs={{0,2},{2,0},{4,6},{6,4},{8,10},{10,8},{12,14},{14,12},{16,18},{18,... | collective-permute-start | bytes 1769480 | tf_op jit(solution)/shard_map/ppermute | solution.py:85
  198.1 22.1 %collective-permute-start.25 = (bf16[2,4,48,384]{3,2,1,0:T(8,128)(2,1)}, bf16[2,4,48,384]{3,2,1,0:T(8,128)(2,1)S(1)}, u32[]{:S(2)}, u32[]{:S(2)}) collective-permute-start(bf16[2,4,48,384]{3,2,1,0:T(8,128)(2,1)} %copy-done.46), channel_id=1, source_target_pairs={{0,4},{2,6},{4,0},{6,2},{8,12},{10,14},{12,8},{14,10},{16,20},{18,... | collective-permute-start | bytes 884744 | tf_op jit(solution)/shard_map/ppermute | solution.py:85
  198.7 21.5 %collective-permute-start.24 = (bf16[2,4,48,384]{3,2,1,0:T(8,128)(2,1)}, bf16[2,4,48,384]{3,2,1,0:T(8,128)(2,1)S(1)}, u32[]{:S(2)}, u32[]{:S(2)}) collective-permute-start(bf16[2,4,48,384]{3,2,1,0:T(8,128)(2,1)} %copy-done.45), channel_id=1, source_target_pairs={{0,2},{2,0},{4,6},{6,4},{8,10},{10,8},{12,14},{14,12},{16,18},{18,... | collective-permute-start | bytes 884744 | tf_op jit(solution)/shard_map/ppermute | solution.py:85
  209.0 21.6 %collective-permute-start.28 = (bf16[2,48,1536]{2,1,0:T(8,128)(2,1)}, bf16[2,48,1536]{2,1,0:T(8,128)(2,1)}, u32[]{:S(2)}, u32[]{:S(2)}) collective-permute-start(bf16[2,48,1536]{2,1,0:T(8,128)(2,1)} %get-tuple-element.213), channel_id=1, source_target_pairs={{0,8},{2,10},{4,12},{6,14},{8,0},{10,2},{12,4},{14,6},{16,24},{18,... | collective-permute-start | bytes 884744 | tf_op jit(solution)/shard_map/ppermute | solution.py:85
  213.1 28.9 %collective-permute-start.33 = (bf16[2,4,48,384]{3,2,1,0:T(8,128)(2,1)}, bf16[2,4,48,384]{3,2,1,0:T(8,128)(2,1)}, u32[]{:S(2)}, u32[]{:S(2)}) collective-permute-start(bf16[2,4,48,384]{3,2,1,0:T(8,128)(2,1)} %get-tuple-element.215), channel_id=1, source_target_pairs={{0,2},{2,0},{4,6},{6,4},{8,10},{10,8},{12,14},{14,12},{16,18},{18,... | collective-permute-start | bytes 884744 | tf_op jit(solution)/shard_map/ppermute | solution.py:85
  225.2 16.0 %collective-permute-start.31 = (bf16[4,48,384]{2,1,0:T(8,128)(2,1)}, bf16[4,48,384]{2,1,0:T(8,128)(2,1)S(1)}, u32[]{:S(2)}, u32[]{:S(2)}) collective-permute-start(bf16[4,48,384]{2,1,0:T(8,128)(2,1)} %copy-done.48), channel_id=1, source_target_pairs={{0,4},{2,6},{4,0},{6,2},{8,12},{10,14},{12,8},{14,10},{16,20},{18,... | collective-permute-start | bytes 442376 | tf_op jit(solution)/shard_map/ppermute | solution.py:85
  226.7 15.2 %collective-permute-start.32 = (bf16[4,48,384]{2,1,0:T(8,128)(2,1)}, bf16[4,48,384]{2,1,0:T(8,128)(2,1)}, u32[]{:S(2)}, u32[]{:S(2)}) collective-permute-start(bf16[4,48,384]{2,1,0:T(8,128)(2,1)} %copy-done.47), channel_id=1, source_target_pairs={{0,2},{2,0},{4,6},{6,4},{8,10},{10,8},{12,14},{14,12},{16,18},{18,... | collective-permute-start | bytes 442376 | tf_op jit(solution)/shard_map/ppermute | solution.py:85
  230.3 11.7 %collective-permute-start.30 = (bf16[2,48,1536]{2,1,0:T(8,128)(2,1)}, bf16[2,48,1536]{2,1,0:T(8,128)(2,1)}, u32[]{:S(2)}, u32[]{:S(2)}) collective-permute-start(bf16[2,48,1536]{2,1,0:T(8,128)(2,1)} %get-tuple-element.226), channel_id=1, source_target_pairs={{0,8},{2,10},{4,12},{6,14},{8,0},{10,2},{12,4},{14,6},{16,24},{18,... | collective-permute-start | bytes 884744 | tf_op jit(solution)/shard_map/ppermute | solution.py:85
  235.0 18.4 %copy-start.19 = (bf16[2,4,48,384]{3,2,1,0:T(8,128)(2,1)S(1)}, bf16[2,4,48,384]{3,2,1,0:T(8,128)(2,1)}, u32[]{:S(2)}) copy-start(bf16[2,4,48,384]{3,2,1,0:T(8,128)(2,1)} %copy-done.18) | copy-start | bytes 884740
  235.0 8.4 %collective-permute-start.34 = (bf16[2,4,48,512]{3,2,1,0:T(8,128)(2,1)}, bf16[2,4,48,512]{3,2,1,0:T(8,128)(2,1)S(1)}, u32[]{:S(2)}, u32[]{:S(2)}) collective-permute-start(bf16[2,4,48,512]{3,2,1,0:T(8,128)(2,1)} %get-tuple-element.236), channel_id=1, source_target_pairs={{0,4},{2,6},{4,0},{6,2},{8,12},{10,14},{12,8},{14,10},{16,20},{18,... | collective-permute-start | bytes 1179656 | tf_op jit(solution)/shard_map/ppermute | solution.py:85
  241.8 25.2 %collective-permute-start.29 = (bf16[1536,768]{1,0:T(8,128)(2,1)S(1)}, bf16[1536,768]{1,0:T(8,128)(2,1)}, u32[]{:S(2)}, u32[]{:S(2)}) collective-permute-start(bf16[1536,768]{1,0:T(8,128)(2,1)S(1)} %source.1.mine_ref), channel_id=1, source_target_pairs={{0,1},{1,0},{2,3},{3,2},{4,5},{5,4},{6,7},{7,6},{8,9},{9,8},{10,11... | collective-permute-start | bytes 7077896 | tf_op jit(solution)/shard_map/ppermute | solution.py:89
  241.9 13.1 %collective-permute-start.38 = (bf16[48,1536]{1,0:T(8,128)(2,1)}, bf16[48,1536]{1,0:T(8,128)(2,1)S(1)}, u32[]{:S(2)}, u32[]{:S(2)}) collective-permute-start(bf16[48,1536]{1,0:T(8,128)(2,1)} %fusion.4), channel_id=1, source_target_pairs={{0,16},{2,18},{4,20},{6,22},{8,24},{10,26},{12,28},{14,30},{16,0},... | collective-permute-start | bytes 442376 | tf_op jit(solution)/shard_map/ppermute | solution.py:85
  249.4 8.3 %collective-permute-start.37 = (bf16[2,48,768]{2,1,0:T(8,128)(2,1)S(1)}, bf16[2,48,768]{2,1,0:T(8,128)(2,1)S(1)}, u32[]{:S(2)}, u32[]{:S(2)}) collective-permute-start(bf16[2,48,768]{2,1,0:T(8,128)(2,1)S(1)} %get-tuple-element.245), channel_id=1, source_target_pairs={{0,8},{2,10},{4,12},{6,14},{8,0},{10,2},{12,4},{14,6},{16,24},{18,... | collective-permute-start | bytes 442376 | tf_op jit(solution)/shard_map/ppermute | solution.py:85
  251.9 11.2 %collective-permute-start.42 = (bf16[48,1536]{1,0:T(8,128)(2,1)S(1)}, bf16[48,1536]{1,0:T(8,128)(2,1)S(1)}, u32[]{:S(2)}, u32[]{:S(2)}) collective-permute-start(bf16[48,1536]{1,0:T(8,128)(2,1)S(1)} %fusion.5), channel_id=1, source_target_pairs={{0,16},{2,18},{4,20},{6,22},{8,24},{10,26},{12,28},{14,30},{16,0},... | collective-permute-start | bytes 442376 | tf_op jit(solution)/shard_map/ppermute | solution.py:85
  254.4 10.8 %collective-permute-start.36 = (bf16[4,48,512]{2,1,0:T(8,128)(2,1)S(1)}, bf16[4,48,512]{2,1,0:T(8,128)(2,1)S(1)}, u32[]{:S(2)}, u32[]{:S(2)}) collective-permute-start(bf16[4,48,512]{2,1,0:T(8,128)(2,1)S(1)} %get-tuple-element.251), channel_id=1, source_target_pairs={{0,2},{2,0},{4,6},{6,4},{8,10},{10,8},{12,14},{14,12},{16,18},{18,... | collective-permute-start | bytes 589832 | tf_op jit(solution)/shard_map/ppermute | solution.py:85
  255.0 10.1 %collective-permute-start.35 = (bf16[4,48,384]{2,1,0:T(8,128)(2,1)S(1)}, bf16[4,48,384]{2,1,0:T(8,128)(2,1)S(1)}, u32[]{:S(2)}, u32[]{:S(2)}) collective-permute-start(bf16[4,48,384]{2,1,0:T(8,128)(2,1)S(1)} %get-tuple-element.250), channel_id=1, source_target_pairs={{0,4},{2,6},{4,0},{6,2},{8,12},{10,14},{12,8},{14,10},{16,20},{18,... | collective-permute-start | bytes 442376 | tf_op jit(solution)/shard_map/ppermute | solution.py:85
  257.7 8.6 %collective-permute-start.39 = (bf16[48,768]{1,0:T(8,128)(2,1)S(1)}, bf16[48,768]{1,0:T(8,128)(2,1)S(1)}, u32[]{:S(2)}, u32[]{:S(2)}) collective-permute-start(bf16[48,768]{1,0:T(8,128)(2,1)S(1)} %fusion.9), channel_id=1, source_target_pairs={{0,16},{2,18},{4,20},{6,22},{8,24},{10,26},{12,28},{14,30},{16,0},... | collective-permute-start | bytes 221192 | tf_op jit(solution)/shard_map/ppermute | solution.py:85
  266.2 6.8 %collective-permute-start.40 = (bf16[2,48,896]{2,1,0:T(8,128)(2,1)S(1)}, bf16[2,48,896]{2,1,0:T(8,128)(2,1)S(1)}, u32[]{:S(2)}, u32[]{:S(2)}) collective-permute-start(bf16[2,48,896]{2,1,0:T(8,128)(2,1)S(1)} %get-tuple-element.257), channel_id=1, source_target_pairs={{0,8},{2,10},{4,12},{6,14},{8,0},{10,2},{12,4},{14,6},{16,24},{18,... | collective-permute-start | bytes 516104 | tf_op jit(solution)/shard_map/ppermute | solution.py:85
  267.1 15.3 %copy-start.54 = (f32[3,48,384]{2,1,0:T(8,128)S(1)}, f32[3,48,384]{2,1,0:T(8,128)}, u32[]{:S(2)}) copy-start(f32[3,48,384]{2,1,0:T(8,128)} %param.31) | copy-start | bytes 663556
  273.0 5.6 %collective-permute-start.41 = (bf16[48,896]{1,0:T(8,128)(2,1)S(1)}, bf16[48,896]{1,0:T(8,128)(2,1)S(1)}, u32[]{:S(2)}, u32[]{:S(2)}) collective-permute-start(bf16[48,896]{1,0:T(8,128)(2,1)S(1)} %fusion.7), channel_id=1, source_target_pairs={{0,16},{2,18},{4,20},{6,22},{8,24},{10,26},{12,28},{14,30},{16,0},... | collective-permute-start | bytes 258056 | tf_op jit(solution)/shard_map/ppermute | solution.py:85
  (72 other events, 526.0 us)
